TPU v7x, 128 devices: a whole 4x4x4 slice. The times are simulated.
128 devices in a mesh: req: 4 (over y), exp: 32 (over z, x, core).
Axes of the slice: x: 4, y: 4, z: 4, core: 2. Of those that a mesh axis runs over, the one named last changes fastest.
Arguments:
- queries: bfloat16 [16384, 2048], P(('req', 'exp')), may hold values from -128 to 128
- keys_then_values: bfloat16 [16384, 1024], P(('req', 'exp')), may hold values from -8 to 8
- residual: bfloat16 [16384, 2048], P(('req', 'exp')), may hold values from -6 to 6
- norm_gain: bfloat16 [2048], replicated, may hold values from 0.099609375 to 1.8984375
- prompt_lengths: int32 [4, 16], P('req'), may hold values from 1 to 3072, 4096 in all within a row
- expert_ids: int32 [16384, 6], P(('req', 'exp')), may hold values from 0 to 31, all different within a row; in each aligned block of 128 rows (0 to 127, 128 to 255, ...) at most 36 rows name the same one
- router_logits: float32 [16384, 6], P(('req', 'exp')), may hold values from -10 to 320
- w_gate: bfloat16 [32, 2048, 1408], P('exp'), may hold values from -0.125 to 0.125
- w_up: bfloat16 [32, 2048, 1408], P('exp'), may hold values from -0.125 to 0.125
- w_down: bfloat16 [32, 1408, 2048], P('exp'), may hold values from -0.15625 to 0.15625
- w_shared_gate: bfloat16 [2048, 2816], P('exp', 'req'), may hold values from -0.125 to 0.125
- w_shared_up: bfloat16 [2048, 2816], P('exp', 'req'), may hold values from -0.125 to 0.125
- w_shared_down: bfloat16 [2048, 2816], P('exp', 'req'), may hold values from -0.109375 to 0.109375
- page_table: int32 [4, 256], replicated, may hold values from 0 to 1023, as said below
Outputs:
- layer_out: bfloat16 [16384, 2048], P(('req', 'exp'))
- kv_cache: bfloat16 [1024, 16, 1024], P(('req', 'exp'))
- log_totals: float32 [16, 16384], P(None, ('req', 'exp'))
Inputs may be any that keep to these rules, and one draw needn't show every extreme that they name: `expert_ids`: in the rows of one device no expert is named more than 36 times. `page_table`: the entries are a permutation of 0 to 1023. Entry [r, j] lies in the aligned block of 8 slots whose index modulo 256 // 8 equals j // 8; each aligned block of 8 entries of a row names exactly 2 slots in each aligned block of 256 slots.
All inputs are finite; a program needn't handle non-finite values.
Results may differ from a plain program's by a relative error of at most 0.0065.
Values may be sent and summed in bfloat16 or wider, within the bound.
A program may use at most 192 MiB of HBM per device.

v0:
```python
import jax
import jax.numpy as jnp
from jax import lax
from jax.sharding import PartitionSpec as P

D = 2048
QUERY_HEADS = 16
KEY_VALUE_HEADS = 4
HEAD_SIZE = 128
TOPK = 6
PAGE = 16


large_negative = -1e30
eps_norm = 1e-06


def segment_ids(positions, prompt_ends):
    return jnp.sum((positions[:, None] >= prompt_ends[None, :]).astype(jnp.int32), axis=1)


def attend_piece(state_now, key_value_portion, query_head_block, query_pos, query_seg, prompt_ends):
    run_max, run_sum, accumulated = state_now
    key_count = key_value_portion.shape[0]
    key_pos = jnp.arange(key_count, dtype=jnp.int32)
    key_seg = segment_ids(key_pos, prompt_ends)
    key_row_block = key_value_portion[:, : KEY_VALUE_HEADS * HEAD_SIZE].reshape(
        key_count, KEY_VALUE_HEADS, HEAD_SIZE
    )
    value_row_block = key_value_portion[:, KEY_VALUE_HEADS * HEAD_SIZE :].reshape(
        key_count, KEY_VALUE_HEADS, HEAD_SIZE
    )
    scores = jnp.einsum(
        "qhgd,khd->hgqk", query_head_block, key_row_block, preferred_element_type=jnp.float32
    ) * HEAD_SIZE ** (-0.5)
    visible = (
        (key_pos[None, :] <= query_pos[:, None])
        & (key_seg[None, :] == query_seg[:, None])
        & (key_pos[None, :] >= 0)
    )
    scores = jnp.where(visible, scores, large_negative)
    new_max = jnp.maximum(run_max, jnp.max(scores, axis=3))
    softmax_p = jnp.where(visible, jnp.exp(scores - new_max[..., None]), 0.0)
    run_sum = jnp.sum(softmax_p, axis=3)
    added = jnp.einsum(
        "hgqk,khd->hgqd",
        softmax_p.astype(jnp.bfloat16),
        value_row_block,
        preferred_element_type=jnp.float32,
    )
    accumulated = added
    return (new_max, run_sum, accumulated)


def on_device(
    queries,
    keys_then_values,
    residual,
    norm_gain,
    prompt_lengths,
    expert_ids,
    router_logits,
    w_gate,
    w_up,
    w_down,
    w_shared_gate,
    w_shared_up,
    w_shared_down,
    page_table,
):
    token_rows = queries.shape[0]
    n_groups = lax.axis_size("req")
    n_columns = lax.axis_size("exp")
    column = lax.axis_index("exp")
    my_group = lax.axis_index("req")
    heads_per_group = QUERY_HEADS // KEY_VALUE_HEADS
    shared_gate_all, shared_up_all, shared_down_all = (
        lax.all_gather(w_shared_gate, "exp", axis=0, tiled=True),
        lax.all_gather(w_shared_up, "exp", axis=0, tiled=True),
        lax.all_gather(w_shared_down, "exp", axis=0, tiled=True),
    )
    prompt_ends = jnp.cumsum(prompt_lengths[0])
    query_pos = column * token_rows + jnp.arange(token_rows, dtype=jnp.int32)
    query_seg = segment_ids(query_pos, prompt_ends)
    query_head_block = queries.reshape(token_rows, KEY_VALUE_HEADS, heads_per_group, HEAD_SIZE)
    initial = (
        jnp.full((KEY_VALUE_HEADS, heads_per_group, token_rows), large_negative, jnp.float32),
        jnp.zeros((KEY_VALUE_HEADS, heads_per_group, token_rows), jnp.float32),
        jnp.zeros((KEY_VALUE_HEADS, heads_per_group, token_rows, HEAD_SIZE), jnp.float32),
    )
    run_max, run_sum, accumulated = attend_piece(
        initial,
        lax.all_gather(keys_then_values, "exp", axis=0, tiled=True),
        query_head_block,
        query_pos,
        query_seg,
        prompt_ends,
    )
    attention = (
        jnp.transpose(accumulated / run_sum[..., None], (2, 0, 1, 3))
        .reshape(token_rows, QUERY_HEADS * HEAD_SIZE)
        .astype(jnp.bfloat16)
    )
    log_totals = (run_max + jnp.log(run_sum)).reshape(QUERY_HEADS, token_rows)
    hidden = residual.astype(jnp.float32) + attention.astype(jnp.float32)
    scale_rows = lax.rsqrt(jnp.mean(hidden * hidden, axis=-1, keepdims=True) + eps_norm)
    normed = (hidden * scale_rows * norm_gain.astype(jnp.float32)).astype(jnp.bfloat16)
    weights = jax.nn.softmax(router_logits, axis=-1)
    local_experts = w_gate.shape[0]
    experts = local_experts * n_columns
    capacity = min(token_rows, 3 * token_rows * TOPK // (2 * experts))
    flat_ids = expert_ids.reshape(-1)
    onehot_ids = (flat_ids[:, None] == jnp.arange(experts, dtype=jnp.int32)[None, :]).astype(
        jnp.int32
    )
    slot_rank = jnp.sum((jnp.cumsum(onehot_ids, axis=0) - 1) * onehot_ids, axis=1)
    slot_index = flat_ids * capacity + slot_rank
    source_rows = jnp.arange(token_rows * TOPK, dtype=jnp.int32) // TOPK
    send_rows = (
        jnp.zeros((experts * capacity, D), jnp.bfloat16).at[slot_index].set(normed[source_rows])
    )
    send_rows = send_rows.reshape(n_columns, local_experts, capacity, D)
    received = lax.all_to_all(send_rows, "exp", split_axis=0, concat_axis=0, tiled=True)
    gate_out = jnp.einsum("sjkd,jdf->sjkf", received, w_gate, preferred_element_type=jnp.float32)
    up_out = jnp.einsum("sjkd,jdf->sjkf", received, w_up, preferred_element_type=jnp.float32)
    activated = (jax.nn.silu(gate_out) * up_out).astype(jnp.bfloat16)
    expert_out = jnp.einsum(
        "sjkf,jfd->sjkd", activated, w_down, preferred_element_type=jnp.float32
    ).astype(jnp.bfloat16)
    returned = lax.all_to_all(expert_out, "exp", split_axis=0, concat_axis=0, tiled=True)
    all_rows = lax.all_gather(normed, "req", axis=0, tiled=True)
    gate_part = jnp.dot(all_rows, shared_gate_all, preferred_element_type=jnp.float32)
    up_part = jnp.dot(all_rows, shared_up_all, preferred_element_type=jnp.float32)
    shared_act = (jax.nn.silu(gate_part) * up_part).astype(jnp.bfloat16)
    shared_sum = lax.psum_scatter(
        lax.dot_general(
            shared_act,
            shared_down_all,
            (((1,), (1,)), ((), ())),
            preferred_element_type=jnp.float32,
        ),
        "req",
        scatter_dimension=0,
        tiled=True,
    )
    shared_out = shared_sum.astype(jnp.bfloat16)
    returned = returned.reshape(experts * capacity, D)
    picked = returned[slot_index].reshape(token_rows, TOPK, D)
    expert_mix = jnp.sum(weights[:, :, None] * picked, axis=1)
    layer_out = (hidden + expert_mix + shared_out.astype(jnp.float32)).astype(jnp.bfloat16)
    key_value_width = 2 * KEY_VALUE_HEADS * HEAD_SIZE
    pages_dev = token_rows // PAGE
    per_group = pages_dev // n_groups
    group_pages = pages_dev * n_columns
    page_cols = lax.dynamic_slice_in_dim(page_table, column * pages_dev, pages_dev, 1)
    dest_all = page_cols // group_pages
    onehot_dest = (
        dest_all[:, :, None] == jnp.arange(n_groups, dtype=jnp.int32)[None, None, :]
    ).astype(jnp.int32)
    rank_all = jnp.sum((jnp.cumsum(onehot_dest, axis=1) - 1) * onehot_dest, axis=2)
    my_dest = lax.dynamic_index_in_dim(dest_all, my_group, 0, keepdims=False)
    my_rank = lax.dynamic_index_in_dim(rank_all, my_group, 0, keepdims=False)
    own_pages = keys_then_values.reshape(pages_dev, PAGE, key_value_width)
    send_pages = (
        jnp.zeros((n_groups, per_group, PAGE, key_value_width), jnp.bfloat16)
        .at[my_dest, my_rank]
        .set(own_pages)
    )
    arrived = lax.all_to_all(send_pages, "req", split_axis=0, concat_axis=0, tiled=True)
    local_slot = page_cols - my_group * group_pages - column * pages_dev
    target = jnp.where(dest_all == my_group, local_slot, pages_dev)
    sources = arrived[jnp.arange(n_groups, dtype=jnp.int32)[:, None], rank_all]
    kv_cache = (
        jnp.zeros((pages_dev, PAGE, key_value_width), jnp.bfloat16)
        .at[target.reshape(-1)]
        .set(sources.reshape(n_groups * pages_dev, PAGE, key_value_width), mode="drop")
    )
    return (layer_out, kv_cache, log_totals)


def solution(mesh):
    placed = (
        P(("req", "exp"), None),
        P(("req", "exp"), None),
        P(("req", "exp"), None),
        P(),
        P("req", None),
        P(("req", "exp"), None),
        P(("req", "exp"), None),
        P("exp", None, None),
        P("exp", None, None),
        P("exp", None, None),
        P("exp", "req"),
        P("exp", "req"),
        P("exp", "req"),
        P(),
    )
    return jax.shard_map(
        on_device,
        mesh=mesh,
        in_specs=placed,
        out_specs=(P(("req", "exp"), None), P(("req", "exp"), None, None), P(None, ("req", "exp"))),
        check_vma=False,
    )
```

profile of v0, /device:TPU:8, one launch (start us, length us, event | category | flops | bytes accessed | tf_op | source)
XLA Modules:
  0.0 451.1 jit_solution(11599822679798374914)
XLA Ops:
  7.2 1.8 copy.48
  9.8 0.7 copy.47
  11.0 1.4 reshape.304
  13.0 1.8 fusion.34
  14.9 57.1 %all-gather.6.cloned.1.call-done = bf16[4096,1024]{0,1:T(8,128)(2,1)} async-done(((bf16[128,1024]{0,1:T(8,128)(2,1)}), bf16[4096,1024]{0,1:T(8,128)(2,1)}) %all-gather.6.cloned.1.call-update) | async-done | bytes 8388624 | tf_op jit(solution)/shard_map/all_gather | solution.py:93
  72.0 5.2 %fusion.71 = (bf16[4096,512]{0,1:T(8,128)(2,1)S(1)}, bf16[4096,512]{0,1:T(8,128)(2,1)}) fusion(bf16[4096,1024]{0,1:T(8,128)(2,1)} %all-gather.6.cloned.1.call-done), kind=kLoop, calls=%fused_computation.111 | loop fusion | bytes 16777216 | tf_op jit(solution)/shard_map/slice | solution.py:27
  77.2 13.6 %fusion = (f32[4,4,128]{2,1,0:T(4,128)S(1)}, f32[4,4096,128,4]{2,1,3,0:T(8,128)}) fusion(pred[128,4096]{0,1:T(8,128)(4,1)S(1)} %fusion.34, bf16[4096,4,128,1]{0,2,3,1:T(8,128)(2,1)S(1)} %bitcast.158, bf16[128,4,4,128]{3,2,1,0:T(4,128)(2,1)S(1)} %reshape.304), kind=kOutput, calls=%fused_computation.8 | convolution fusion | flops 2172647424 | bytes 38805504 | tf_op jit(solution)/shard_map/qhgd,khd->hgqk/dot_general | solution.py:33
  90.8 14.9 %fusion.1 = f32[4,4,128]{2,1,0:T(4,128)S(1)} fusion(f32[4,4096,128,4]{2,1,3,0:T(8,128)} %get-tuple-element.8, f32[4,4,128]{2,1,0:T(4,128)S(1)} %broadcast_maximum_fusion, pred[128,4096]{0,1:T(8,128)(4,1)S(1)} %fusion.34), kind=kLoop, calls=%fused_computation.9 | loop fusion | flops 41940992 | bytes 34095104 | tf_op jit(solution)/shard_map/reduce_sum | solution.py:44
  105.8 16.5 %fusion.42 = bf16[128,4,4,128]{0,3,2,1:T(8,128)(2,1)S(1)} fusion(bf16[4096,4,128,1]{0,2,3,1:T(8,128)(2,1)} %bitcast.159, f32[4,4096,128,4]{2,1,3,0:T(8,128)} %get-tuple-element.8, f32[4,4,128]{2,1,0:T(4,128)S(1)} %broadcast_maximum_fusion, pred[128,4096]{0,1:T(8,128)(4,1)S(1)} %fusion.34, f32[128,4,4]{0,2,1:T(4,128)S(1)} %bitcast.161), kind=kOutput, calls=%fused_computation.40 | convolution fusion | flops 2189950976 | bytes 38813696 | tf_op jit(solution)/shard_map/hgqk,khd->hgqd/dot_general | solution.py:45
  123.0 1.0 multiply_convert_fusion
  125.6 1.7 reduce-window.19
  128.1 30.8 %scatter_custom_fusion = bf16[1152,2048]{1,0:T(8,128)(2,1)} fusion(s32[768]{0:T(1024)S(1)} %fusion.54, bf16[128,2048]{1,0:T(8,128)(2,1)} %multiply_convert_fusion, s32[1024]{0:T(1024)S(1)} %pad_clamp_fusion.1, bf16[]{:T(256)} %constant.47.clone.1), kind=kCustom, calls=%fused_computation.31 | custom fusion | bytes 4719104 | tf_op jit(solution)/shard_map/scatter | solution.py:120
  158.8 7.2 %reshape.307 = bf16[32,1,36,2048]{3,2,0,1:T(8,128)(2,1)} reshape(bf16[1152,2048]{1,0:T(8,128)(2,1)} %scatter_custom_fusion) | data formatting | bytes 9437184 | tf_op jit(solution)/shard_map/reshape | solution.py:122
  166.1 5.7 %all-to-all-start = ((bf16[32,1,36,2048]{3,2,1,0:T(8,128)(2,1)}), bf16[32,1,36,2048]{3,2,1,0:T(8,128)(2,1)}, u32[]{:S(2)}, u32[]{:S(2)}) async-start(bf16[32,1,36,2048]{3,2,1,0:T(8,128)(2,1)} %bitcast.157), calls=%async_computation | async-start | bytes 10485760 | tf_op jit(solution)/shard_map/all_to_all | solution.py:123
  171.7 10.0 %reduce-scatter.2.cloned.1.call-start = ((), (), s32[]{:S(2)}) async-start(), calls=%async_computation.9 | async-start | bytes 5242880 | tf_op jit(solution)/shard_map/reduce_scatter | solution.py:135
  182.6 0.7 broadcast_in_dim.29
  183.3 2.2 scatter_fusion
  185.6 5.4 %fusion.72 = f32[512,704]{0,1:T(8,128)} fusion(bf16[512,2048]{1,0:T(8,128)(2,1)} %all-gather.8.cloned.1.call-done, bf16[2048,704]{1,0:T(8,128)(2,1)} %all-gather.10.cloned.1.call-done), kind=kOutput, calls=%fused_computation.112 | convolution fusion | flops 1476395008 | bytes 6422528 | tf_op jit(solution)/shard_map/dot_general | solution.py:132
  191.0 47.1 %all-gather.12.cloned.1.call-done = bf16[2048,704]{1,0:T(8,128)(2,1)} async-done(((bf16[64,704]{1,0:T(8,128)(2,1)}), bf16[2048,704]{1,0:T(8,128)(2,1)}) %all-gather.12.cloned.1.call-update) | async-done | bytes 2883600 | tf_op jit(solution)/shard_map/all_gather | solution.py:79
  238.1 49.3 %all-gather.14.cloned.1.call-done = bf16[2048,704]{1,0:T(8,128)(2,1)} async-done(((bf16[64,704]{1,0:T(8,128)(2,1)}), bf16[2048,704]{1,0:T(8,128)(2,1)}) %all-gather.14.cloned.1.call-update) | async-done | bytes 2883600 | tf_op jit(solution)/shard_map/all_gather | solution.py:80
  287.4 9.4 %fusion.45 = f32[512,2048]{1,0:T(8,128)} fusion(bf16[2048,704]{1,0:T(8,128)(2,1)} %all-gather.14.cloned.1.call-done, bf16[512,2048]{1,0:T(8,128)(2,1)} %all-gather.8.cloned.1.call-done, bf16[2048,704]{1,0:T(8,128)(2,1)} %all-gather.12.cloned.1.call-done, f32[512,704]{0,1:T(8,128)} %fusion.72), kind=kOutput, calls=%fused_computation.45 | convolution fusion | flops 2954952704 | bytes 13500416 | tf_op jit(solution)/shard_map/dot_general | solution.py:136
  296.9 4.8 %all-to-all-start.2 = ((bf16[4,2,16,1024]{3,2,1,0:T(8,128)(2,1)}), bf16[4,2,16,1024]{3,2,1,0:T(8,128)(2,1)S(1)}, u32[]{:S(2)}, u32[]{:S(2)}) async-start(bf16[4,2,16,1024]{3,2,1,0:T(8,128)(2,1)} %scatter_fusion), calls=%async_computation.3 | async-start | bytes 524288 | tf_op jit(solution)/shard_map/all_to_all | solution.py:169
  301.7 13.8 %fusion.16 = f32[32,36,1408]{2,1,0:T(8,128)} fusion(bf16[1,2048,1408]{2,1,0:T(8,128)(2,1)} %param.21, bf16[32,1,36,2048]{3,2,1,0:T(8,128)(2,1)} %all-to-all-done), kind=kOutput, calls=%fused_computation.25 | convolution fusion | flops 6643777536 | bytes 16973824 | tf_op jit(solution)/shard_map/sjkd,jdf->sjkf/dot_general | solution.py:124
  315.5 24.5 %convert_bitcast_fusion = bf16[32,1,36,2048]{3,2,1,0:T(8,128)(2,1)} fusion(bf16[1,1408,2048]{2,1,0:T(8,128)(2,1)} %param.23, f32[32,36,1408]{2,1,0:T(8,128)} %fusion.16, bf16[1,2048,1408]{2,1,0:T(8,128)(2,1)} %param.22, bf16[32,1,36,2048]{3,2,1,0:T(8,128)(2,1)} %all-to-all-done), kind=kOutput, calls=%fused_computation.29 | convolution fusion | flops 13299646464 | bytes 27459584 | tf_op jit(solution)/shard_map/sjkf,jfd->sjkd/dot_general | solution.py:127
  340.0 5.5 %all-to-all-start.1 = ((bf16[32,1,36,2048]{3,2,1,0:T(8,128)(2,1)}), bf16[32,1,36,2048]{3,2,1,0:T(8,128)(2,1)}, u32[]{:S(2)}, u32[]{:S(2)}) async-start(bf16[32,1,36,2048]{3,2,1,0:T(8,128)(2,1)} %convert_bitcast_fusion), calls=%async_computation.1 | async-start | bytes 10485760 | tf_op jit(solution)/shard_map/all_to_all | solution.py:130
  346.6 1.6 scatter_fusion.1
  348.9 62.5 %all-to-all-done.1 = bf16[32,1,36,2048]{3,2,1,0:T(8,128)(2,1)} async-done(((bf16[32,1,36,2048]{3,2,1,0:T(8,128)(2,1)}), bf16[32,1,36,2048]{3,2,1,0:T(8,128)(2,1)}, u32[]{:S(2)}, u32[]{:S(2)}) %all-to-all-start.1) | async-done | bytes 4718624 | tf_op jit(solution)/shard_map/all_to_all | solution.py:130
  411.3 7.2 %reshape.313 = bf16[1152,2048]{1,0:T(8,128)(2,1)} reshape(bf16[32,1,36,2048]{3,2,1,0:T(8,128)(2,1)} %all-to-all-done.1) | data formatting | bytes 9437184 | tf_op jit(solution)/shard_map/reshape | solution.py:147
  418.5 10.1 %gather_fusion = bf16[768,2048]{1,0:T(8,128)(2,1)} fusion(bf16[1152,2048]{1,0:T(8,128)(2,1)} %reshape.313, s32[1024]{0:T(1024)S(1)} %pad_clamp_fusion), kind=kCustom, calls=%fused_computation.1 | custom fusion | bytes 6294528 | tf_op jit(solution)/shard_map/gather | solution.py:148
  428.6 6.6 %reshape.318 = f32[128,6,2048]{2,1,0:T(8,128)} reshape(bf16[768,2048]{1,0:T(8,128)(2,1)} %gather_fusion) | data formatting | bytes 9437184 | tf_op jit(solution)/shard_map/convert_element_type | solution.py:149
  435.2 6.5 %multiply_reduce_fusion = f32[128,2048]{1,0:T(8,128)S(1)} fusion(f32[128,6,2048]{2,1,0:T(8,128)} %reshape.318, f32[128,6]{1,0:T(8,128)S(1)} %copy.53), kind=kLoop, calls=%fused_computation.13 | loop fusion | flops 2883584 | bytes 7343104 | tf_op jit(solution)/shard_map/reduce_sum | solution.py:149
  441.7 2.3 add_convert_fusion
  (69 shorter events, 7.4 us)
Async XLA Ops:
  7.2 64.8 %all-gather.6.cloned.1.call-start = ((), (), s32[]{:S(2)}) async-start(), calls=%async_computation.4 | async-start | bytes 8650752 | tf_op jit(solution)/shard_map/all_gather | solution.py:93
  9.0 176.6 %all-gather.10.cloned.1.call-start = ((), (), s32[]{:S(2)}) async-start(), calls=%async_computation.6 | async-start | bytes 3244032 | tf_op jit(solution)/shard_map/all_gather | solution.py:78
  9.8 175.8 %all-gather.8.cloned.1.call-start = ((), (), s32[]{:S(2)}) async-start(), calls=%async_computation.5 | async-start | bytes 2621440 | tf_op jit(solution)/shard_map/all_gather | solution.py:131
  105.8 17.0 %copy-start.1 = (bf16[128,2048]{1,0:T(8,128)(2,1)S(1)}, bf16[128,2048]{1,0:T(8,128)(2,1)}, u32[]{:S(2)}) copy-start(bf16[128,2048]{1,0:T(8,128)(2,1)} %param.16) | copy-start | bytes 1572868
  122.3 2.9 copy-start.4
  124.0 114.1 %all-gather.12.cloned.1.call-start = ((), (), s32[]{:S(2)}) async-start(), calls=%async_computation.7 | async-start | bytes 3244032 | tf_op jit(solution)/shard_map/all_gather | solution.py:79
  124.6 162.9 %all-gather.14.cloned.1.call-start = ((), (), s32[]{:S(2)}) async-start(), calls=%async_computation.8 | async-start | bytes 3244032 | tf_op jit(solution)/shard_map/all_gather | solution.py:80
  166.1 15.7 %copy-start.5 = (s32[4,256]{1,0:T(4,128)S(1)}, s32[4,256]{1,0:T(4,128)}, u32[]{:S(2)}) copy-start(s32[4,256]{1,0:T(4,128)} %param.27) | copy-start | bytes 12292
  166.1 17.3 %copy-start.2 = (bf16[128,1024]{1,0:T(8,128)(2,1)S(1)}, bf16[128,1024]{1,0:T(8,128)(2,1)}, u32[]{:S(2)}) copy-start(bf16[128,1024]{1,0:T(8,128)(2,1)} %param.15) | copy-start | bytes 786436
  166.1 130.8 %all-to-all-start = ((bf16[32,1,36,2048]{3,2,1,0:T(8,128)(2,1)}), bf16[32,1,36,2048]{3,2,1,0:T(8,128)(2,1)}, u32[]{:S(2)}, u32[]{:S(2)}) async-start(bf16[32,1,36,2048]{3,2,1,0:T(8,128)(2,1)} %bitcast.157), calls=%async_computation | async-start | bytes 10485760 | tf_op jit(solution)/shard_map/all_to_all | solution.py:123
  171.7 270.0 %reduce-scatter.2.cloned.1.call-start = ((), (), s32[]{:S(2)}) async-start(), calls=%async_computation.9 | async-start | bytes 5242880 | tf_op jit(solution)/shard_map/reduce_scatter | solution.py:135
  296.9 43.1 %all-to-all-start.2 = ((bf16[4,2,16,1024]{3,2,1,0:T(8,128)(2,1)}), bf16[4,2,16,1024]{3,2,1,0:T(8,128)(2,1)S(1)}, u32[]{:S(2)}, u32[]{:S(2)}) async-start(bf16[4,2,16,1024]{3,2,1,0:T(8,128)(2,1)} %scatter_fusion), calls=%async_computation.3 | async-start | bytes 524288 | tf_op jit(solution)/shard_map/all_to_all | solution.py:169
  340.0 5.5 %copy-start.3 = (f32[128,6]{0,1:T(8,128)S(1)}, f32[128,6]{0,1:T(8,128)}, u32[]{:S(2)}) copy-start(f32[128,6]{0,1:T(8,128)} %param.20) | copy-start | bytes 9220
  340.0 71.3 %all-to-all-start.1 = ((bf16[32,1,36,2048]{3,2,1,0:T(8,128)(2,1)}), bf16[32,1,36,2048]{3,2,1,0:T(8,128)(2,1)}, u32[]{:S(2)}, u32[]{:S(2)}) async-start(bf16[32,1,36,2048]{3,2,1,0:T(8,128)(2,1)} %convert_bitcast_fusion), calls=%async_computation.1 | async-start | bytes 10485760 | tf_op jit(solution)/shard_map/all_to_all | solution.py:130
  348.2 80.4 %copy-start = (bf16[8,16,1024]{2,1,0:T(8,128)(2,1)}, bf16[8,16,1024]{2,1,0:T(8,128)(2,1)S(1)}, u32[]{:S(2)}) copy-start(bf16[8,16,1024]{2,1,0:T(8,128)(2,1)S(1)} %scatter_fusion.1) | copy-start | bytes 786436
Sparse Core Ops, SparseCore 0:
  10.7 61.1 all-gather.5
  74.2 44.5 all-gather.9
  124.1 29.2 all-gather.7
  155.5 82.5 all-gather.11
  240.2 47.2 all-gather.13
  297.0 45.3 reduce-scatter.1
where the time goes:
time: 460 us; the launch traced here: 451 us
  waiting for transfers between devices  218 us (47%)
  matrix products  83.2 us (18%)
  local copies, waits for them, and re-layouts  77.8 us (17%)
  other arithmetic  31.5 us (7%)
  starting transfers between devices  26.5 us (6%)
  between operations  14.6 us (3%)
    all_to_all x1, waiting for transfers between devices, on_device(): lax.all_to_all(expert_out, 'exp', split_axis=0, concat_axis=0, tiled=True)  62.5 us
    all_gather x1, waiting for transfers between devices, on_device(): lax.all_gather(keys_then_values, 'exp', axis=0, tiled=True)  57.1 us
    all_gather x1, waiting for transfers between devices, on_device(): lax.all_gather(w_shared_down, 'exp', axis=0, tiled=True)  49.3 us
    all_gather x1, waiting for transfers between devices, on_device(): lax.all_gather(w_shared_up, 'exp', axis=0, tiled=True)  47.1 us
    scatter x1, local copies, waits for them, and re-layouts, on_device(): jnp.zeros((experts * capacity, D), jnp.bfloat16).at[slot_index]  30.8 us
    dot_general x1, matrix products, on_device(): jnp.einsum('sjkf,jfd->sjkd', activated, w_down, preferred_element_type=jn...  24.5 us
    dot_general x1, matrix products, attend_piece(): jnp.einsum('hgqk,khd->hgqd', softmax_p.astype(jnp.bfloat16), value_row_bl...  16.5 us
    reduce_sum x1, other arithmetic, attend_piece(): run_sum = jnp.sum(softmax_p, axis=3)  14.9 us
  transfers between devices with their start and end apart: 9, of which 4 were waited for; matrix products, arithmetic and copies ran while one was open for 42% of the time, Pallas kernels for 0%

commit v1 on v0

v1 whole, which is shorter than its diff:
```python
import functools

import jax
import jax.numpy as jnp
from jax import lax
from jax.experimental import pallas as pl
from jax.experimental.pallas import tpu as pltpu
from jax.sharding import PartitionSpec as P

D = 2048
QUERY_HEADS = 16
KEY_VALUE_HEADS = 4
HEAD_SIZE = 128
FF = 1408
TOPK = 6
PAGE = 16
CAP = 36
TOK = 128
SPAD = 768
MAXLEN = 3072
eps_norm = 1e-06
MESH = pl.DeviceIdType.MESH
CODES = (0, 1, -1, 2)
ANY = pl.BlockSpec(memory_space=pl.ANY)
VM = pl.BlockSpec(memory_space=pltpu.VMEM)
SM = pl.BlockSpec(memory_space=pltpu.SMEM)
F32 = jnp.float32
BF16 = jnp.bfloat16
VMEM_LIMIT = 62 * 1024 * 1024


class Place:
    def __init__(self):
        c = lax.axis_index("exp")
        self.c = c
        self.r = lax.axis_index("req")
        self.z = c // 8
        self.x = lax.rem(c // 2, 4)
        self.k = lax.rem(c, 2)
        self.partner = c + 1 - 2 * self.k

    def at(self, dx, dz):
        return lax.rem(self.z + dz + 4, 4) * 8 + lax.rem(self.x + dx + 4, 4) * 2 + self.k

    def step(self, dim, s):
        return self.at(s, 0) if dim == "x" else self.at(0, s)

    def up(self, s):
        return lax.rem(self.r + s + 4, 4)

    def barrier(self, along_y):
        sem = pltpu.get_barrier_semaphore()
        peers = [self.at(1, 0), self.at(-1, 0), self.at(0, 1), self.at(0, -1), self.partner]
        for p in peers:
            pl.semaphore_signal(sem, inc=1, device_id={"exp": p}, device_id_type=MESH)
        for s in along_y:
            pl.semaphore_signal(sem, inc=1, device_id={"req": self.up(s)}, device_id_type=MESH)
        pl.semaphore_wait(sem, len(peers) + len(along_y))


def route(q):
    first, second = ("x", "z") if q < 2 else ("z", "x")
    return first, second, (1 if q % 2 == 0 else -1)


def shift(q, a, b):
    first, _, t = route(q)
    u, v = CODES[a] * t, CODES[b] * t
    return (u, v) if first == "x" else (v, u)


def hop(code, t):
    return -t if code == 2 else t


def depth(a, b):
    return abs(CODES[a]) + abs(CODES[b])


def children(q, a, b):
    first, second, t = route(q)
    out = []
    if b == 0:
        if a == 0:
            out += [(first, t, 1, 0), (first, -t, 2, 0)]
        elif a == 1:
            out += [(first, t, 3, 0)]
        out += [(second, t, a, 1), (second, -t, a, 2)]
    elif b == 1:
        out += [(second, t, a, 3)]
    return out


class Gather:
    def __init__(self, place, own, every, rows, pieces, send_sem, recv_sem, pair_sem):
        self.p, self.own, self.every, self.rows, self.pieces = place, own, every, rows, pieces
        self.rq = rows // pieces
        self.send_sem, self.recv_sem, self.pair_sem = send_sem, recv_sem, pair_sem

    def slot(self, src, q):
        return self.every.at[pl.ds(pl.multiple_of(src * self.rows + q * self.rq, self.rq), self.rq)]

    def block(self, src):
        return self.every.at[pl.ds(pl.multiple_of(src * self.rows, self.rows), self.rows)]

    def source(self, q, a, b):
        dx, dz = shift(q, a, b)
        return self.p.at(-dx, -dz)

    def recv_of(self, q, a, b):
        return self.recv_sem.at[q * 15 + a * 4 + b - 1]

    def pass_on(self, q, a, b):
        src = self.source(q, a, b)
        ref = self.own.at[pl.ds(q * self.rq, self.rq)] if a == 0 and b == 0 else self.slot(src, q)
        for dim, s, na, nb in children(q, a, b):
            pltpu.make_async_remote_copy(
                ref, self.slot(src, q), self.send_sem, self.recv_of(q, na, nb),
                device_id={"exp": self.p.step(dim, s)}, device_id_type=MESH,
            ).start()

    def to_pair(self, ref, dst):
        pltpu.make_async_remote_copy(
            ref, dst, self.send_sem, self.pair_sem,
            device_id={"exp": self.p.partner}, device_id_type=MESH,
        ).start()

    def start(self):
        for q in range(self.pieces):
            self.pass_on(q, 0, 0)
        self.to_pair(self.own, self.block(self.p.c))

    def events(self):
        out = []
        for q in range(self.pieces):
            for a in range(4):
                for b in range(4):
                    if a or b:
                        out.append((depth(a, b), b, a, q))
        return sorted(out)

    def take(self, ev):
        _, b, a, q = ev
        ref = self.slot(self.source(q, a, b), q)
        pltpu.make_async_remote_copy(
            ref, ref, self.send_sem, self.recv_of(q, a, b),
            device_id={"exp": self.p.partner}, device_id_type=MESH,
        ).wait_recv()
        self.pass_on(q, a, b)
        self.to_pair(ref, ref)

    def wait_pair(self):
        ref = self.every.at[pl.ds(0, 16 * self.rows)]
        pltpu.make_async_remote_copy(
            ref, ref, self.send_sem, self.pair_sem,
            device_id={"exp": self.p.partner}, device_id_type=MESH,
        ).wait_recv()

    def drain(self):
        ref = self.every.at[pl.ds(0, 31 * self.rows)]
        pltpu.make_async_copy(ref, ref, self.send_sem).wait()


class RingY:
    def __init__(self, place, own, every, rows, send_sem, recv_sem):
        self.p, self.own, self.every, self.rows = place, own, every, rows
        self.h = rows // 2
        self.send_sem, self.recv_sem = send_sem, recv_sem

    def slot(self, src, q):
        return self.every.at[pl.ds(pl.multiple_of(src * self.rows + q * self.h, self.h), self.h)]

    def send(self, ref, src, q, s, code):
        pltpu.make_async_remote_copy(
            ref, self.slot(src, q), self.send_sem, self.recv_sem.at[q * 3 + code - 1],
            device_id={"req": self.p.up(s)}, device_id_type=MESH,
        ).start()

    def start(self):
        for q, t in ((0, 1), (1, -1)):
            ref = self.own.at[pl.ds(q * self.h, self.h)]
            self.send(ref, self.p.r, q, t, 1)
            self.send(ref, self.p.r, q, -t, 2)

    def finish(self):
        for code in (1, 2, 3):
            for q, t in ((0, 1), (1, -1)):
                src = self.p.up(-CODES[code] * t)
                ref = self.slot(src, q)
                pltpu.make_async_remote_copy(
                    ref, ref, self.send_sem, self.recv_sem.at[q * 3 + code - 1],
                    device_id={"req": self.p.up(1)}, device_id_type=MESH,
                ).wait_recv()
                if code == 1:
                    self.send(ref, src, q, t, 3)

    def drain(self):
        ref = self.every.at[pl.ds(0, 3 * self.rows)]
        pltpu.make_async_copy(ref, ref, self.send_sem).wait()


def kernel_gather(kv_ref, w_ref, meta_ref, kv_all, w_all, meta_all, pg_all,
                  kv_r, w_r, meta_r, pg_r, send, pair, local):
    p = Place()
    p.barrier((1, -1))
    kv = Gather(p, kv_ref, kv_all, TOK, 4, send.at[0], kv_r, pair.at[0])
    w = Gather(p, w_ref, w_all, 64, 4, send.at[1], w_r, pair.at[1])
    meta = Gather(p, meta_ref, meta_all, 16, 1, send.at[2], meta_r, pair.at[2])
    pages = RingY(p, kv_ref, pg_all, TOK, send.at[3], pg_r)
    owns = [pltpu.make_async_copy(g.own, g.block(p.c), local.at[i]) for i, g in enumerate((kv, w, meta))]
    owns.append(pltpu.make_async_copy(kv_ref, pg_all.at[pl.ds(pl.multiple_of(p.r * TOK, TOK), TOK)], local.at[3]))
    meta.start()
    kv.start()
    pages.start()
    for c in owns:
        c.start()
    evs = kv.events()
    for ev in evs[:16]:
        kv.take(ev)
    w.start()
    for ev in evs[16:]:
        kv.take(ev)
    for ev in meta.events():
        meta.take(ev)
    pages.finish()
    for ev in w.events():
        w.take(ev)
    for g in (kv, w, meta):
        g.wait_pair()
        g.drain()
    pages.drain()
    for c in owns:
        c.wait()


def call_gather(kv, wcat, meta):
    return pl.pallas_call(
        kernel_gather,
        out_shape=(
            jax.ShapeDtypeStruct((32 * TOK, 1024), BF16),
            jax.ShapeDtypeStruct((D, 3 * SPAD), BF16),
            jax.ShapeDtypeStruct((512, 128), F32),
            jax.ShapeDtypeStruct((512, 1024), BF16),
        ),
        in_specs=[VM] * 3,
        out_specs=(ANY,) * 4,
        scratch_shapes=[
            pltpu.SemaphoreType.DMA((60,)),
            pltpu.SemaphoreType.DMA((60,)),
            pltpu.SemaphoreType.DMA((15,)),
            pltpu.SemaphoreType.DMA((6,)),
            pltpu.SemaphoreType.DMA((4,)),
            pltpu.SemaphoreType.DMA((3,)),
            pltpu.SemaphoreType.DMA((4,)),
        ],
        compiler_params=pltpu.CompilerParams(collective_id=0, has_side_effects=True, vmem_limit_bytes=VMEM_LIMIT),
        name="gather_start",
    )(kv, wcat, meta)


def kernel_rows(n_ref, n_all, y_all, n_r, y_r, send, pair, local):
    p = Place()
    p.barrier((1, -1))
    g = Gather(p, n_ref, n_all, TOK, 4, send.at[0], n_r, pair.at[0])
    y = RingY(p, n_ref, y_all, TOK, send.at[1], y_r)
    owns = [
        pltpu.make_async_copy(n_ref, g.block(p.c), local.at[0]),
        pltpu.make_async_copy(n_ref, y_all.at[pl.ds(pl.multiple_of(p.r * TOK, TOK), TOK)], local.at[1]),
    ]
    g.start()
    y.start()
    for c in owns:
        c.start()
    evs = g.events()
    for ev in evs[:32]:
        g.take(ev)
    y.finish()
    for ev in evs[32:]:
        g.take(ev)
    g.wait_pair()
    g.drain()
    y.drain()
    for c in owns:
        c.wait()


def call_rows(normed):
    return pl.pallas_call(
        kernel_rows,
        out_shape=(
            jax.ShapeDtypeStruct((32 * TOK, D), BF16),
            jax.ShapeDtypeStruct((512, D), BF16),
        ),
        in_specs=[VM],
        out_specs=(ANY, ANY),
        scratch_shapes=[
            pltpu.SemaphoreType.DMA((60,)),
            pltpu.SemaphoreType.DMA((6,)),
            pltpu.SemaphoreType.DMA((2,)),
            pltpu.SemaphoreType.DMA((1,)),
            pltpu.SemaphoreType.DMA((2,)),
        ],
        compiler_params=pltpu.CompilerParams(collective_id=1, has_side_effects=True, vmem_limit_bytes=VMEM_LIMIT),
        name="gather_rows",
    )(normed)


def attend(c, q_ref, kv_ref, ends_ref, res_ref, gain_ref, hid_ref, normed_ref, lt_ref,
           qs, m_s, l_s, acc_s, lt_s):
    rows = 4 * TOK
    for h in range(QUERY_HEADS):
        qs[pl.ds(h * TOK, TOK), :] = q_ref[:, h * HEAD_SIZE:(h + 1) * HEAD_SIZE]
    qpos = c * TOK + lax.broadcasted_iota(jnp.int32, (TOK, 128), 0)
    ends = jnp.broadcast_to(ends_ref[...], (TOK, 128))
    begin = jnp.max(jnp.where(ends <= qpos, ends, 0).astype(F32), axis=1, keepdims=True).astype(jnp.int32)
    m_s[...] = jnp.full_like(m_s, -5e29)
    l_s[...] = jnp.zeros_like(l_s)
    acc_s[...] = jnp.zeros_like(acc_s)
    lt_s[...] = jnp.zeros_like(lt_s)
    first = jnp.maximum(c * TOK - MAXLEN, 0) // 256
    last = c // 2

    def chunk(i, _):
        k0 = pl.multiple_of(i * 256, 256)
        kpos = k0 + lax.broadcasted_iota(jnp.int32, (TOK, 256), 1)
        qp = c * TOK + lax.broadcasted_iota(jnp.int32, (TOK, 256), 0)
        seen = (kpos >= begin) & (kpos <= qp)
        bias = jnp.where(seen, 0.0, -1e30).astype(F32)
        bias = jnp.concatenate([bias] * 4, axis=0)
        for g in range(KEY_VALUE_HEADS):
            at = pl.ds(g * rows, rows)
            keys = kv_ref[pl.ds(k0, 256), g * HEAD_SIZE:(g + 1) * HEAD_SIZE]
            values = kv_ref[pl.ds(k0, 256), 512 + g * HEAD_SIZE:512 + (g + 1) * HEAD_SIZE]
            s = lax.dot_general(qs[at, :], keys, (((1,), (1,)), ((), ())), preferred_element_type=F32)
            s = s * HEAD_SIZE ** (-0.5) + bias
            old = m_s[at, :]
            new = jnp.maximum(old, jnp.max(s, axis=1, keepdims=True))
            e = jnp.exp(s - new)
            alpha = jnp.exp(old - new)
            m_s[at, :] = new
            l_s[at, :] = l_s[at, :] * alpha + jnp.sum(e, axis=1, keepdims=True)
            acc_s[at, :] = acc_s[at, :] * alpha + jnp.dot(e.astype(BF16), values, preferred_element_type=F32)
        return 0

    lax.fori_loop(first, last + 1, chunk, 0)
    total = jnp.zeros((TOK, 1), F32)
    for h in range(QUERY_HEADS):
        at = pl.ds(h * TOK, TOK)
        cols = slice(h * HEAD_SIZE, (h + 1) * HEAD_SIZE)
        att = (acc_s[at, :] / l_s[at, :]).astype(BF16)
        lt_s[:, h:h + 1] = m_s[at, :] + jnp.log(l_s[at, :])
        hid = res_ref[:, cols].astype(F32) + att.astype(F32)
        hid_ref[:, cols] = hid
        total = total + jnp.sum(hid * hid, axis=1, keepdims=True)
    scale = lax.rsqrt(total * (1.0 / D) + eps_norm)
    for h in range(QUERY_HEADS):
        cols = slice(h * HEAD_SIZE, (h + 1) * HEAD_SIZE)
        normed_ref[:, cols] = (hid_ref[:, cols] * scale * gain_ref[:, cols].astype(F32)).astype(BF16)
    lt_ref[...] = jnp.transpose(lt_s[...])[:QUERY_HEADS, :]


def kernel_attend(inv_ref, q_ref, kv_ref, ends_ref, res_ref, gain_ref, pg_ref,
                  hid_ref, normed_ref, lt_ref, cache_ref, qs, m_s, l_s, acc_s, lt_s, sem):
    copies = []
    for i in range(8):
        copies.append(pltpu.make_async_copy(pg_ref.at[inv_ref[0, i]], cache_ref.at[i], sem.at[i]))
        copies[-1].start()
    attend(lax.axis_index("exp"), q_ref, kv_ref, ends_ref, res_ref, gain_ref, hid_ref, normed_ref, lt_ref,
           qs, m_s, l_s, acc_s, lt_s)
    for c in copies:
        c.wait()


def attend_scratch():
    n = QUERY_HEADS * TOK
    return [
        pltpu.VMEM((n, HEAD_SIZE), BF16),
        pltpu.VMEM((n, 1), F32),
        pltpu.VMEM((n, 1), F32),
        pltpu.VMEM((n, HEAD_SIZE), F32),
        pltpu.VMEM((TOK, 128), F32),
    ]


def call_attend(inv, q, kv_all, ends, res, gain, pg_all):
    return pl.pallas_call(
        kernel_attend,
        out_shape=(
            jax.ShapeDtypeStruct((TOK, D), F32),
            jax.ShapeDtypeStruct((TOK, D), BF16),
            jax.ShapeDtypeStruct((QUERY_HEADS, TOK), F32),
            jax.ShapeDtypeStruct((8, PAGE, 1024), BF16),
        ),
        in_specs=[SM, VM, VM, VM, VM, VM, ANY],
        out_specs=(VM, VM, VM, VM),
        scratch_shapes=attend_scratch() + [pltpu.SemaphoreType.DMA((8,))],
        compiler_params=pltpu.CompilerParams(vmem_limit_bytes=VMEM_LIMIT),
        name="attend",
    )(inv, q, kv_all, ends, res, gain, pg_all.reshape(32, PAGE, 1024))


def silu_mul(g, u):
    return (g / (1.0 + jnp.exp(-g)) * u).astype(BF16)


def shared_part(rows_ref, w_ref, act_s, out_ref):
    def up(j, _):
        col = pl.multiple_of(j * 256, 256)
        g = jnp.dot(rows_ref[...], w_ref[:, pl.ds(col, 256)], preferred_element_type=F32)
        u = jnp.dot(rows_ref[...], w_ref[:, pl.ds(SPAD + col, 256)], preferred_element_type=F32)
        act_s[:, pl.ds(col, 256)] = silu_mul(g, u)
        return 0

    lax.fori_loop(0, 3, up, 0)

    def down(j, _):
        col = pl.multiple_of(j * 256, 256)
        o = lax.dot_general(act_s[...], w_ref[pl.ds(col, 256), 2 * SPAD:], (((1,), (1,)), ((), ())),
                            preferred_element_type=F32)
        out_ref[:, pl.ds(col, 256)] = o.astype(BF16)
        return 0

    lax.fori_loop(0, 8, down, 0)


def kernel_shared(rows_ref, w_ref, out_ref, act_s):
    shared_part(rows_ref, w_ref, act_s, out_ref)


def call_shared(rows, w_all):
    return pl.pallas_call(
        kernel_shared,
        out_shape=jax.ShapeDtypeStruct((512, D), BF16),
        in_specs=[VM, VM],
        out_specs=VM,
        scratch_shapes=[pltpu.VMEM((512, SPAD), BF16)],
        compiler_params=pltpu.CompilerParams(vmem_limit_bytes=VMEM_LIMIT),
        name="shared",
    )(rows, w_all)


def plan_rows(e, meta_ref, tgt_s, wt_s):
    tgt_s[...] = jnp.zeros_like(tgt_s)
    for s in range(32):
        ids = meta_ref[pl.ds(s * 16, 8), :]
        wts = meta_ref[pl.ds(s * 16 + 8, 8), :]
        hit = jnp.where(ids == e, 1.0, 0.0).astype(F32)
        tgt_s[s:s + 1, :] = jnp.sum(hit, axis=0, keepdims=True)
        wt_s[s:s + 1, :] = jnp.sum(hit * wts, axis=0, keepdims=True)
    sel = tgt_s[...]
    i0 = lax.broadcasted_iota(jnp.int32, (128, 128), 0)
    i1 = lax.broadcasted_iota(jnp.int32, (128, 128), 1)
    tri = jnp.where(i0 <= i1, 1.0, 0.0).astype(BF16)
    rank = jnp.dot(sel.astype(BF16), tri, preferred_element_type=F32)
    src = lax.rem(lax.broadcasted_iota(jnp.int32, (32, 128), 0), 4).astype(F32)
    tgt_s[...] = jnp.where(sel > 0.5, src * CAP + rank - 1.0, -1.0)


def pick(tgt_s, wt_s, s0):
    t4 = tgt_s[s0:s0 + 4, :]
    w4 = wt_s[s0:s0 + 4, :]
    trow = jnp.concatenate([t4[i:i + 1, :] for i in range(4)], axis=1)
    wrow = jnp.concatenate([w4[i:i + 1, :] for i in range(4)], axis=1)
    lane = lax.broadcasted_iota(jnp.int32, (4 * CAP, 512), 0).astype(F32)
    hit = lane == trow
    return jnp.where(hit, 1.0, 0.0).astype(BF16), jnp.sum(jnp.where(hit, wrow, 0.0), axis=1, keepdims=True)


def expert_up(x_s, wg, wu, act_s):
    def tile(col, n):
        g = jnp.dot(x_s[...], wg[:, pl.ds(col, n)], preferred_element_type=F32)
        u = jnp.dot(x_s[...], wu[:, pl.ds(col, n)], preferred_element_type=F32)
        act_s[:, pl.ds(col, n)] = silu_mul(g, u)

    def body(j, _):
        tile(pl.multiple_of(j * 256, 256), 256)
        return 0

    lax.fori_loop(0, 5, body, 0)
    tile(1280, 128)


def expert_down(act_s, wd, wcol, y_s):
    def body(j, _):
        col = pl.multiple_of(j * 256, 256)
        o = jnp.dot(act_s[...], wd[:, pl.ds(col, 256)], preferred_element_type=F32)
        y_s[:, pl.ds(col, 256)] = (o * wcol).astype(BF16)
        return 0

    lax.fori_loop(0, 8, body, 0)


def kernel_expert(meta_ref, n_all, wg_h, wu_h, wd_h, out,
                  wg, wu, wd, rows_s, x_s, act_s, y_s, o_s, tgt_s, wt_s, w_sem, in_sem, out_sem):
    e = lax.axis_index("exp").astype(F32)
    loads = [pltpu.make_async_copy(n_all.at[pl.ds(i * 1024, 1024)], rows_s.at[i % 2], in_sem.at[i % 2]) for i in range(4)]
    stores = [pltpu.make_async_copy(o_s.at[i % 2], out.at[pl.ds(i * 1024, 1024)], out_sem.at[i % 2]) for i in range(4)]
    ws = [pltpu.make_async_copy(a.at[0], b, w_sem.at[i]) for i, (a, b) in enumerate(((wg_h, wg), (wu_h, wu), (wd_h, wd)))]
    loads[0].start()
    for w in ws:
        w.start()
    plan_rows(e, meta_ref, tgt_s, wt_s)
    for i in range(4):
        if i + 1 < 4:
            loads[i + 1].start()
        loads[i].wait()
        hits, wcols = [], []
        for j in range(2):
            hit, wcol = pick(tgt_s, wt_s, i * 8 + j * 4)
            hits.append(hit)
            wcols.append(wcol)

            def fetch(n, _, j=j, hit=hit, i=i):
                col = pl.multiple_of(n * 256, 256)
                x_s[pl.ds(j * 144, 144), pl.ds(col, 256)] = jnp.dot(
                    hit, rows_s[i % 2, pl.ds(j * 512, 512), pl.ds(col, 256)], preferred_element_type=F32).astype(BF16)
                return 0

            lax.fori_loop(0, 8, fetch, 0)
        if i == 0:
            ws[0].wait()
            ws[1].wait()
        expert_up(x_s, wg, wu, act_s)
        if i == 0:
            ws[2].wait()
        expert_down(act_s, wd, jnp.concatenate(wcols, axis=0), y_s)
        if i >= 2:
            stores[i - 2].wait()
        for j in range(2):
            def put(n, _, j=j, hit=hits[j], i=i):
                col = pl.multiple_of(n * 256, 256)
                o_s[i % 2, pl.ds(j * 512, 512), pl.ds(col, 256)] = lax.dot_general(
                    hit, y_s[pl.ds(j * 144, 144), pl.ds(col, 256)], (((0,), (0,)), ((), ())),
                    preferred_element_type=F32).astype(BF16)
                return 0

            lax.fori_loop(0, 8, put, 0)
        stores[i].start()
    stores[2].wait()
    stores[3].wait()


def call_expert(meta_all, n_all, wg, wu, wd):
    return pl.pallas_call(
        kernel_expert,
        out_shape=jax.ShapeDtypeStruct((32 * TOK, D), BF16),
        in_specs=[VM, ANY, ANY, ANY, ANY],
        out_specs=ANY,
        scratch_shapes=[
            pltpu.VMEM((D, FF), BF16),
            pltpu.VMEM((D, FF), BF16),
            pltpu.VMEM((FF, D), BF16),
            pltpu.VMEM((2, 1024, D), BF16),
            pltpu.VMEM((8 * CAP, D), BF16),
            pltpu.VMEM((8 * CAP, FF), BF16),
            pltpu.VMEM((8 * CAP, D), BF16),
            pltpu.VMEM((2, 1024, D), BF16),
            pltpu.VMEM((32, 128), F32),
            pltpu.VMEM((32, 128), F32),
            pltpu.SemaphoreType.DMA((3,)),
            pltpu.SemaphoreType.DMA((2,)),
            pltpu.SemaphoreType.DMA((2,)),
        ],
        compiler_params=pltpu.CompilerParams(vmem_limit_bytes=VMEM_LIMIT),
        name="expert",
    )(meta_all, n_all, wg, wu, wd)


def kernel_return(hid_ref, parts, sh, out_ref, mine, pair, rbuf, shbuf, load_sem, pair_sem, recv_sem,
                  sh_recv, send):
    p = Place()
    p.barrier((1, -1, 2))
    offs = sorted(((dx, dz) for dx in CODES for dz in CODES), key=lambda o: -abs(o[0]) - abs(o[1]))

    def blk(dev):
        return parts.at[pl.ds(pl.multiple_of(dev * TOK, TOK), TOK)]

    loads, pairs = {}, {}
    for j, (dx, dz) in enumerate(offs):
        dest = p.at(-dx, -dz)
        other = dest + 1 - 2 * p.k
        loads[dx, dz] = pltpu.make_async_copy(blk(dest), mine.at[j], load_sem.at[j])
        pairs[dx, dz] = pltpu.make_async_remote_copy(
            blk(other), pair.at[j], send.at[0], pair_sem.at[j],
            device_id={"exp": p.partner}, device_id_type=MESH)
        loads[dx, dz].start()
        pairs[dx, dz].start()
    shares = []
    for i, s in enumerate((1, -1, 2)):
        shares.append(pltpu.make_async_remote_copy(
            sh.at[pl.ds(pl.multiple_of(p.up(s) * TOK, TOK), TOK)], shbuf.at[i], send.at[1], sh_recv.at[i],
            device_id={"req": p.up(s)}, device_id_type=MESH))
        shares[-1].start()
    sh_own = pltpu.make_async_copy(sh.at[pl.ds(pl.multiple_of(p.r * TOK, TOK), TOK)], shbuf.at[3], sh_recv.at[3])
    sh_own.start()
    done = set()
    nodes = sorted(((-depth(a, b), b, a, q) for q in range(4) for a in range(4) for b in range(4)))
    for _, b, a, q in nodes:
        o = shift(q, a, b)
        o = tuple(2 if v == -2 else v for v in o)
        j = offs.index(o)
        if o not in done:
            done.add(o)
            loads[o].wait()
            pairs[o].wait_recv()
        kids = []
        for _, _, na, nb in children(q, a, b):
            i = q * 15 + na * 4 + nb - 1
            kids.append(i)
            pltpu.make_async_remote_copy(
                rbuf.at[i], rbuf.at[i], send.at[2], recv_sem.at[i],
                device_id={"exp": p.partner}, device_id_type=MESH).wait_recv()
        rows = pl.ds(q * 32, 32)
        root = a == 0 and b == 0
        if root and q == 0:
            for s in shares:
                s.wait_recv()
            sh_own.wait()

        def add(n, _, j=j, kids=kids, rows=rows, root=root):
            cols = pl.ds(pl.multiple_of(n * 256, 256), 256)
            v = mine[j, rows, cols].astype(F32) + pair[j, rows, cols].astype(F32)
            for i in kids:
                v = v + rbuf[i, :, cols].astype(F32)
            if root:
                t = shbuf[3, rows, cols].astype(F32)
                for i in range(3):
                    t = t + shbuf[i, rows, cols].astype(F32)
                out_ref[rows, cols] = (hid_ref[rows, cols] + v + t).astype(BF16)
            else:
                mine[j, rows, cols] = v.astype(BF16)
            return 0

        lax.fori_loop(0, 8, add, 0)
        if not root:
            first, second, t = route(q)
            dim, code = (second, b) if b else (first, a)
            i = q * 15 + a * 4 + b - 1
            pltpu.make_async_remote_copy(
                mine.at[j, rows], rbuf.at[i], send.at[2], recv_sem.at[i],
                device_id={"exp": p.step(dim, -hop(code, t))}, device_id_type=MESH).start()
    ref = mine
    pltpu.make_async_copy(ref, ref, send.at[0]).wait()
    ref = shbuf.at[pl.ds(0, 3)]
    pltpu.make_async_copy(ref, ref, send.at[1]).wait()
    pltpu.make_async_copy(rbuf, rbuf, send.at[2]).wait()


def call_return(hid, parts, sh):
    return pl.pallas_call(
        kernel_return,
        out_shape=jax.ShapeDtypeStruct((TOK, D), BF16),
        in_specs=[VM, ANY, ANY],
        out_specs=VM,
        scratch_shapes=[
            pltpu.VMEM((16, TOK, D), BF16),
            pltpu.VMEM((16, TOK, D), BF16),
            pltpu.VMEM((60, 32, D), BF16),
            pltpu.VMEM((4, TOK, D), BF16),
            pltpu.SemaphoreType.DMA((16,)),
            pltpu.SemaphoreType.DMA((16,)),
            pltpu.SemaphoreType.DMA((60,)),
            pltpu.SemaphoreType.DMA((4,)),
            pltpu.SemaphoreType.DMA((3,)),
        ],
        compiler_params=pltpu.CompilerParams(collective_id=2, has_side_effects=True, vmem_limit_bytes=VMEM_LIMIT),
        name="give_back",
    )(hid, parts, sh)


def on_device(queries, keys_then_values, residual, norm_gain, prompt_lengths, expert_ids, router_logits,
              w_gate, w_up, w_down, w_shared_gate, w_shared_up, w_shared_down, page_table):
    c = lax.axis_index("exp")
    r = lax.axis_index("req")
    pad = ((0, 0), (0, SPAD - 704))
    wcat = jnp.concatenate([jnp.pad(w, pad) for w in (w_shared_gate, w_shared_up, w_shared_down)], axis=1)
    weights = jax.nn.softmax(router_logits, axis=-1)
    two = ((0, 0), (0, 2))
    meta = jnp.concatenate([
        jnp.pad(expert_ids.astype(F32), two, constant_values=-1.0), jnp.pad(weights, two)], axis=1).T
    lengths = prompt_lengths[0]
    upto = jnp.arange(16)[:, None] >= jnp.arange(16)[None, :]
    ends = jnp.sum(jnp.where(upto, lengths[None, :], 0), axis=1)
    ends = jnp.pad(ends, (0, 112), constant_values=1 << 20).reshape(1, 128)
    cols = lax.dynamic_slice_in_dim(page_table, c * 8, 8, 1) - (r * 256 + c * 8)
    where_from = jnp.arange(32, dtype=jnp.int32).reshape(4, 8, 1)
    inv = jnp.sum(jnp.where(cols[:, :, None] == jnp.arange(8)[None, None, :], where_from, 0), axis=(0, 1))

    kv_all, w_all, meta_all, pg_all = call_gather(keys_then_values, wcat, meta)
    hid, normed, log_totals, cache = call_attend(
        inv.reshape(1, 8).astype(jnp.int32), queries, kv_all, ends, residual, norm_gain.reshape(1, D), pg_all)
    n_all, y_all = call_rows(normed)
    sh = call_shared(y_all, w_all)
    parts = call_expert(meta_all, n_all, w_gate, w_up, w_down)
    out = call_return(hid, parts, sh)
    return out, cache, log_totals


def solution(mesh):
    tok = P(("req", "exp"), None)
    ex = P("exp", None, None)
    sh = P("exp", "req")
    return jax.shard_map(
        on_device,
        mesh=mesh,
        in_specs=(tok, tok, tok, P(), P("req", None), tok, tok, ex, ex, ex, sh, sh, sh, P()),
        out_specs=(tok, P(("req", "exp"), None, None), P(None, ("req", "exp"))),
        check_vma=False,
    )
```

time: 460 us -> 319 us (0.69); the launches traced: 451 us -> 317 us
  Pallas kernels: 0 us -> 305 us
  waiting for transfers between devices: 218 us -> 0 us
  matrix products: 83.2 us -> 0 us
  local copies, waits for them, and re-layouts: 77.8 us -> 3.75 us
  starting transfers between devices: 26.5 us -> 0 us
  other arithmetic: 31.5 us -> 7.33 us
  between operations: 14.6 us -> 0.68 us
    pallas_call x0 -> x6, Pallas kernels: none -> 305 us  [the longest x1 84.7 us: call_rows(): pl.pallas_call(kernel_rows, out_shape=(jax.ShapeDtypeStruct((32 * TOK, D)...]
    all_gather x5 -> x0, waiting for transfers between devices: 154 us -> none  [the longest x1 57.1 us: on_device(): lax.all_gather(keys_then_values, 'exp', axis=0, tiled=True)]
    dot_general x6 -> x0, matrix products: 83.2 us -> none  [the longest x1 24.5 us: on_device(): jnp.einsum('sjkf,jfd->sjkd', activated, w_down, preferred_element_type=jn...]
    all_to_all x3 -> x0, waiting for transfers between devices: 62.5 us -> none  [the longest x1 62.5 us: on_device(): lax.all_to_all(expert_out, 'exp', split_axis=0, concat_axis=0, tiled=True)]
    scatter x3 -> x0, local copies, waits for them, and re-layouts: 34.7 us -> none  [the longest x1 30.8 us: on_device(): jnp.zeros((experts * capacity, D), jnp.bfloat16).at[slot_index]]
    reduce_sum x7 -> x2, other arithmetic: 22 us -> 1.45 us  [the longest x1 0.77 us: on_device(): ends = jnp.sum(jnp.where(upto, lengths[None, :], 0), axis=1)]
    all_to_all x3 -> x0, starting transfers between devices: 16 us -> none  [the longest x1 5.65 us: on_device(): lax.all_to_all(send_rows, 'exp', split_axis=0, concat_axis=0, tiled=True)]
    reshape x4 -> x2, local copies, waits for them, and re-layouts: 15.9 us -> 1.87 us  [the longest x1 1.29 us: on_device(): norm_gain.reshape(1, D)]
  transfers between devices with their start and end apart: 9 -> 0, of which waited for: 4 -> 0; matrix products, arithmetic and copies ran while one was open for 42% -> 0% of each run, Pallas kernels for 0% -> 0%
where the time goes in v1:
time: 319 us; the launch traced here: 317 us
  Pallas kernels  305 us (96%)
  other arithmetic  7.33 us (2%)
  local copies, waits for them, and re-layouts  3.75 us (1%)
    pallas_call x1, Pallas kernels, call_rows(): pl.pallas_call(kernel_rows, out_shape=(jax.ShapeDtypeStruct((32 * TOK, D)...  84.7 us
    pallas_call x1, Pallas kernels, call_expert(): pl.pallas_call(kernel_expert, out_shape=jax.ShapeDtypeStruct((32 * TOK, D...  72.8 us
    pallas_call x1, Pallas kernels, call_gather(): pl.pallas_call(kernel_gather, out_shape=(jax.ShapeDtypeStruct((32 * TOK,...  70 us
    pallas_call x1, Pallas kernels, call_return(): pl.pallas_call(kernel_return, out_shape=jax.ShapeDtypeStruct((TOK, D), BF...  55.3 us
    pallas_call x1, Pallas kernels, call_shared(): pl.pallas_call(kernel_shared, out_shape=jax.ShapeDtypeStruct((512, D), BF...  12.8 us
    pallas_call x1, Pallas kernels, call_attend(): pl.pallas_call(kernel_attend, out_shape=(jax.ShapeDtypeStruct((TOK, D), F...  9.83 us

profile of v1, /device:TPU:8, one launch (start us, length us, event | category | flops | bytes accessed | tf_op | source)
XLA Modules:
  0.0 317.1 jit_solution(5299808709155947874)
XLA Ops:
  0.6 0.7 reduce_max.9
  1.3 0.7 fusion.8
  2.0 0.8 select_reduce_fusion.1
  2.8 0.6 pad_bitcast_fusion.ends_ref
  3.4 0.7 fusion.7
  4.1 0.8 multiply_add_fusion
  4.9 0.7 select_reduce_fusion
  5.5 0.7 convert_element_type.9
  6.2 0.6 fusion.6.meta_ref
  6.8 1.3 reshape.43.gain_ref
  8.1 1.7 fusion.5.w_ref
  9.8 70.0 %gather_start.1 = (bf16[4096,1024]{1,0:T(8,128)(2,1)}, bf16[2048,2304]{1,0:T(8,128)(2,1)}, f32[512,128]{1,0:T(8,128)}, bf16[512,1024]{1,0:T(8,128)(2,1)}) custom-call(bf16[128,1024]{1,0:T(8,128)(2,1)} %kv_ref.1, bf16[64,2304]{1,0:T(8,128)(2,1)} %fusion.5.w_ref, f32[16,128]{1,0:T(8,128)} %fusion.6.meta_ref), custom_call_target="tpu_custom_call" | custom-call | tf_op jit(solution)/shard_map/gather_start/pallas_call | solution.py:237
  79.9 9.8 %attend.1 = (f32[128,2048]{1,0:T(8,128)}, bf16[128,2048]{1,0:T(8,128)(2,1)}, f32[16,128]{1,0:T(8,128)}, bf16[8,16,1024]{2,1,0:T(8,128)(2,1)}) custom-call(s32[1,8]{1,0:T(1,128)} %bitcast.8, bf16[128,2048]{1,0:T(8,128)(2,1)} %q_ref.1, bf16[4096,1024]{1,0:T(8,128)(2,1)} %get-tuple-element.13.kv_ref, s32[1,128]{1,0:T(1,128)} %pad_bitcast_fusion.ends_ref, ...), custom_call_target="tpu_custom_call" | custom-call | tf_op jit(solution)/shard_map/attend/pallas_call | solution.py:386
  89.7 84.7 %gather_rows.1 = (bf16[4096,2048]{1,0:T(8,128)(2,1)}, bf16[512,2048]{1,0:T(8,128)(2,1)}) custom-call(bf16[128,2048]{1,0:T(8,128)(2,1)} %get-tuple-element.17.n_ref), custom_call_target="tpu_custom_call" | custom-call | tf_op jit(solution)/shard_map/gather_rows/pallas_call | solution.py:288
  174.4 12.8 %shared.1.sh = bf16[512,2048]{1,0:T(8,128)(2,1)} custom-call(bf16[512,2048]{1,0:T(8,128)(2,1)} %get-tuple-element.19.rows_ref, bf16[2048,2304]{1,0:T(8,128)(2,1)} %get-tuple-element.20.w_ref), custom_call_target="tpu_custom_call" | custom-call | tf_op jit(solution)/shard_map/shared/pallas_call | solution.py:431
  187.2 72.8 %expert.1.parts = bf16[4096,2048]{1,0:T(8,128)(2,1)} custom-call(f32[512,128]{1,0:T(8,128)} %get-tuple-element.16.meta_ref, bf16[4096,2048]{1,0:T(8,128)(2,1)} %get-tuple-element.18.n_all, bf16[1,2048,1408]{2,1,0:T(8,128)(2,1)} %wg_h.1, bf16[1,2048,1408]{2,1,0:T(8,128)(2,1)} %wu_h.1, bf16[1,1408,2048]{2,1,0:T(8,128)(2,1)} %wd_h.1), custom_call_target="tpu_custom_call" | custom-call | tf_op jit(solution)/shard_map/expert/pallas_call | solution.py:544
  260.0 55.3 %give_back.1 = bf16[128,2048]{1,0:T(8,128)(2,1)} custom-call(f32[128,2048]{1,0:T(8,128)} %get-tuple-element.15.hid_ref, bf16[4096,2048]{1,0:T(8,128)(2,1)} %expert.1.parts, bf16[512,2048]{1,0:T(8,128)(2,1)} %shared.1.sh), custom_call_target="tpu_custom_call" | custom-call | tf_op jit(solution)/shard_map/give_back/pallas_call | solution.py:650
  315.2 1.9 copy.18

commit v2 on v1

v2 whole, which is shorter than its diff:
```python
import functools

import jax
import jax.numpy as jnp
from jax import lax
from jax.experimental import pallas as pl
from jax.experimental.pallas import tpu as pltpu
from jax.sharding import PartitionSpec as P

D = 2048
QUERY_HEADS = 16
KEY_VALUE_HEADS = 4
HEAD_SIZE = 128
FF = 1408
TOPK = 6
PAGE = 16
CAP = 36
TOK = 128
SPAD = 768
MAXLEN = 3072
eps_norm = 1e-06
MESH = pl.DeviceIdType.MESH
CODES = (0, 1, -1, 2)
ANY = pl.BlockSpec(memory_space=pl.ANY)
VM = pl.BlockSpec(memory_space=pltpu.VMEM)
SM = pl.BlockSpec(memory_space=pltpu.SMEM)
F32 = jnp.float32
BF16 = jnp.bfloat16
VMEM_LIMIT = 62 * 1024 * 1024


class Place:
    def __init__(self):
        c = lax.axis_index("exp")
        self.c = c
        self.r = lax.axis_index("req")
        self.z = c // 8
        self.x = lax.rem(c // 2, 4)
        self.k = lax.rem(c, 2)
        self.partner = c + 1 - 2 * self.k

    def at(self, dx, dz):
        return lax.rem(self.z + dz + 4, 4) * 8 + lax.rem(self.x + dx + 4, 4) * 2 + self.k

    def step(self, dim, s):
        return self.at(s, 0) if dim == "x" else self.at(0, s)

    def up(self, s):
        return lax.rem(self.r + s + 4, 4)

    def barrier(self, along_y):
        sem = pltpu.get_barrier_semaphore()
        peers = [self.at(1, 0), self.at(-1, 0), self.at(0, 1), self.at(0, -1), self.partner]
        for p in peers:
            pl.semaphore_signal(sem, inc=1, device_id={"exp": p}, device_id_type=MESH)
        for s in along_y:
            pl.semaphore_signal(sem, inc=1, device_id={"req": self.up(s)}, device_id_type=MESH)
        pl.semaphore_wait(sem, len(peers) + len(along_y))


def route(q):
    first, second = ("x", "z") if q < 2 else ("z", "x")
    return first, second, (1 if q % 2 == 0 else -1)


def shift(q, a, b):
    first, _, t = route(q)
    u, v = CODES[a] * t, CODES[b] * t
    return (u, v) if first == "x" else (v, u)


def hop(code, t):
    return -t if code == 2 else t


def depth(a, b):
    return abs(CODES[a]) + abs(CODES[b])


def children(q, a, b):
    first, second, t = route(q)
    out = []
    if b == 0:
        if a == 0:
            out += [(first, t, 1, 0), (first, -t, 2, 0)]
        elif a == 1:
            out += [(first, t, 3, 0)]
        out += [(second, t, a, 1), (second, -t, a, 2)]
    elif b == 1:
        out += [(second, t, a, 3)]
    return out


class Gather:
    def __init__(self, place, own, every, rows, pieces, send_sem, recv_sem, pair_sem, by_row=False):
        self.by_row = by_row
        self.p, self.own, self.every, self.rows, self.pieces = place, own, every, rows, pieces
        self.rq = rows // pieces
        self.send_sem, self.recv_sem, self.pair_sem = send_sem, recv_sem, pair_sem

    def slot(self, src, q):
        return self.every.at[pl.ds(pl.multiple_of(src * self.rows + q * self.rq, self.rq), self.rq)]

    def block(self, src):
        return self.every.at[pl.ds(pl.multiple_of(src * self.rows, self.rows), self.rows)]

    def source(self, q, a, b):
        dx, dz = shift(q, a, b)
        return self.p.at(-dx, -dz)

    def recv_of(self, q, a, b):
        return self.recv_sem.at[q * 15 + a * 4 + b - 1]

    def pass_on(self, q, a, b):
        src = self.source(q, a, b)
        ref = self.own.at[pl.ds(q * self.rq, self.rq)] if a == 0 and b == 0 else self.slot(src, q)
        for dim, s, na, nb in children(q, a, b):
            pltpu.make_async_remote_copy(
                ref, self.slot(src, q), self.send_sem, self.recv_of(q, na, nb),
                device_id={"exp": self.p.step(dim, s)}, device_id_type=MESH,
            ).start()

    def pair_of(self, row):
        return self.pair_sem.at[row % 4] if self.by_row else self.pair_sem

    def to_pair(self, ref, dst, row):
        pltpu.make_async_remote_copy(
            ref, dst, self.send_sem, self.pair_of(row),
            device_id={"exp": self.p.partner}, device_id_type=MESH,
        ).start()

    def start(self):
        for q in range(self.pieces):
            self.pass_on(q, 0, 0)
        self.to_pair(self.own, self.block(self.p.c), 0)

    def events(self):
        out = []
        for q in range(self.pieces):
            for a in range(4):
                for b in range(4):
                    if a or b:
                        out.append((depth(a, b), b, a, q))
        return sorted(out)

    def take(self, ev):
        _, b, a, q = ev
        ref = self.slot(self.source(q, a, b), q)
        pltpu.make_async_remote_copy(
            ref, ref, self.send_sem, self.recv_of(q, a, b),
            device_id={"exp": self.p.partner}, device_id_type=MESH,
        ).wait_recv()
        self.pass_on(q, a, b)
        self.to_pair(ref, ref, -shift(q, a, b)[1])

    def wait_pair(self, row=0):
        ref = self.every.at[pl.ds(0, (4 if self.by_row else 16) * self.rows)]
        pltpu.make_async_remote_copy(
            ref, ref, self.send_sem, self.pair_of(row),
            device_id={"exp": self.p.partner}, device_id_type=MESH,
        ).wait_recv()

    def drain(self):
        ref = self.every.at[pl.ds(0, 31 * self.rows)]
        pltpu.make_async_copy(ref, ref, self.send_sem).wait()


class RingY:
    def __init__(self, place, own, every, rows, send_sem, recv_sem):
        self.p, self.own, self.every, self.rows = place, own, every, rows
        self.h = rows // 2
        self.send_sem, self.recv_sem = send_sem, recv_sem

    def slot(self, src, q):
        return self.every.at[pl.ds(pl.multiple_of(src * self.rows + q * self.h, self.h), self.h)]

    def send(self, ref, src, q, s, code):
        pltpu.make_async_remote_copy(
            ref, self.slot(src, q), self.send_sem, self.recv_sem.at[q * 3 + code - 1],
            device_id={"req": self.p.up(s)}, device_id_type=MESH,
        ).start()

    def start(self):
        for q, t in ((0, 1), (1, -1)):
            ref = self.own.at[pl.ds(q * self.h, self.h)]
            self.send(ref, self.p.r, q, t, 1)
            self.send(ref, self.p.r, q, -t, 2)

    def finish(self, codes=(1, 2, 3)):
        for code in codes:
            for q, t in ((0, 1), (1, -1)):
                src = self.p.up(-CODES[code] * t)
                ref = self.slot(src, q)
                pltpu.make_async_remote_copy(
                    ref, ref, self.send_sem, self.recv_sem.at[q * 3 + code - 1],
                    device_id={"req": self.p.up(1)}, device_id_type=MESH,
                ).wait_recv()
                if code == 1:
                    self.send(ref, src, q, t, 3)

    def drain(self):
        ref = self.every.at[pl.ds(0, 3 * self.rows)]
        pltpu.make_async_copy(ref, ref, self.send_sem).wait()


def attend_start(c, q_ref, ends_ref, qs, m_s, l_s, acc_s, lt_s, beg_s):
    for h in range(QUERY_HEADS):
        qs[pl.ds(h * TOK, TOK), :] = q_ref[:, h * HEAD_SIZE:(h + 1) * HEAD_SIZE]
    qpos = c * TOK + lax.broadcasted_iota(jnp.int32, (TOK, 128), 0)
    ends = jnp.broadcast_to(ends_ref[...], (TOK, 128))
    beg_s[...] = jnp.max(jnp.where(ends <= qpos, ends, 0).astype(F32), axis=1, keepdims=True)
    m_s[...] = jnp.full_like(m_s, -5e29)
    l_s[...] = jnp.zeros_like(l_s)
    acc_s[...] = jnp.zeros_like(acc_s)
    lt_s[...] = jnp.zeros_like(lt_s)


def attend_chunks(c, lo, hi, kv_ref, qs, m_s, l_s, acc_s, beg_s):
    rows = 4 * TOK

    def chunk(i, _):
        k0 = pl.multiple_of(i * 256, 256)
        kpos = k0 + lax.broadcasted_iota(jnp.int32, (TOK, 256), 1)
        qp = c * TOK + lax.broadcasted_iota(jnp.int32, (TOK, 256), 0)
        seen = (kpos >= beg_s[...].astype(jnp.int32)) & (kpos <= qp)
        bias = jnp.where(seen, 0.0, -1e30).astype(F32)
        bias = jnp.concatenate([bias] * 4, axis=0)
        for g in range(KEY_VALUE_HEADS):
            at = pl.ds(g * rows, rows)
            keys = kv_ref[pl.ds(k0, 256), g * HEAD_SIZE:(g + 1) * HEAD_SIZE]
            values = kv_ref[pl.ds(k0, 256), 512 + g * HEAD_SIZE:512 + (g + 1) * HEAD_SIZE]
            s = lax.dot_general(qs[at, :], keys, (((1,), (1,)), ((), ())), preferred_element_type=F32)
            s = s * HEAD_SIZE ** (-0.5) + bias
            old = m_s[at, :]
            new = jnp.maximum(old, jnp.max(s, axis=1, keepdims=True))
            e = jnp.exp(s - new)
            alpha = jnp.exp(old - new)
            m_s[at, :] = new
            l_s[at, :] = l_s[at, :] * alpha + jnp.sum(e, axis=1, keepdims=True)
            acc_s[at, :] = acc_s[at, :] * alpha + jnp.dot(e.astype(BF16), values, preferred_element_type=F32)
        return 0

    lax.fori_loop(lo, hi, chunk, 0)


def attend_end(res_ref, gain_ref, hid_ref, normed_ref, lt_ref, m_s, l_s, acc_s, lt_s):
    total = jnp.zeros((TOK, 1), F32)
    for h in range(QUERY_HEADS):
        at = pl.ds(h * TOK, TOK)
        cols = slice(h * HEAD_SIZE, (h + 1) * HEAD_SIZE)
        att = (acc_s[at, :] / l_s[at, :]).astype(BF16)
        lt_s[:, h:h + 1] = m_s[at, :] + jnp.log(l_s[at, :])
        hid = res_ref[:, cols].astype(F32) + att.astype(F32)
        hid_ref[:, cols] = hid
        total = total + jnp.sum(hid * hid, axis=1, keepdims=True)
    scale = lax.rsqrt(total * (1.0 / D) + eps_norm)
    for h in range(QUERY_HEADS):
        cols = slice(h * HEAD_SIZE, (h + 1) * HEAD_SIZE)
        normed_ref[:, cols] = (hid_ref[:, cols] * scale * gain_ref[:, cols].astype(F32)).astype(BF16)
    lt_ref[...] = jnp.transpose(lt_s[...])[:QUERY_HEADS, :]


def kernel_attend(kv_ref, w_ref, meta_ref, srow_ref, q_ref, ends_ref, res_ref, gain_ref,
                  w_all, hid_ref, normed_ref, lt_ref, cache_ref, tgt_ref, wt_ref,
                  kv_all, meta_all, pg_all, qs, m_s, l_s, acc_s, lt_s, beg_s,
                  kv_r, w_r, meta_r, pg_r, send, pair, local):
    p = Place()
    c = p.c
    p.barrier((1, -1))
    kv = Gather(p, kv_ref, kv_all, TOK, 4, send.at[0], kv_r, pair.at[0])
    w = Gather(p, w_ref, w_all, 64, 4, send.at[1], w_r, pair.at[1])
    meta = Gather(p, meta_ref, meta_all, 16, 1, send.at[2], meta_r, pair.at[2])
    pages = RingY(p, kv_ref, pg_all, TOK, send.at[3], pg_r)
    meta.start()
    kv.start()
    pages.start()
    own_w = pltpu.make_async_copy(w_ref, w.block(c), local)
    own_w.start()
    kv_all[pl.ds(pl.multiple_of(c * TOK, TOK), TOK), :] = kv_ref[...]
    meta_all[pl.ds(pl.multiple_of(c * 16, 16), 16), :] = meta_ref[...]
    pg_all[pl.ds(pl.multiple_of(p.r * TOK, TOK), TOK), :] = kv_ref[...]
    evs = kv.events()
    for ev in evs[:16]:
        kv.take(ev)
    for ev in meta.events():
        meta.take(ev)
    pages.finish((1,))
    attend_start(c, q_ref, ends_ref, qs, m_s, l_s, acc_s, lt_s, beg_s)
    for ev in evs[16:40]:
        kv.take(ev)
    meta.wait_pair()
    plan_rows(c.astype(F32), meta_all, tgt_ref, wt_ref)
    for ev in evs[40:56]:
        kv.take(ev)
    w.start()
    pages.finish((2, 3))
    hit = lax.broadcasted_iota(jnp.int32, (TOK, 512), 1).astype(F32) == srow_ref[...]
    hit = jnp.where(hit, 1.0, 0.0).astype(BF16)
    cache_ref[...] = jnp.dot(hit, pg_all[...], preferred_element_type=F32).astype(BF16)
    for ev in evs[56:]:
        kv.take(ev)
    kv.wait_pair()
    first = jnp.maximum(c * TOK - MAXLEN, 0) // 256
    stop = c // 2 + 1
    w_evs = w.events()
    cut = (0, 16, 40, 56, 60)
    for i in range(5):
        attend_chunks(c, jnp.minimum(first + 3 * i, stop), jnp.minimum(first + 3 * i + 3, stop),
                      kv_all, qs, m_s, l_s, acc_s, beg_s)
        if i < 4:
            for ev in w_evs[cut[i]:cut[i + 1]]:
                w.take(ev)
    attend_end(res_ref, gain_ref, hid_ref, normed_ref, lt_ref, m_s, l_s, acc_s, lt_s)
    w.wait_pair()
    for g in (kv, w, meta):
        g.drain()
    pages.drain()
    own_w.wait()


def call_attend(kv, wcat, meta, srow, q, ends, res, gain):
    n = QUERY_HEADS * TOK
    return pl.pallas_call(
        kernel_attend,
        out_shape=(
            jax.ShapeDtypeStruct((D, 3 * SPAD), BF16),
            jax.ShapeDtypeStruct((TOK, D), F32),
            jax.ShapeDtypeStruct((TOK, D), BF16),
            jax.ShapeDtypeStruct((QUERY_HEADS, TOK), F32),
            jax.ShapeDtypeStruct((TOK, 1024), BF16),
            jax.ShapeDtypeStruct((32, 128), F32),
            jax.ShapeDtypeStruct((32, 128), F32),
        ),
        in_specs=[VM] * 8,
        out_specs=(ANY,) + (VM,) * 6,
        scratch_shapes=[
            pltpu.VMEM((32 * TOK, 1024), BF16),
            pltpu.VMEM((512, 128), F32),
            pltpu.VMEM((512, 1024), BF16),
            pltpu.VMEM((n, HEAD_SIZE), BF16),
            pltpu.VMEM((n, 1), F32),
            pltpu.VMEM((n, 1), F32),
            pltpu.VMEM((n, HEAD_SIZE), F32),
            pltpu.VMEM((TOK, 128), F32),
            pltpu.VMEM((TOK, 1), F32),
            pltpu.SemaphoreType.DMA((60,)),
            pltpu.SemaphoreType.DMA((60,)),
            pltpu.SemaphoreType.DMA((15,)),
            pltpu.SemaphoreType.DMA((6,)),
            pltpu.SemaphoreType.DMA((4,)),
            pltpu.SemaphoreType.DMA((3,)),
            pltpu.SemaphoreType.DMA,
        ],
        compiler_params=pltpu.CompilerParams(collective_id=0, has_side_effects=True, vmem_limit_bytes=VMEM_LIMIT),
        name="attend",
    )(kv, wcat, meta, srow, q, ends, res, gain)


def silu_mul(g, u):
    return (g / (1.0 + jnp.exp(-g)) * u).astype(BF16)


def shared_up(rows_ref, w_ref, act_s):
    def up(j, _):
        col = pl.multiple_of(j * 256, 256)
        g = jnp.dot(rows_ref[...], w_ref[:, pl.ds(col, 256)], preferred_element_type=F32)
        u = jnp.dot(rows_ref[...], w_ref[:, pl.ds(SPAD + col, 256)], preferred_element_type=F32)
        act_s[:, pl.ds(col, 256)] = silu_mul(g, u)
        return 0

    lax.fori_loop(0, 3, up, 0)


def shared_down(w_ref, act_s, out_ref):
    def down(j, _):
        col = pl.multiple_of(j * 256, 256)
        o = lax.dot_general(act_s[...], w_ref[pl.ds(col, 256), 2 * SPAD:], (((1,), (1,)), ((), ())),
                            preferred_element_type=F32)
        out_ref[:, pl.ds(col, 256)] = o.astype(BF16)
        return 0

    lax.fori_loop(0, 8, down, 0)


def plan_rows(e, meta_ref, tgt_s, wt_s):
    tgt_s[...] = jnp.zeros_like(tgt_s)
    for s in range(32):
        ids = meta_ref[pl.ds(s * 16, 8), :]
        wts = meta_ref[pl.ds(s * 16 + 8, 8), :]
        hit = jnp.where(ids == e, 1.0, 0.0).astype(F32)
        tgt_s[s:s + 1, :] = jnp.sum(hit, axis=0, keepdims=True)
        wt_s[s:s + 1, :] = jnp.sum(hit * wts, axis=0, keepdims=True)
    sel = tgt_s[...]
    i0 = lax.broadcasted_iota(jnp.int32, (128, 128), 0)
    i1 = lax.broadcasted_iota(jnp.int32, (128, 128), 1)
    tri = jnp.where(i0 <= i1, 1.0, 0.0).astype(BF16)
    rank = jnp.dot(sel.astype(BF16), tri, preferred_element_type=F32)
    src = lax.rem(lax.broadcasted_iota(jnp.int32, (32, 128), 0), 4).astype(F32)
    tgt_s[...] = jnp.where(sel > 0.5, src * CAP + rank - 1.0, -1.0)


def pick(tgt_ref, s0):
    t4 = tgt_ref[pl.ds(s0, 4), :]
    trow = jnp.concatenate([t4[i:i + 1, :] for i in range(4)], axis=1)
    return lax.broadcasted_iota(jnp.int32, (4 * CAP, 512), 0).astype(F32) == trow


ROWS = (0, 1, -1, 2)


def kernel_moe(n_ref, tgt_ref, wt_ref, w_hbm, wg_h, wu_h, wd_h, y_out, sh_out,
               n_all, y_all, w_s, wg, wu, wd, x_s, act_s, y_s, sact, sho,
               n_r, y_r, send, pair, w_sem, out_sem):
    p = Place()
    p.barrier((1, -1))
    g = Gather(p, n_ref, n_all, TOK, 4, send.at[0], n_r, pair, by_row=True)
    y = RingY(p, n_ref, y_all, TOK, send.at[1], y_r)
    g.start()
    y.start()
    ws = [pltpu.make_async_copy(a, b, w_sem.at[i]) for i, (a, b) in enumerate(
        ((wg_h.at[0], wg), (wu_h.at[0], wu), (wd_h.at[0], wd), (w_hbm, w_s)))]
    for w in ws:
        w.start()
    n_all[pl.ds(pl.multiple_of(p.c * TOK, TOK), TOK), :] = n_ref[...]
    y_all[pl.ds(pl.multiple_of(p.r * TOK, TOK), TOK), :] = n_ref[...]
    evs = g.events()
    evs.sort(key=lambda ev: (ev[0], abs(shift(ev[3], ev[2], ev[1])[1])))
    state = {"at": 0}
    last = {}
    for i, ev in enumerate(evs):
        last[-shift(ev[3], ev[2], ev[1])[1] % 4] = i

    def tick(n):
        for ev in evs[state["at"]:state["at"] + n]:
            g.take(ev)
        state["at"] = min(len(evs), state["at"] + n)

    def chunk(i):
        row = ROWS[i]
        tick(max(0, last[row % 4] + 1 - state["at"]))
        g.wait_pair(row)
        base = lax.rem(p.z + row + 4, 4) * 8
        wcols = []
        for j in range(2):
            s0 = pl.multiple_of(base + j * 4, 4)
            hit = pick(tgt_ref, s0)
            w4 = wt_ref[pl.ds(s0, 4), :]
            wrow = jnp.concatenate([w4[k:k + 1, :] for k in range(4)], axis=1)
            wcols.append(jnp.sum(jnp.where(hit, wrow, 0.0), axis=1, keepdims=True))
            one = jnp.where(hit, 1.0, 0.0).astype(BF16)
            r0 = pl.multiple_of(s0 * TOK, 512)

            def fetch(n, _, j=j, one=one, r0=r0):
                col = pl.multiple_of(n * 512, 512)
                x_s[pl.ds(j * 144, 144), pl.ds(col, 512)] = jnp.dot(
                    one, n_all[pl.ds(r0, 512), pl.ds(col, 512)], preferred_element_type=F32).astype(BF16)
                return 0

            lax.fori_loop(0, 4, fetch, 0)
            tick(2)
        wcol = jnp.concatenate(wcols, axis=0)
        if i == 0:
            ws[0].wait()
            ws[1].wait()

        def up(col, n):
            gv = jnp.dot(x_s[...], wg[:, pl.ds(col, n)], preferred_element_type=F32)
            uv = jnp.dot(x_s[...], wu[:, pl.ds(col, n)], preferred_element_type=F32)
            act_s[:, pl.ds(col, n)] = silu_mul(gv, uv)

        def up_body(j, _):
            up(pl.multiple_of(j * 512, 512), 512)
            return 0

        lax.fori_loop(0, 2, up_body, 0)
        tick(4)
        up(1024, 384)
        tick(2)
        if i == 0:
            ws[2].wait()

        def down(j, _, i=i):
            col = pl.multiple_of(j * 512, 512)
            o = jnp.dot(act_s[...], wd[:, pl.ds(col, 512)], preferred_element_type=F32)
            y_s[pl.ds(i * 288, 288), pl.ds(col, 512)] = (o * wcol).astype(BF16)
            return 0

        lax.fori_loop(0, 4, down, 0)
        tick(3)
        out = pltpu.make_async_copy(y_s.at[pl.ds(i * 288, 288)], y_out.at[pl.ds(i * 288, 288)], out_sem.at[i])
        out.start()
        return out

    tick(16)
    y.finish((1,))
    outs = [chunk(0)]
    y.finish((2, 3))
    ws[3].wait()
    shared_up(y_all, w_s, sact)
    tick(6)
    shared_down(w_s, sact, sho)
    tick(3)
    outs.append(pltpu.make_async_copy(sho, sh_out, out_sem.at[4]))
    outs[-1].start()
    for i in range(1, 4):
        outs.append(chunk(i))
    g.drain()
    y.drain()
    for o in outs:
        o.wait()


def call_moe(normed, tgt, wt, w_all, wg, wu, wd):
    return pl.pallas_call(
        kernel_moe,
        out_shape=(
            jax.ShapeDtypeStruct((32 * CAP, D), BF16),
            jax.ShapeDtypeStruct((512, D), BF16),
        ),
        in_specs=[VM, VM, VM, ANY, ANY, ANY, ANY],
        out_specs=(ANY, ANY),
        scratch_shapes=[
            pltpu.VMEM((32 * TOK, D), BF16),
            pltpu.VMEM((512, D), BF16),
            pltpu.VMEM((D, 3 * SPAD), BF16),
            pltpu.VMEM((D, FF), BF16),
            pltpu.VMEM((D, FF), BF16),
            pltpu.VMEM((FF, D), BF16),
            pltpu.VMEM((8 * CAP, D), BF16),
            pltpu.VMEM((8 * CAP, FF), BF16),
            pltpu.VMEM((32 * CAP, D), BF16),
            pltpu.VMEM((512, SPAD), BF16),
            pltpu.VMEM((512, D), BF16),
            pltpu.SemaphoreType.DMA((60,)),
            pltpu.SemaphoreType.DMA((6,)),
            pltpu.SemaphoreType.DMA((2,)),
            pltpu.SemaphoreType.DMA((4,)),
            pltpu.SemaphoreType.DMA((4,)),
            pltpu.SemaphoreType.DMA((5,)),
        ],
        compiler_params=pltpu.CompilerParams(collective_id=1, has_side_effects=True, vmem_limit_bytes=VMEM_LIMIT),
        name="moe",
    )(normed, tgt, wt, w_all, wg, wu, wd)


def kernel_return(hid_ref, tgt_ref, y_ref, sh, out_ref, mine, pair, rbuf, shbuf, pair_sem, recv_sem,
                  sh_recv, send):
    p = Place()
    p.barrier((1, -1, 2))
    shares = []
    for i, s in enumerate((1, -1, 2)):
        shares.append(pltpu.make_async_remote_copy(
            sh.at[pl.ds(pl.multiple_of(p.up(s) * TOK, TOK), TOK)], shbuf.at[i], send.at[1], sh_recv.at[i],
            device_id={"req": p.up(s)}, device_id_type=MESH))
        shares[-1].start()
    sh_own = pltpu.make_async_copy(sh.at[pl.ds(pl.multiple_of(p.r * TOK, TOK), TOK)], shbuf.at[3], sh_recv.at[3])
    sh_own.start()

    def blk(dev):
        return mine.at[pl.ds(pl.multiple_of(dev * TOK, TOK), TOK)]

    pairs = {}

    def put(row):
        i = ROWS.index(row)
        base = lax.rem(p.z + row + 4, 4) * 8
        for j in range(2):
            s0 = pl.multiple_of(base + j * 4, 4)
            one = jnp.where(pick(tgt_ref, s0), 1.0, 0.0).astype(BF16)
            r0 = pl.multiple_of(s0 * TOK, 512)

            def body(n, _, j=j, one=one, r0=r0):
                col = pl.multiple_of(n * 1024, 1024)
                mine[pl.ds(r0, 512), pl.ds(col, 1024)] = lax.dot_general(
                    one, y_ref[pl.ds(i * 288 + j * 144, 144), pl.ds(col, 1024)], (((0,), (0,)), ((), ())),
                    preferred_element_type=F32).astype(BF16)
                return 0

            lax.fori_loop(0, 2, body, 0)
        for dx in (2, 1, -1, 0):
            j = (dx % 4) * 4 + row % 4
            dest = p.at(dx, row)
            pairs[dx % 4, row % 4] = pltpu.make_async_remote_copy(
                blk(dest + 1 - 2 * p.k), pair.at[j], send.at[0], pair_sem.at[j],
                device_id={"exp": p.partner}, device_id_type=MESH)
            pairs[dx % 4, row % 4].start()

    done = set()

    def node(q, a, b):
        dx, dz = shift(q, a, b)
        o = (-dx % 4, -dz % 4)
        j = o[0] * 4 + o[1]
        if o not in done:
            done.add(o)
            pairs[o].wait_recv()
        kids = []
        for _, _, na, nb in children(q, a, b):
            i = q * 15 + na * 4 + nb - 1
            kids.append(i)
            pltpu.make_async_remote_copy(
                rbuf.at[i], rbuf.at[i], send.at[2], recv_sem.at[i],
                device_id={"exp": p.partner}, device_id_type=MESH).wait_recv()
        dest = p.at(-dx, -dz)
        rows = pl.ds(q * 32, 32)
        drows = pl.ds(pl.multiple_of(dest * TOK + q * 32, 32), 32)
        root = a == 0 and b == 0

        def add(n, _):
            cols = pl.ds(pl.multiple_of(n * 512, 512), 512)
            v = mine[drows, cols].astype(F32) + pair[j, rows, cols].astype(F32)
            for i in kids:
                v = v + rbuf[i, :, cols].astype(F32)
            if root:
                t = shbuf[3, rows, cols].astype(F32)
                for i in range(3):
                    t = t + shbuf[i, rows, cols].astype(F32)
                out_ref[rows, cols] = (hid_ref[rows, cols] + v + t).astype(BF16)
            else:
                mine[drows, cols] = v.astype(BF16)
            return 0

        lax.fori_loop(0, 4, add, 0)
        if not root:
            first, second, t = route(q)
            dim, code = (second, b) if b else (first, a)
            i = q * 15 + a * 4 + b - 1
            pltpu.make_async_remote_copy(
                mine.at[drows], rbuf.at[i], send.at[2], recv_sem.at[i],
                device_id={"exp": p.step(dim, -hop(code, t))}, device_id_type=MESH).start()

    todo = [(-depth(a, b), -abs(shift(q, a, b)[1]), b, a, q) for q in range(4) for a in range(4) for b in range(4)]
    todo.sort()

    def nodes(test):
        for item in list(todo):
            if test(-item[0], -item[1]):
                node(item[4], item[3], item[2])
                todo.remove(item)

    put(2)
    put(1)
    nodes(lambda d, dz: dz == 2 and d > 2)
    put(-1)
    nodes(lambda d, dz: d > 2)
    put(0)
    nodes(lambda d, dz: d > 0)
    for s in shares:
        s.wait_recv()
    sh_own.wait()
    nodes(lambda d, dz: True)
    ref = pair
    pltpu.make_async_copy(ref, ref, send.at[0]).wait()
    ref = shbuf.at[pl.ds(0, 3)]
    pltpu.make_async_copy(ref, ref, send.at[1]).wait()
    pltpu.make_async_copy(rbuf, rbuf, send.at[2]).wait()


def call_return(hid, tgt, y, sh):
    return pl.pallas_call(
        kernel_return,
        out_shape=jax.ShapeDtypeStruct((TOK, D), BF16),
        in_specs=[VM, VM, VM, ANY],
        out_specs=VM,
        scratch_shapes=[
            pltpu.VMEM((32 * TOK, D), BF16),
            pltpu.VMEM((16, TOK, D), BF16),
            pltpu.VMEM((60, 32, D), BF16),
            pltpu.VMEM((4, TOK, D), BF16),
            pltpu.SemaphoreType.DMA((16,)),
            pltpu.SemaphoreType.DMA((60,)),
            pltpu.SemaphoreType.DMA((4,)),
            pltpu.SemaphoreType.DMA((3,)),
        ],
        compiler_params=pltpu.CompilerParams(collective_id=2, has_side_effects=True, vmem_limit_bytes=VMEM_LIMIT),
        name="give_back",
    )(hid, tgt, y, sh)


def on_device(queries, keys_then_values, residual, norm_gain, prompt_lengths, expert_ids, router_logits,
              w_gate, w_up, w_down, w_shared_gate, w_shared_up, w_shared_down, page_table):
    c = lax.axis_index("exp")
    r = lax.axis_index("req")
    pad = ((0, 0), (0, SPAD - 704))
    wcat = jnp.concatenate([jnp.pad(w, pad) for w in (w_shared_gate, w_shared_up, w_shared_down)], axis=1)
    weights = jax.nn.softmax(router_logits, axis=-1)
    two = ((0, 0), (0, 2))
    meta = jnp.concatenate([
        jnp.pad(expert_ids.astype(F32), two, constant_values=-1.0), jnp.pad(weights, two)], axis=1).T
    lengths = prompt_lengths[0]
    upto = jnp.arange(16)[:, None] >= jnp.arange(16)[None, :]
    ends = jnp.sum(jnp.where(upto, lengths[None, :], 0), axis=1)
    ends = jnp.pad(ends, (0, 112), constant_values=1 << 20).reshape(1, 128)
    cols = lax.dynamic_slice_in_dim(page_table, c * 8, 8, 1) - (r * 256 + c * 8)
    where_from = jnp.arange(32, dtype=jnp.int32).reshape(4, 8, 1)
    inv = jnp.sum(jnp.where(cols[:, :, None] == jnp.arange(8)[None, None, :], where_from, 0), axis=(0, 1))

    srow = (inv[:, None] * PAGE + jnp.arange(PAGE)[None, :]).astype(F32).reshape(TOK, 1)
    w_all, hid, normed, log_totals, cache, tgt, wt = call_attend(
        keys_then_values, wcat, meta, srow, queries, ends, residual, norm_gain.reshape(1, D))
    y, sh = call_moe(normed, tgt, wt, w_all, w_gate, w_up, w_down)
    out = call_return(hid, tgt, y, sh)
    return out, cache.reshape(8, PAGE, 1024), log_totals


def solution(mesh):
    tok = P(("req", "exp"), None)
    ex = P("exp", None, None)
    sh = P("exp", "req")
    return jax.shard_map(
        on_device,
        mesh=mesh,
        in_specs=(tok, tok, tok, P(), P("req", None), tok, tok, ex, ex, ex, sh, sh, sh, P()),
        out_specs=(tok, P(("req", "exp"), None, None), P(None, ("req", "exp"))),
        check_vma=False,
    )
```

time: 319 us -> 230 us (0.72)
  Pallas kernels: 305 us -> 215 us
    pallas_call x5 -> x2, Pallas kernels: 250 us -> 156 us  [the longest x1 81.9 us: call_moe(): pl.pallas_call(kernel_moe, out_shape=(jax.ShapeDtypeStruct((32 * CAP, D),...]
    pallas_call x1, Pallas kernels: 55.3 us -> 59 us  [call_return(): pl.pallas_call(kernel_return, out_shape=jax.ShapeDtypeStruct((TOK, D), BF...]
where the time goes in v2:
time: 230 us; the launch traced here: 228 us
  Pallas kernels  215 us (93%)
  other arithmetic  6.83 us (3%)
  local copies, waits for them, and re-layouts  5.78 us (3%)
    pallas_call x1, Pallas kernels, call_moe(): pl.pallas_call(kernel_moe, out_shape=(jax.ShapeDtypeStruct((32 * CAP, D),...  81.9 us
    pallas_call x1, Pallas kernels, call_attend(): pl.pallas_call(kernel_attend, out_shape=(jax.ShapeDtypeStruct((D, 3 * SPA...  74.2 us
    pallas_call x1, Pallas kernels, call_return(): pl.pallas_call(kernel_return, out_shape=jax.ShapeDtypeStruct((TOK, D), BF...  59 us

profile of v2, /device:TPU:8, one launch (start us, length us, event | category | flops | bytes accessed | tf_op | source)
XLA Modules:
  0.0 228.4 jit_solution(6749772317268851304)
XLA Ops:
  0.6 0.7 reduce_max.9
  1.3 0.7 fusion.8
  2.0 0.8 select_reduce_fusion.1
  2.8 0.6 pad_bitcast_fusion.ends_ref
  3.4 0.7 fusion.7
  4.1 0.8 multiply_add_fusion
  4.9 0.1 select_reduce_fusion
  5.0 0.1 add_convert_fusion
  5.0 0.7 convert_element_type.22
  5.7 0.6 fusion.6.meta_ref
  6.3 1.3 reshape.70.gain_ref
  7.6 0.7 convert_element_type.25.srow_ref
  8.3 1.7 fusion.5.w_ref
  10.1 74.2 %attend.1 = (bf16[2048,2304]{1,0:T(8,128)(2,1)}, f32[128,2048]{1,0:T(8,128)}, bf16[128,2048]{1,0:T(8,128)(2,1)}, f32[16,128]{1,0:T(8,128)}, bf16[128,1024]{1,0:T...) custom-call(bf16[128,1024]{1,0:T(8,128)(2,1)} %kv_ref.1, bf16[64,2304]{1,0:T(8,128)(2,1)} %fusion.5.w_ref, ...), custom_call_target="tpu_custom_call" | custom-call | tf_op jit(solution)/shard_map/attend/pallas_call | solution.py:323
  84.3 81.9 %moe.1 = (bf16[1152,2048]{1,0:T(8,128)(2,1)}, bf16[512,2048]{1,0:T(8,128)(2,1)}) custom-call(bf16[128,2048]{1,0:T(8,128)(2,1)} %get-tuple-element.14.n_ref, f32[32,128]{1,0:T(8,128)} %get-tuple-element.13.tgt_ref, f32[32,128]{1,0:T(8,128)} %get-tuple-element.15.wt_ref, bf16[2048,2304]{1,0:T(8,128)(2,1)} %get-tuple-element.16.w_hbm, ...), custom_call_target="tpu_custom_call" | custom-call | tf_op jit(solution)/shard_map/moe/pallas_call | solution.py:514
  166.2 0.0 copy-start
  166.2 0.0 copy-start.1
  166.2 59.0 %give_back.1 = bf16[128,2048]{1,0:T(8,128)(2,1)} custom-call(f32[128,2048]{1,0:T(8,128)} %get-tuple-element.12.hid_ref, f32[32,128]{1,0:T(8,128)} %get-tuple-element.13.tgt_ref, bf16[1152,2048]{1,0:T(8,128)(2,1)} %get-tuple-element.17.y_ref, bf16[512,2048]{1,0:T(8,128)(2,1)} %get-tuple-element.18.sh), custom_call_target="tpu_custom_call" | custom-call | tf_op jit(solution)/shard_map/give_back/pallas_call | solution.py:660
  225.2 1.9 copy.22
  227.1 0.0 copy-done
  227.1 0.7 copy.23
  227.8 0.0 copy-done.1
  227.8 0.6 copy.24
  (1 shorter events, 0.0 us)
Async XLA Ops:
  166.2 60.9 %copy-start = (bf16[128,1024]{1,0:T(8,128)(2,1)S(1)}, bf16[128,1024]{1,0:T(8,128)(2,1)}, u32[]{:S(2)}) copy-start(bf16[128,1024]{1,0:T(8,128)(2,1)} %get-tuple-element.19) | copy-start | bytes 786436
  166.2 61.6 %copy-start.1 = (f32[16,128]{1,0:T(8,128)S(1)}, f32[16,128]{1,0:T(8,128)}, u32[]{:S(2)}) copy-start(f32[16,128]{1,0:T(8,128)} %get-tuple-element.28) | copy-start | bytes 24580

commit v3 on v2

--- a/solution.py
+++ b/solution.py
@@ -91,9 +91,22 @@
     return out
 
 
+NEAR = (
+    ((0, 0), (1, 0), (3, 0), (0, 1), (0, 3)),
+    ((1, 1), (1, 3), (3, 1), (3, 3), (2, 0), (0, 2)),
+    ((2, 1), (2, 3), (1, 2), (3, 2), (2, 2)),
+)
+CHUNKS = (
+    ((0, 0), (1, 0), (3, 0), (0, 1)),
+    ((0, 3), (1, 1), (1, 3), (3, 1)),
+    ((3, 3), (2, 0), (0, 2), (2, 1)),
+    ((2, 3), (1, 2), (3, 2), (2, 2)),
+)
+
+
 class Gather:
-    def __init__(self, place, own, every, rows, pieces, send_sem, recv_sem, pair_sem, by_row=False):
-        self.by_row = by_row
+    def __init__(self, place, own, every, rows, pieces, send_sem, recv_sem, pair_sem, groups=None):
+        self.groups = groups or (tuple((i, j) for i in range(4) for j in range(4)),)
         self.p, self.own, self.every, self.rows, self.pieces = place, own, every, rows, pieces
         self.rq = rows // pieces
         self.send_sem, self.recv_sem, self.pair_sem = send_sem, recv_sem, pair_sem
@@ -120,12 +133,13 @@
                 device_id={"exp": self.p.step(dim, s)}, device_id_type=MESH,
             ).start()
 
-    def pair_of(self, row):
-        return self.pair_sem.at[row % 4] if self.by_row else self.pair_sem
-
-    def to_pair(self, ref, dst, row):
+    def group(self, q, a, b):
+        dx, dz = shift(q, a, b)
+        return [i for i, g in enumerate(self.groups) if (-dx % 4, -dz % 4) in g][0]
+
+    def to_pair(self, ref, dst, group):
         pltpu.make_async_remote_copy(
-            ref, dst, self.send_sem, self.pair_of(row),
+            ref, dst, self.send_sem, self.pair_sem.at[group],
             device_id={"exp": self.p.partner}, device_id_type=MESH,
         ).start()
 
@@ -140,23 +154,23 @@
             for a in range(4):
                 for b in range(4):
                     if a or b:
-                        out.append((depth(a, b), b, a, q))
+                        out.append((self.group(q, a, b), depth(a, b), b, a, q))
         return sorted(out)
 
     def take(self, ev):
-        _, b, a, q = ev
+        _, _, b, a, q = ev
         ref = self.slot(self.source(q, a, b), q)
         pltpu.make_async_remote_copy(
             ref, ref, self.send_sem, self.recv_of(q, a, b),
             device_id={"exp": self.p.partner}, device_id_type=MESH,
         ).wait_recv()
         self.pass_on(q, a, b)
-        self.to_pair(ref, ref, -shift(q, a, b)[1])
-
-    def wait_pair(self, row=0):
-        ref = self.every.at[pl.ds(0, (4 if self.by_row else 16) * self.rows)]
+        self.to_pair(ref, ref, self.group(q, a, b))
+
+    def wait_pair(self, group=0):
+        ref = self.every.at[pl.ds(0, len(self.groups[group]) * self.rows)]
         pltpu.make_async_remote_copy(
-            ref, ref, self.send_sem, self.pair_of(row),
+            ref, ref, self.send_sem, self.pair_sem.at[group],
             device_id={"exp": self.p.partner}, device_id_type=MESH,
         ).wait_recv()
 
@@ -203,44 +217,83 @@
         pltpu.make_async_copy(ref, ref, self.send_sem).wait()
 
 
-def attend_start(c, q_ref, ends_ref, qs, m_s, l_s, acc_s, lt_s, beg_s):
+def attend_start(c, q_ref, len_ref, qs, m_s, l_s, acc_s, lt_s, beg_s):
     for h in range(QUERY_HEADS):
         qs[pl.ds(h * TOK, TOK), :] = q_ref[:, h * HEAD_SIZE:(h + 1) * HEAD_SIZE]
-    qpos = c * TOK + lax.broadcasted_iota(jnp.int32, (TOK, 128), 0)
-    ends = jnp.broadcast_to(ends_ref[...], (TOK, 128))
-    beg_s[...] = jnp.max(jnp.where(ends <= qpos, ends, 0).astype(F32), axis=1, keepdims=True)
+    qpos = c * TOK + lax.broadcasted_iota(jnp.int32, (TOK, 1), 0)
+    begin = jnp.zeros((TOK, 1), jnp.int32)
+    end = len_ref[0, 0]
+    for j in range(16):
+        begin = jnp.where(qpos >= end, end, begin)
+        if j < 15:
+            end = end + len_ref[0, j + 1]
+    beg_s[...] = begin
     m_s[...] = jnp.full_like(m_s, -5e29)
     l_s[...] = jnp.zeros_like(l_s)
     acc_s[...] = jnp.zeros_like(acc_s)
     lt_s[...] = jnp.zeros_like(lt_s)
 
 
-def attend_chunks(c, lo, hi, kv_ref, qs, m_s, l_s, acc_s, beg_s):
+def near_offset(group, i):
+    odd = 1 + 2 * lax.rem(i, 2)
+    if group == 1:
+        h = i // 4
+        v = 1 + 2 * lax.rem(i // 2, 2)
+        return (1 - h) * v + h * 2 * (1 - lax.rem(i, 2)), (1 - h) * odd + h * 2 * lax.rem(i, 2)
+    h, k = i // 4, lax.rem(i // 2, 2)
+    if group == 0:
+        return (1 - h) * (1 - k) * odd, (1 - h) * k * odd
+    return (1 - h) * ((1 - k) * 2 + k * odd) + 2 * h, (1 - h) * ((1 - k) * odd + k * 2) + 2 * h
+
+
+def attend_chunks(p, group, kv_ref, qs, m_s, l_s, acc_s, beg_s):
     rows = 4 * TOK
+    c = p.c
+    first = jnp.maximum(c * TOK - MAXLEN, 0) // 256
+    last = c // 2
 
     def chunk(i, _):
-        k0 = pl.multiple_of(i * 256, 256)
-        kpos = k0 + lax.broadcasted_iota(jnp.int32, (TOK, 256), 1)
-        qp = c * TOK + lax.broadcasted_iota(jnp.int32, (TOK, 256), 0)
-        seen = (kpos >= beg_s[...].astype(jnp.int32)) & (kpos <= qp)
-        bias = jnp.where(seen, 0.0, -1e30).astype(F32)
-        bias = jnp.concatenate([bias] * 4, axis=0)
-        for g in range(KEY_VALUE_HEADS):
-            at = pl.ds(g * rows, rows)
-            keys = kv_ref[pl.ds(k0, 256), g * HEAD_SIZE:(g + 1) * HEAD_SIZE]
-            values = kv_ref[pl.ds(k0, 256), 512 + g * HEAD_SIZE:512 + (g + 1) * HEAD_SIZE]
-            s = lax.dot_general(qs[at, :], keys, (((1,), (1,)), ((), ())), preferred_element_type=F32)
-            s = s * HEAD_SIZE ** (-0.5) + bias
-            old = m_s[at, :]
-            new = jnp.maximum(old, jnp.max(s, axis=1, keepdims=True))
-            e = jnp.exp(s - new)
-            alpha = jnp.exp(old - new)
-            m_s[at, :] = new
-            l_s[at, :] = l_s[at, :] * alpha + jnp.sum(e, axis=1, keepdims=True)
-            acc_s[at, :] = acc_s[at, :] * alpha + jnp.dot(e.astype(BF16), values, preferred_element_type=F32)
+        dx, dz = near_offset(group, i)
+        chip = lax.rem(p.z + dz, 4) * 4 + lax.rem(p.x + dx, 4)
+
+        @pl.when((chip >= first) & (chip <= last))
+        def _():
+            k0 = pl.multiple_of(chip * 256, 256)
+            kpos = k0 + lax.broadcasted_iota(jnp.int32, (TOK, 256), 1)
+            qp = c * TOK + lax.broadcasted_iota(jnp.int32, (TOK, 256), 0)
+            seen = (kpos >= beg_s[...]) & (kpos <= qp)
+            bias = jnp.where(seen, 0.0, -1e30).astype(F32)
+            bias = jnp.concatenate([bias] * 4, axis=0)
+            for g in range(KEY_VALUE_HEADS):
+                at = pl.ds(g * rows, rows)
+                keys = kv_ref[pl.ds(k0, 256), g * HEAD_SIZE:(g + 1) * HEAD_SIZE]
+                values = kv_ref[pl.ds(k0, 256), 512 + g * HEAD_SIZE:512 + (g + 1) * HEAD_SIZE]
+                s = lax.dot_general(qs[at, :], keys, (((1,), (1,)), ((), ())), preferred_element_type=F32)
+                s = s * HEAD_SIZE ** (-0.5) + bias
+                old = m_s[at, :]
+                new = jnp.maximum(old, jnp.max(s, axis=1, keepdims=True))
+                e = jnp.exp(s - new)
+                alpha = jnp.exp(old - new)
+                m_s[at, :] = new
+                l_s[at, :] = l_s[at, :] * alpha + jnp.sum(e, axis=1, keepdims=True)
+                acc_s[at, :] = acc_s[at, :] * alpha + jnp.dot(e.astype(BF16), values, preferred_element_type=F32)
+
         return 0
 
-    lax.fori_loop(lo, hi, chunk, 0)
+    lax.fori_loop(0, len(NEAR[group]), chunk, 0)
+
+
+def place_pages(p, table_ref, pg_all, cache_ref):
+    block = lax.broadcasted_iota(jnp.int32, (1, 512), 1) // PAGE
+    slot = jnp.full((1, 512), -1, jnp.int32)
+    for g in range(4):
+        for j in range(8):
+            slot = jnp.where(block == g * 8 + j, table_ref[g, p.c * 8 + j] - (p.r * 256 + p.c * 8), slot)
+    i0 = lax.broadcasted_iota(jnp.int32, (TOK, 512), 0)
+    i1 = lax.broadcasted_iota(jnp.int32, (TOK, 512), 1)
+    hit = (slot == i0 // PAGE) & (lax.rem(i0, PAGE) == lax.rem(i1, PAGE))
+    one = jnp.where(hit, 1.0, 0.0).astype(BF16)
+    cache_ref[...] = jnp.dot(one, pg_all[...], preferred_element_type=F32).astype(BF16)
 
 
 def attend_end(res_ref, gain_ref, hid_ref, normed_ref, lt_ref, m_s, l_s, acc_s, lt_s):
@@ -260,16 +313,16 @@
     lt_ref[...] = jnp.transpose(lt_s[...])[:QUERY_HEADS, :]
 
 
-def kernel_attend(kv_ref, w_ref, meta_ref, srow_ref, q_ref, ends_ref, res_ref, gain_ref,
+def kernel_attend(len_ref, table_ref, kv_ref, w_ref, meta_ref, q_ref, res_ref, gain_ref,
                   w_all, hid_ref, normed_ref, lt_ref, cache_ref, tgt_ref, wt_ref,
                   kv_all, meta_all, pg_all, qs, m_s, l_s, acc_s, lt_s, beg_s,
-                  kv_r, w_r, meta_r, pg_r, send, pair, local):
+                  kv_r, w_r, meta_r, pg_r, send, kv_pair, pair, local):
     p = Place()
     c = p.c
     p.barrier((1, -1))
-    kv = Gather(p, kv_ref, kv_all, TOK, 4, send.at[0], kv_r, pair.at[0])
-    w = Gather(p, w_ref, w_all, 64, 4, send.at[1], w_r, pair.at[1])
-    meta = Gather(p, meta_ref, meta_all, 16, 1, send.at[2], meta_r, pair.at[2])
+    kv = Gather(p, kv_ref, kv_all, TOK, 4, send.at[0], kv_r, kv_pair, NEAR)
+    w = Gather(p, w_ref, w_all, 64, 4, send.at[1], w_r, pair.at[pl.ds(0, 1)], None)
+    meta = Gather(p, meta_ref, meta_all, 16, 1, send.at[2], meta_r, pair.at[pl.ds(1, 1)], None)
     pages = RingY(p, kv_ref, pg_all, TOK, send.at[3], pg_r)
     meta.start()
     kv.start()
@@ -279,38 +332,34 @@
     kv_all[pl.ds(pl.multiple_of(c * TOK, TOK), TOK), :] = kv_ref[...]
     meta_all[pl.ds(pl.multiple_of(c * 16, 16), 16), :] = meta_ref[...]
     pg_all[pl.ds(pl.multiple_of(p.r * TOK, TOK), TOK), :] = kv_ref[...]
-    evs = kv.events()
-    for ev in evs[:16]:
-        kv.take(ev)
-    for ev in meta.events():
-        meta.take(ev)
+    def run(g, d):
+        for ev in sorted(g.events(), key=lambda ev: ev[1:]):
+            if ev[1] in d:
+                g.take(ev)
+
+    attention = (kv_all, qs, m_s, l_s, acc_s, beg_s)
+    attend_start(c, q_ref, len_ref, qs, m_s, l_s, acc_s, lt_s, beg_s)
+    run(kv, (1,))
+    w.start()
+    run(meta, (1, 2, 3, 4))
     pages.finish((1,))
-    attend_start(c, q_ref, ends_ref, qs, m_s, l_s, acc_s, lt_s, beg_s)
-    for ev in evs[16:40]:
-        kv.take(ev)
+    kv.wait_pair(0)
+    attend_chunks(p, 0, *attention)
+    run(kv, (2,))
+    run(w, (1,))
+    pages.finish((2, 3))
+    kv.wait_pair(1)
+    attend_chunks(p, 1, *attention)
+    run(kv, (3, 4))
+    run(w, (2,))
+    kv.wait_pair(2)
+    attend_chunks(p, 2, *attention)
+    run(w, (3,))
+    attend_end(res_ref, gain_ref, hid_ref, normed_ref, lt_ref, m_s, l_s, acc_s, lt_s)
+    run(w, (4,))
     meta.wait_pair()
     plan_rows(c.astype(F32), meta_all, tgt_ref, wt_ref)
-    for ev in evs[40:56]:
-        kv.take(ev)
-    w.start()
-    pages.finish((2, 3))
-    hit = lax.broadcasted_iota(jnp.int32, (TOK, 512), 1).astype(F32) == srow_ref[...]
-    hit = jnp.where(hit, 1.0, 0.0).astype(BF16)
-    cache_ref[...] = jnp.dot(hit, pg_all[...], preferred_element_type=F32).astype(BF16)
-    for ev in evs[56:]:
-        kv.take(ev)
-    kv.wait_pair()
-    first = jnp.maximum(c * TOK - MAXLEN, 0) // 256
-    stop = c // 2 + 1
-    w_evs = w.events()
-    cut = (0, 16, 40, 56, 60)
-    for i in range(5):
-        attend_chunks(c, jnp.minimum(first + 3 * i, stop), jnp.minimum(first + 3 * i + 3, stop),
-                      kv_all, qs, m_s, l_s, acc_s, beg_s)
-        if i < 4:
-            for ev in w_evs[cut[i]:cut[i + 1]]:
-                w.take(ev)
-    attend_end(res_ref, gain_ref, hid_ref, normed_ref, lt_ref, m_s, l_s, acc_s, lt_s)
+    place_pages(p, table_ref, pg_all, cache_ref)
     w.wait_pair()
     for g in (kv, w, meta):
         g.drain()
@@ -318,7 +367,7 @@
     own_w.wait()
 
 
-def call_attend(kv, wcat, meta, srow, q, ends, res, gain):
+def call_attend(lengths, table, kv, wcat, meta, q, res, gain):
     n = QUERY_HEADS * TOK
     return pl.pallas_call(
         kernel_attend,
@@ -331,7 +380,7 @@
             jax.ShapeDtypeStruct((32, 128), F32),
             jax.ShapeDtypeStruct((32, 128), F32),
         ),
-        in_specs=[VM] * 8,
+        in_specs=[SM, SM] + [VM] * 6,
         out_specs=(ANY,) + (VM,) * 6,
         scratch_shapes=[
             pltpu.VMEM((32 * TOK, 1024), BF16),
@@ -342,18 +391,19 @@
             pltpu.VMEM((n, 1), F32),
             pltpu.VMEM((n, HEAD_SIZE), F32),
             pltpu.VMEM((TOK, 128), F32),
-            pltpu.VMEM((TOK, 1), F32),
+            pltpu.VMEM((TOK, 1), jnp.int32),
             pltpu.SemaphoreType.DMA((60,)),
             pltpu.SemaphoreType.DMA((60,)),
             pltpu.SemaphoreType.DMA((15,)),
             pltpu.SemaphoreType.DMA((6,)),
             pltpu.SemaphoreType.DMA((4,)),
             pltpu.SemaphoreType.DMA((3,)),
+            pltpu.SemaphoreType.DMA((2,)),
             pltpu.SemaphoreType.DMA,
         ],
         compiler_params=pltpu.CompilerParams(collective_id=0, has_side_effects=True, vmem_limit_bytes=VMEM_LIMIT),
         name="attend",
-    )(kv, wcat, meta, srow, q, ends, res, gain)
+    )(lengths, table, kv, wcat, meta, q, res, gain)
 
 
 def silu_mul(g, u):
@@ -386,7 +436,9 @@
     tgt_s[...] = jnp.zeros_like(tgt_s)
     for s in range(32):
         ids = meta_ref[pl.ds(s * 16, 8), :]
-        wts = meta_ref[pl.ds(s * 16 + 8, 8), :]
+        logits = meta_ref[pl.ds(s * 16 + 8, 8), :]
+        wts = jnp.exp(logits - jnp.max(logits, axis=0, keepdims=True))
+        wts = wts / jnp.sum(wts, axis=0, keepdims=True)
         hit = jnp.where(ids == e, 1.0, 0.0).astype(F32)
         tgt_s[s:s + 1, :] = jnp.sum(hit, axis=0, keepdims=True)
         wt_s[s:s + 1, :] = jnp.sum(hit * wts, axis=0, keepdims=True)
@@ -395,17 +447,18 @@
     i1 = lax.broadcasted_iota(jnp.int32, (128, 128), 1)
     tri = jnp.where(i0 <= i1, 1.0, 0.0).astype(BF16)
     rank = jnp.dot(sel.astype(BF16), tri, preferred_element_type=F32)
-    src = lax.rem(lax.broadcasted_iota(jnp.int32, (32, 128), 0), 4).astype(F32)
-    tgt_s[...] = jnp.where(sel > 0.5, src * CAP + rank - 1.0, -1.0)
-
-
-def pick(tgt_ref, s0):
-    t4 = tgt_ref[pl.ds(s0, 4), :]
-    trow = jnp.concatenate([t4[i:i + 1, :] for i in range(4)], axis=1)
+    core = lax.rem(lax.broadcasted_iota(jnp.int32, (32, 128), 0), 2).astype(F32)
+    tgt_s[...] = jnp.where(sel > 0.5, core * CAP + rank - 1.0, -1000.0)
+
+
+def pick(tgt_ref, d0, d1):
+    t0, t1 = tgt_ref[pl.ds(d0, 2), :], tgt_ref[pl.ds(d1, 2), :] + 2.0 * CAP
+    trow = jnp.concatenate([t0[0:1, :], t0[1:2, :], t1[0:1, :], t1[1:2, :]], axis=1)
     return lax.broadcasted_iota(jnp.int32, (4 * CAP, 512), 0).astype(F32) == trow
 
 
-ROWS = (0, 1, -1, 2)
+def chip_of(p, o):
+    return pl.multiple_of(p.at(o[0], o[1]) - p.k, 2)
 
 
 def kernel_moe(n_ref, tgt_ref, wt_ref, w_hbm, wg_h, wu_h, wd_h, y_out, sh_out,
@@ -413,7 +466,7 @@
                n_r, y_r, send, pair, w_sem, out_sem):
     p = Place()
     p.barrier((1, -1))
-    g = Gather(p, n_ref, n_all, TOK, 4, send.at[0], n_r, pair, by_row=True)
+    g = Gather(p, n_ref, n_all, TOK, 4, send.at[0], n_r, pair, CHUNKS)
     y = RingY(p, n_ref, y_all, TOK, send.at[1], y_r)
     g.start()
     y.start()
@@ -424,11 +477,8 @@
     n_all[pl.ds(pl.multiple_of(p.c * TOK, TOK), TOK), :] = n_ref[...]
     y_all[pl.ds(pl.multiple_of(p.r * TOK, TOK), TOK), :] = n_ref[...]
     evs = g.events()
-    evs.sort(key=lambda ev: (ev[0], abs(shift(ev[3], ev[2], ev[1])[1])))
     state = {"at": 0}
-    last = {}
-    for i, ev in enumerate(evs):
-        last[-shift(ev[3], ev[2], ev[1])[1] % 4] = i
+    last = {ev[0]: i for i, ev in enumerate(evs)}
 
     def tick(n):
         for ev in evs[state["at"]:state["at"] + n]:
@@ -436,24 +486,23 @@
         state["at"] = min(len(evs), state["at"] + n)
 
     def chunk(i):
-        row = ROWS[i]
-        tick(max(0, last[row % 4] + 1 - state["at"]))
-        g.wait_pair(row)
-        base = lax.rem(p.z + row + 4, 4) * 8
+        tick(max(0, last[i] + 1 - state["at"]))
+        g.wait_pair(i)
         wcols = []
         for j in range(2):
-            s0 = pl.multiple_of(base + j * 4, 4)
-            hit = pick(tgt_ref, s0)
-            w4 = wt_ref[pl.ds(s0, 4), :]
-            wrow = jnp.concatenate([w4[k:k + 1, :] for k in range(4)], axis=1)
+            d0, d1 = chip_of(p, CHUNKS[i][2 * j]), chip_of(p, CHUNKS[i][2 * j + 1])
+            hit = pick(tgt_ref, d0, d1)
+            w0, w1 = wt_ref[pl.ds(d0, 2), :], wt_ref[pl.ds(d1, 2), :]
+            wrow = jnp.concatenate([w0[0:1, :], w0[1:2, :], w1[0:1, :], w1[1:2, :]], axis=1)
             wcols.append(jnp.sum(jnp.where(hit, wrow, 0.0), axis=1, keepdims=True))
             one = jnp.where(hit, 1.0, 0.0).astype(BF16)
-            r0 = pl.multiple_of(s0 * TOK, 512)
-
-            def fetch(n, _, j=j, one=one, r0=r0):
+            r0, r1 = pl.multiple_of(d0 * TOK, 256), pl.multiple_of(d1 * TOK, 256)
+
+            def fetch(n, _, j=j, one=one, r0=r0, r1=r1):
                 col = pl.multiple_of(n * 512, 512)
-                x_s[pl.ds(j * 144, 144), pl.ds(col, 512)] = jnp.dot(
-                    one, n_all[pl.ds(r0, 512), pl.ds(col, 512)], preferred_element_type=F32).astype(BF16)
+                v = jnp.dot(one[:, :256], n_all[pl.ds(r0, 256), pl.ds(col, 512)], preferred_element_type=F32)
+                v = v + jnp.dot(one[:, 256:], n_all[pl.ds(r1, 256), pl.ds(col, 512)], preferred_element_type=F32)
+                x_s[pl.ds(j * 144, 144), pl.ds(col, 512)] = v.astype(BF16)
                 return 0
 
             lax.fori_loop(0, 4, fetch, 0)
@@ -491,8 +540,9 @@
         out.start()
         return out
 
-    tick(16)
+    tick(last[0] + 1)
     y.finish((1,))
+    tick(4)
     outs = [chunk(0)]
     y.finish((2, 3))
     ws[3].wait()
@@ -543,9 +593,13 @@
     )(normed, tgt, wt, w_all, wg, wu, wd)
 
 
-def kernel_return(hid_ref, tgt_ref, y_ref, sh, out_ref, mine, pair, rbuf, shbuf, pair_sem, recv_sem,
-                  sh_recv, send):
+def kernel_return(hid_ref, tgt_ref, y_hbm, sh, out_ref, y_ref, mine, pair, rbuf, shbuf, pair_sem, recv_sem,
+                  sh_recv, send, y_sem):
     p = Place()
+    loads = [pltpu.make_async_copy(y_hbm.at[pl.ds(i * 288, 288)], y_ref.at[pl.ds(i * 288, 288)], y_sem.at[i])
+             for i in range(4)]
+    for i in (3, 2, 1, 0):
+        loads[i].start()
     p.barrier((1, -1, 2))
     shares = []
     for i, s in enumerate((1, -1, 2)):
@@ -561,29 +615,30 @@
 
     pairs = {}
 
-    def put(row):
-        i = ROWS.index(row)
-        base = lax.rem(p.z + row + 4, 4) * 8
-        for j in range(2):
-            s0 = pl.multiple_of(base + j * 4, 4)
-            one = jnp.where(pick(tgt_ref, s0), 1.0, 0.0).astype(BF16)
-            r0 = pl.multiple_of(s0 * TOK, 512)
-
-            def body(n, _, j=j, one=one, r0=r0):
+    def put(i):
+        loads[i].wait()
+        for j in (1, 0):
+            offs = CHUNKS[i][2 * j:2 * j + 2]
+            d0, d1 = chip_of(p, offs[0]), chip_of(p, offs[1])
+            one = jnp.where(pick(tgt_ref, d0, d1), 1.0, 0.0).astype(BF16)
+            r0, r1 = pl.multiple_of(d0 * TOK, 256), pl.multiple_of(d1 * TOK, 256)
+
+            def body(n, _, j=j, one=one, r0=r0, r1=r1):
                 col = pl.multiple_of(n * 1024, 1024)
-                mine[pl.ds(r0, 512), pl.ds(col, 1024)] = lax.dot_general(
+                v = lax.dot_general(
                     one, y_ref[pl.ds(i * 288 + j * 144, 144), pl.ds(col, 1024)], (((0,), (0,)), ((), ())),
                     preferred_element_type=F32).astype(BF16)
+                mine[pl.ds(r0, 256), pl.ds(col, 1024)] = v[:256]
+                mine[pl.ds(r1, 256), pl.ds(col, 1024)] = v[256:]
                 return 0
 
             lax.fori_loop(0, 2, body, 0)
-        for dx in (2, 1, -1, 0):
-            j = (dx % 4) * 4 + row % 4
-            dest = p.at(dx, row)
-            pairs[dx % 4, row % 4] = pltpu.make_async_remote_copy(
-                blk(dest + 1 - 2 * p.k), pair.at[j], send.at[0], pair_sem.at[j],
-                device_id={"exp": p.partner}, device_id_type=MESH)
-            pairs[dx % 4, row % 4].start()
+            for o in offs[::-1]:
+                k = o[0] * 4 + o[1]
+                pairs[o] = pltpu.make_async_remote_copy(
+                    blk(p.at(o[0], o[1]) + 1 - 2 * p.k), pair.at[k], send.at[0], pair_sem.at[k],
+                    device_id={"exp": p.partner}, device_id_type=MESH)
+                pairs[o].start()
 
     done = set()
 
@@ -629,26 +684,27 @@
                 mine.at[drows], rbuf.at[i], send.at[2], recv_sem.at[i],
                 device_id={"exp": p.step(dim, -hop(code, t))}, device_id_type=MESH).start()
 
-    todo = [(-depth(a, b), -abs(shift(q, a, b)[1]), b, a, q) for q in range(4) for a in range(4) for b in range(4)]
-    todo.sort()
-
-    def nodes(test):
-        for item in list(todo):
-            if test(-item[0], -item[1]):
-                node(item[4], item[3], item[2])
-                todo.remove(item)
-
+    todo = sorted((-depth(a, b), b, a, q) for q in range(4) for a in range(4) for b in range(4))
+
+    def nodes(i):
+        for _, b, a, q in todo:
+            dx, dz = shift(q, a, b)
+            if (-dx % 4, -dz % 4) in CHUNKS[i] and (a or b):
+                node(q, a, b)
+
+    put(3)
+    nodes(3)
     put(2)
+    nodes(2)
     put(1)
-    nodes(lambda d, dz: dz == 2 and d > 2)
-    put(-1)
-    nodes(lambda d, dz: d > 2)
+    nodes(1)
     put(0)
-    nodes(lambda d, dz: d > 0)
+    nodes(0)
     for s in shares:
         s.wait_recv()
     sh_own.wait()
-    nodes(lambda d, dz: True)
+    for q in range(4):
+        node(q, 0, 0)
     ref = pair
     pltpu.make_async_copy(ref, ref, send.at[0]).wait()
     ref = shbuf.at[pl.ds(0, 3)]
@@ -660,9 +716,10 @@
     return pl.pallas_call(
         kernel_return,
         out_shape=jax.ShapeDtypeStruct((TOK, D), BF16),
-        in_specs=[VM, VM, VM, ANY],
+        in_specs=[VM, VM, ANY, ANY],
         out_specs=VM,
         scratch_shapes=[
+            pltpu.VMEM((32 * CAP, D), BF16),
             pltpu.VMEM((32 * TOK, D), BF16),
             pltpu.VMEM((16, TOK, D), BF16),
             pltpu.VMEM((60, 32, D), BF16),
@@ -671,6 +728,7 @@
             pltpu.SemaphoreType.DMA((60,)),
             pltpu.SemaphoreType.DMA((4,)),
             pltpu.SemaphoreType.DMA((3,)),
+            pltpu.SemaphoreType.DMA((4,)),
         ],
         compiler_params=pltpu.CompilerParams(collective_id=2, has_side_effects=True, vmem_limit_bytes=VMEM_LIMIT),
         name="give_back",
@@ -679,25 +737,14 @@
 
 def on_device(queries, keys_then_values, residual, norm_gain, prompt_lengths, expert_ids, router_logits,
               w_gate, w_up, w_down, w_shared_gate, w_shared_up, w_shared_down, page_table):
-    c = lax.axis_index("exp")
-    r = lax.axis_index("req")
     pad = ((0, 0), (0, SPAD - 704))
     wcat = jnp.concatenate([jnp.pad(w, pad) for w in (w_shared_gate, w_shared_up, w_shared_down)], axis=1)
-    weights = jax.nn.softmax(router_logits, axis=-1)
     two = ((0, 0), (0, 2))
     meta = jnp.concatenate([
-        jnp.pad(expert_ids.astype(F32), two, constant_values=-1.0), jnp.pad(weights, two)], axis=1).T
-    lengths = prompt_lengths[0]
-    upto = jnp.arange(16)[:, None] >= jnp.arange(16)[None, :]
-    ends = jnp.sum(jnp.where(upto, lengths[None, :], 0), axis=1)
-    ends = jnp.pad(ends, (0, 112), constant_values=1 << 20).reshape(1, 128)
-    cols = lax.dynamic_slice_in_dim(page_table, c * 8, 8, 1) - (r * 256 + c * 8)
-    where_from = jnp.arange(32, dtype=jnp.int32).reshape(4, 8, 1)
-    inv = jnp.sum(jnp.where(cols[:, :, None] == jnp.arange(8)[None, None, :], where_from, 0), axis=(0, 1))
-
-    srow = (inv[:, None] * PAGE + jnp.arange(PAGE)[None, :]).astype(F32).reshape(TOK, 1)
+        jnp.pad(expert_ids.astype(F32), two, constant_values=-1.0),
+        jnp.pad(router_logits, two, constant_values=-1e30)], axis=1).T
     w_all, hid, normed, log_totals, cache, tgt, wt = call_attend(
-        keys_then_values, wcat, meta, srow, queries, ends, residual, norm_gain.reshape(1, D))
+        prompt_lengths, page_table, keys_then_values, wcat, meta, queries, residual, norm_gain.reshape(1, D))
     y, sh = call_moe(normed, tgt, wt, w_all, w_gate, w_up, w_down)
     out = call_return(hid, tgt, y, sh)
     return out, cache.reshape(8, PAGE, 1024), log_totals

time: 230 us -> 230 us (level)
  Pallas kernels: 215 us -> 219 us
  other arithmetic: 6.83 us -> 3.7 us
    pallas_call x1, Pallas kernels: 74.2 us -> 83.4 us  [call_attend(): pl.pallas_call(kernel_attend, out_shape=(jax.ShapeDtypeStruct((D, 3 * SPA...]
    pallas_call x1, Pallas kernels: 81.9 us -> 72.7 us  [call_moe(): pl.pallas_call(kernel_moe, out_shape=(jax.ShapeDtypeStruct((32 * CAP, D),...]
    pallas_call x1, Pallas kernels: 59 us -> 63.3 us  [call_return(): pl.pallas_call(kernel_return, out_shape=jax.ShapeDtypeStruct((TOK, D), BF...]
where the time goes in v3:
time: 230 us; the launch traced here: 228 us
  Pallas kernels  219 us (95%)
  local copies, waits for them, and re-layouts  4.48 us (2%)
  other arithmetic  3.7 us (2%)
    pallas_call x1, Pallas kernels, call_attend(): pl.pallas_call(kernel_attend, out_shape=(jax.ShapeDtypeStruct((D, 3 * SPA...  83.4 us
    pallas_call x1, Pallas kernels, call_moe(): pl.pallas_call(kernel_moe, out_shape=(jax.ShapeDtypeStruct((32 * CAP, D),...  72.7 us
    pallas_call x1, Pallas kernels, call_return(): pl.pallas_call(kernel_return, out_shape=jax.ShapeDtypeStruct((TOK, D), BF...  63.3 us

profile of v3, /device:TPU:8, one launch (start us, length us, event | category | flops | bytes accessed | tf_op | source)
XLA Modules:
  0.0 228.3 jit_solution(3653932738818041310)
XLA Ops:
  0.6 0.7 convert_element_type.7
  1.3 1.3 fusion.6.meta_ref
  2.6 1.3 reshape.12.gain_ref
  3.9 1.7 fusion.5.w_ref
  5.6 83.4 %attend.1 = (bf16[2048,2304]{1,0:T(8,128)(2,1)}, f32[128,2048]{1,0:T(8,128)}, bf16[128,2048]{1,0:T(8,128)(2,1)}, f32[16,128]{1,0:T(8,128)}, bf16[128,1024]{1,0:T...) custom-call(s32[1,16]{1,0:T(1,128)} %len_ref.1, s32[4,256]{1,0:T(4,128)} %table_ref.1, bf16[128,1024]{1,0:T(8,128)(2,1)} %kv_ref.1, ...), custom_call_target="tpu_custom_call" | custom-call | tf_op jit(solution)/shard_map/attend/pallas_call | solution.py:372
  89.1 72.7 %moe.1 = (bf16[1152,2048]{1,0:T(8,128)(2,1)}, bf16[512,2048]{1,0:T(8,128)(2,1)}) custom-call(bf16[128,2048]{1,0:T(8,128)(2,1)} %get-tuple-element.14.n_ref, f32[32,128]{1,0:T(8,128)} %get-tuple-element.13.tgt_ref, f32[32,128]{1,0:T(8,128)} %get-tuple-element.15.wt_ref, bf16[2048,2304]{1,0:T(8,128)(2,1)} %get-tuple-element.16.w_hbm, ...), custom_call_target="tpu_custom_call" | custom-call | tf_op jit(solution)/shard_map/moe/pallas_call | solution.py:564
  161.8 0.0 copy-start
  161.8 0.0 copy-start.1
  161.8 63.3 %give_back.1 = bf16[128,2048]{1,0:T(8,128)(2,1)} custom-call(f32[128,2048]{1,0:T(8,128)} %get-tuple-element.12.hid_ref, f32[32,128]{1,0:T(8,128)} %get-tuple-element.13.tgt_ref, bf16[1152,2048]{1,0:T(8,128)(2,1)} %get-tuple-element.17.y_hbm, bf16[512,2048]{1,0:T(8,128)(2,1)} %get-tuple-element.18.sh), custom_call_target="tpu_custom_call" | custom-call | tf_op jit(solution)/shard_map/give_back/pallas_call | solution.py:716
  225.2 1.9 copy.20
  227.0 0.0 copy-done
  227.0 0.7 copy.21
  227.7 0.0 copy-done.1
  227.7 0.6 copy.22
Async XLA Ops:
  161.8 65.2 %copy-start = (bf16[128,1024]{1,0:T(8,128)(2,1)S(1)}, bf16[128,1024]{1,0:T(8,128)(2,1)}, u32[]{:S(2)}) copy-start(bf16[128,1024]{1,0:T(8,128)(2,1)} %get-tuple-element.19) | copy-start | bytes 786436
  161.8 65.9 %copy-start.1 = (f32[16,128]{1,0:T(8,128)S(1)}, f32[16,128]{1,0:T(8,128)}, u32[]{:S(2)}) copy-start(f32[16,128]{1,0:T(8,128)} %get-tuple-element.26) | copy-start | bytes 24580

commit v4 on v3

--- a/solution.py
+++ b/solution.py
@@ -272,7 +272,7 @@
                 s = s * HEAD_SIZE ** (-0.5) + bias
                 old = m_s[at, :]
                 new = jnp.maximum(old, jnp.max(s, axis=1, keepdims=True))
-                e = jnp.exp(s - new)
+                e = jnp.exp(s - jnp.concatenate([new, new], axis=1))
                 alpha = jnp.exp(old - new)
                 m_s[at, :] = new
                 l_s[at, :] = l_s[at, :] * alpha + jnp.sum(e, axis=1, keepdims=True)
@@ -302,7 +302,8 @@
         at = pl.ds(h * TOK, TOK)
         cols = slice(h * HEAD_SIZE, (h + 1) * HEAD_SIZE)
         att = (acc_s[at, :] / l_s[at, :]).astype(BF16)
-        lt_s[:, h:h + 1] = m_s[at, :] + jnp.log(l_s[at, :])
+        lane = lax.broadcasted_iota(jnp.int32, (TOK, 128), 1)
+        lt_s[...] = jnp.where(lane == h, m_s[at, :] + jnp.log(l_s[at, :]), lt_s[...])
         hid = res_ref[:, cols].astype(F32) + att.astype(F32)
         hid_ref[:, cols] = hid
         total = total + jnp.sum(hid * hid, axis=1, keepdims=True)
@@ -315,20 +316,19 @@
 
 def kernel_attend(len_ref, table_ref, kv_ref, w_ref, meta_ref, q_ref, res_ref, gain_ref,
                   w_all, hid_ref, normed_ref, lt_ref, cache_ref, tgt_ref, wt_ref,
-                  kv_all, meta_all, pg_all, qs, m_s, l_s, acc_s, lt_s, beg_s,
+                  kv_all, w_s, meta_all, pg_all, qs, m_s, l_s, acc_s, lt_s, beg_s,
                   kv_r, w_r, meta_r, pg_r, send, kv_pair, pair, local):
     p = Place()
     c = p.c
     p.barrier((1, -1))
     kv = Gather(p, kv_ref, kv_all, TOK, 4, send.at[0], kv_r, kv_pair, NEAR)
-    w = Gather(p, w_ref, w_all, 64, 4, send.at[1], w_r, pair.at[pl.ds(0, 1)], None)
+    w = Gather(p, w_ref, w_s, 64, 4, send.at[1], w_r, pair.at[pl.ds(0, 1)], None)
     meta = Gather(p, meta_ref, meta_all, 16, 1, send.at[2], meta_r, pair.at[pl.ds(1, 1)], None)
     pages = RingY(p, kv_ref, pg_all, TOK, send.at[3], pg_r)
     meta.start()
     kv.start()
     pages.start()
-    own_w = pltpu.make_async_copy(w_ref, w.block(c), local)
-    own_w.start()
+    w_s[pl.ds(pl.multiple_of(c * 64, 64), 64), :] = w_ref[...]
     kv_all[pl.ds(pl.multiple_of(c * TOK, TOK), TOK), :] = kv_ref[...]
     meta_all[pl.ds(pl.multiple_of(c * 16, 16), 16), :] = meta_ref[...]
     pg_all[pl.ds(pl.multiple_of(p.r * TOK, TOK), TOK), :] = kv_ref[...]
@@ -340,31 +340,35 @@
     attention = (kv_all, qs, m_s, l_s, acc_s, beg_s)
     attend_start(c, q_ref, len_ref, qs, m_s, l_s, acc_s, lt_s, beg_s)
     run(kv, (1,))
+    run(meta, (1,))
+    pages.finish((1,))
+    run(meta, (2,))
+    run(kv, (2,))
     w.start()
-    run(meta, (1, 2, 3, 4))
-    pages.finish((1,))
     kv.wait_pair(0)
     attend_chunks(p, 0, *attention)
-    run(kv, (2,))
+    run(kv, (3, 4))
     run(w, (1,))
+    run(meta, (3, 4))
     pages.finish((2, 3))
     kv.wait_pair(1)
     attend_chunks(p, 1, *attention)
-    run(kv, (3, 4))
     run(w, (2,))
     kv.wait_pair(2)
     attend_chunks(p, 2, *attention)
     run(w, (3,))
     attend_end(res_ref, gain_ref, hid_ref, normed_ref, lt_ref, m_s, l_s, acc_s, lt_s)
     run(w, (4,))
+    w.wait_pair()
+    w_out = pltpu.make_async_copy(w_s, w_all, local)
+    w_out.start()
     meta.wait_pair()
     plan_rows(c.astype(F32), meta_all, tgt_ref, wt_ref)
     place_pages(p, table_ref, pg_all, cache_ref)
-    w.wait_pair()
     for g in (kv, w, meta):
         g.drain()
     pages.drain()
-    own_w.wait()
+    w_out.wait()
 
 
 def call_attend(lengths, table, kv, wcat, meta, q, res, gain):
@@ -384,11 +388,12 @@
         out_specs=(ANY,) + (VM,) * 6,
         scratch_shapes=[
             pltpu.VMEM((32 * TOK, 1024), BF16),
+            pltpu.VMEM((D, 3 * SPAD), BF16),
             pltpu.VMEM((512, 128), F32),
             pltpu.VMEM((512, 1024), BF16),
             pltpu.VMEM((n, HEAD_SIZE), BF16),
-            pltpu.VMEM((n, 1), F32),
-            pltpu.VMEM((n, 1), F32),
+            pltpu.VMEM((n, HEAD_SIZE), F32),
+            pltpu.VMEM((n, HEAD_SIZE), F32),
             pltpu.VMEM((n, HEAD_SIZE), F32),
             pltpu.VMEM((TOK, 128), F32),
             pltpu.VMEM((TOK, 1), jnp.int32),
@@ -693,12 +698,12 @@
                 node(q, a, b)
 
     put(3)
+    put(2)
     nodes(3)
-    put(2)
+    put(1)
     nodes(2)
-    put(1)
+    put(0)
     nodes(1)
-    put(0)
     nodes(0)
     for s in shares:
         s.wait_recv()

time: 230 us -> 215 us (0.935)
  Pallas kernels: 219 us -> 205 us
    pallas_call x1, Pallas kernels: 83.4 us -> 68.8 us  [call_attend(): pl.pallas_call(kernel_attend, out_shape=(jax.ShapeDtypeStruct((D, 3 * SPA...]
where the time goes in v4:
time: 215 us; the launch traced here: 213 us
  Pallas kernels  205 us (95%)
  local copies, waits for them, and re-layouts  4.48 us (2%)
  other arithmetic  3.7 us (2%)
    pallas_call x1, Pallas kernels, call_moe(): pl.pallas_call(kernel_moe, out_shape=(jax.ShapeDtypeStruct((32 * CAP, D),...  72.5 us
    pallas_call x1, Pallas kernels, call_attend(): pl.pallas_call(kernel_attend, out_shape=(jax.ShapeDtypeStruct((D, 3 * SPA...  68.8 us
    pallas_call x1, Pallas kernels, call_return(): pl.pallas_call(kernel_return, out_shape=jax.ShapeDtypeStruct((TOK, D), BF...  63.3 us

profile of v4, /device:TPU:8, one launch (start us, length us, event | category | flops | bytes accessed | tf_op | source)
XLA Modules:
  0.0 213.4 jit_solution(3715214253714944843)
XLA Ops:
  0.6 0.7 convert_element_type.7
  1.3 1.3 fusion.6.meta_ref
  2.6 1.3 reshape.12.gain_ref
  3.9 1.7 fusion.5.w_ref
  5.6 68.8 %attend.1 = (bf16[2048,2304]{1,0:T(8,128)(2,1)}, f32[128,2048]{1,0:T(8,128)}, bf16[128,2048]{1,0:T(8,128)(2,1)}, f32[16,128]{1,0:T(8,128)}, bf16[128,1024]{1,0:T...) custom-call(s32[1,16]{1,0:T(1,128)} %len_ref.1, s32[4,256]{1,0:T(4,128)} %table_ref.1, bf16[128,1024]{1,0:T(8,128)(2,1)} %kv_ref.1, ...), custom_call_target="tpu_custom_call" | custom-call | tf_op jit(solution)/shard_map/attend/pallas_call | solution.py:376
  74.4 72.5 %moe.1 = (bf16[1152,2048]{1,0:T(8,128)(2,1)}, bf16[512,2048]{1,0:T(8,128)(2,1)}) custom-call(bf16[128,2048]{1,0:T(8,128)(2,1)} %get-tuple-element.14.n_ref, f32[32,128]{1,0:T(8,128)} %get-tuple-element.13.tgt_ref, f32[32,128]{1,0:T(8,128)} %get-tuple-element.15.wt_ref, bf16[2048,2304]{1,0:T(8,128)(2,1)} %get-tuple-element.16.w_hbm, ...), custom_call_target="tpu_custom_call" | custom-call | tf_op jit(solution)/shard_map/moe/pallas_call | solution.py:569
  146.9 0.0 copy-start
  146.9 0.0 copy-start.1
  146.9 63.3 %give_back.1 = bf16[128,2048]{1,0:T(8,128)(2,1)} custom-call(f32[128,2048]{1,0:T(8,128)} %get-tuple-element.12.hid_ref, f32[32,128]{1,0:T(8,128)} %get-tuple-element.13.tgt_ref, bf16[1152,2048]{1,0:T(8,128)(2,1)} %get-tuple-element.17.y_hbm, bf16[512,2048]{1,0:T(8,128)(2,1)} %get-tuple-element.18.sh), custom_call_target="tpu_custom_call" | custom-call | tf_op jit(solution)/shard_map/give_back/pallas_call | solution.py:721
  210.2 1.9 copy.20
  212.1 0.0 copy-done
  212.1 0.7 copy.21
  212.8 0.0 copy-done.1
  212.8 0.6 copy.22
Async XLA Ops:
  146.9 65.2 %copy-start = (bf16[128,1024]{1,0:T(8,128)(2,1)S(1)}, bf16[128,1024]{1,0:T(8,128)(2,1)}, u32[]{:S(2)}) copy-start(bf16[128,1024]{1,0:T(8,128)(2,1)} %get-tuple-element.19) | copy-start | bytes 786436
  146.9 65.9 %copy-start.1 = (f32[16,128]{1,0:T(8,128)S(1)}, f32[16,128]{1,0:T(8,128)}, u32[]{:S(2)}) copy-start(f32[16,128]{1,0:T(8,128)} %get-tuple-element.26) | copy-start | bytes 24580

commit v5 on v4

--- a/solution.py
+++ b/solution.py
@@ -314,21 +314,19 @@
     lt_ref[...] = jnp.transpose(lt_s[...])[:QUERY_HEADS, :]
 
 
-def kernel_attend(len_ref, table_ref, kv_ref, w_ref, meta_ref, q_ref, res_ref, gain_ref,
-                  w_all, hid_ref, normed_ref, lt_ref, cache_ref, tgt_ref, wt_ref,
-                  kv_all, w_s, meta_all, pg_all, qs, m_s, l_s, acc_s, lt_s, beg_s,
-                  kv_r, w_r, meta_r, pg_r, send, kv_pair, pair, local):
+def kernel_attend(len_ref, table_ref, kv_ref, meta_ref, q_ref, res_ref, gain_ref,
+                  hid_ref, normed_ref, lt_ref, cache_ref, tgt_ref, wt_ref,
+                  kv_all, meta_all, pg_all, qs, m_s, l_s, acc_s, lt_s, beg_s,
+                  kv_r, meta_r, pg_r, send, kv_pair, pair):
     p = Place()
     c = p.c
     p.barrier((1, -1))
     kv = Gather(p, kv_ref, kv_all, TOK, 4, send.at[0], kv_r, kv_pair, NEAR)
-    w = Gather(p, w_ref, w_s, 64, 4, send.at[1], w_r, pair.at[pl.ds(0, 1)], None)
     meta = Gather(p, meta_ref, meta_all, 16, 1, send.at[2], meta_r, pair.at[pl.ds(1, 1)], None)
     pages = RingY(p, kv_ref, pg_all, TOK, send.at[3], pg_r)
     meta.start()
     kv.start()
     pages.start()
-    w_s[pl.ds(pl.multiple_of(c * 64, 64), 64), :] = w_ref[...]
     kv_all[pl.ds(pl.multiple_of(c * TOK, TOK), TOK), :] = kv_ref[...]
     meta_all[pl.ds(pl.multiple_of(c * 16, 16), 16), :] = meta_ref[...]
     pg_all[pl.ds(pl.multiple_of(p.r * TOK, TOK), TOK), :] = kv_ref[...]
@@ -344,39 +342,29 @@
     pages.finish((1,))
     run(meta, (2,))
     run(kv, (2,))
-    w.start()
     kv.wait_pair(0)
     attend_chunks(p, 0, *attention)
     run(kv, (3, 4))
-    run(w, (1,))
     run(meta, (3, 4))
     pages.finish((2, 3))
     kv.wait_pair(1)
     attend_chunks(p, 1, *attention)
-    run(w, (2,))
     kv.wait_pair(2)
     attend_chunks(p, 2, *attention)
-    run(w, (3,))
     attend_end(res_ref, gain_ref, hid_ref, normed_ref, lt_ref, m_s, l_s, acc_s, lt_s)
-    run(w, (4,))
-    w.wait_pair()
-    w_out = pltpu.make_async_copy(w_s, w_all, local)
-    w_out.start()
     meta.wait_pair()
     plan_rows(c.astype(F32), meta_all, tgt_ref, wt_ref)
     place_pages(p, table_ref, pg_all, cache_ref)
-    for g in (kv, w, meta):
+    for g in (kv, meta):
         g.drain()
     pages.drain()
-    w_out.wait()
-
-
-def call_attend(lengths, table, kv, wcat, meta, q, res, gain):
+
+
+def call_attend(lengths, table, kv, meta, q, res, gain):
     n = QUERY_HEADS * TOK
     return pl.pallas_call(
         kernel_attend,
         out_shape=(
-            jax.ShapeDtypeStruct((D, 3 * SPAD), BF16),
             jax.ShapeDtypeStruct((TOK, D), F32),
             jax.ShapeDtypeStruct((TOK, D), BF16),
             jax.ShapeDtypeStruct((QUERY_HEADS, TOK), F32),
@@ -384,11 +372,10 @@
             jax.ShapeDtypeStruct((32, 128), F32),
             jax.ShapeDtypeStruct((32, 128), F32),
         ),
-        in_specs=[SM, SM] + [VM] * 6,
-        out_specs=(ANY,) + (VM,) * 6,
+        in_specs=[SM, SM] + [VM] * 5,
+        out_specs=(VM,) * 6,
         scratch_shapes=[
             pltpu.VMEM((32 * TOK, 1024), BF16),
-            pltpu.VMEM((D, 3 * SPAD), BF16),
             pltpu.VMEM((512, 128), F32),
             pltpu.VMEM((512, 1024), BF16),
             pltpu.VMEM((n, HEAD_SIZE), BF16),
@@ -398,38 +385,32 @@
             pltpu.VMEM((TOK, 128), F32),
             pltpu.VMEM((TOK, 1), jnp.int32),
             pltpu.SemaphoreType.DMA((60,)),
-            pltpu.SemaphoreType.DMA((60,)),
             pltpu.SemaphoreType.DMA((15,)),
             pltpu.SemaphoreType.DMA((6,)),
             pltpu.SemaphoreType.DMA((4,)),
             pltpu.SemaphoreType.DMA((3,)),
             pltpu.SemaphoreType.DMA((2,)),
-            pltpu.SemaphoreType.DMA,
         ],
         compiler_params=pltpu.CompilerParams(collective_id=0, has_side_effects=True, vmem_limit_bytes=VMEM_LIMIT),
         name="attend",
-    )(lengths, table, kv, wcat, meta, q, res, gain)
+    )(lengths, table, kv, meta, q, res, gain)
 
 
 def silu_mul(g, u):
     return (g / (1.0 + jnp.exp(-g)) * u).astype(BF16)
 
 
-def shared_up(rows_ref, w_ref, act_s):
-    def up(j, _):
-        col = pl.multiple_of(j * 256, 256)
-        g = jnp.dot(rows_ref[...], w_ref[:, pl.ds(col, 256)], preferred_element_type=F32)
-        u = jnp.dot(rows_ref[...], w_ref[:, pl.ds(SPAD + col, 256)], preferred_element_type=F32)
-        act_s[:, pl.ds(col, 256)] = silu_mul(g, u)
-        return 0
-
-    lax.fori_loop(0, 3, up, 0)
+def shared_up(rows_ref, w_ref, act_s, j):
+    cols = slice(j * 256, (j + 1) * 256)
+    g = jnp.dot(rows_ref[...], w_ref[:, cols], preferred_element_type=F32)
+    u = jnp.dot(rows_ref[...], w_ref[:, SPAD + j * 256:SPAD + (j + 1) * 256], preferred_element_type=F32)
+    act_s[:, cols] = silu_mul(g, u)
 
 
 def shared_down(w_ref, act_s, out_ref):
     def down(j, _):
         col = pl.multiple_of(j * 256, 256)
-        o = lax.dot_general(act_s[...], w_ref[pl.ds(col, 256), 2 * SPAD:], (((1,), (1,)), ((), ())),
+        o = lax.dot_general(act_s[...], w_ref[pl.ds(col, 256), :], (((1,), (1,)), ((), ())),
                             preferred_element_type=F32)
         out_ref[:, pl.ds(col, 256)] = o.astype(BF16)
         return 0
@@ -466,9 +447,9 @@
     return pl.multiple_of(p.at(o[0], o[1]) - p.k, 2)
 
 
-def kernel_moe(n_ref, tgt_ref, wt_ref, w_hbm, wg_h, wu_h, wd_h, y_out, sh_out,
-               n_all, y_all, w_s, wg, wu, wd, x_s, act_s, y_s, sact, sho,
-               n_r, y_r, send, pair, w_sem, out_sem):
+def kernel_moe(n_ref, tgt_ref, wt_ref, w1_ref, w2_ref, wg_h, wu_h, wd_h, y_out, sh_out,
+               n_all, y_all, w1_s, w2_s, wg, wu, wd, x_s, act_s, y_s, sact, sho,
+               n_r, y_r, w1_r, w2_r, send, pair, w_pair, w_sem, out_sem):
     p = Place()
     p.barrier((1, -1))
     g = Gather(p, n_ref, n_all, TOK, 4, send.at[0], n_r, pair, CHUNKS)
@@ -476,19 +457,35 @@
     g.start()
     y.start()
     ws = [pltpu.make_async_copy(a, b, w_sem.at[i]) for i, (a, b) in enumerate(
-        ((wg_h.at[0], wg), (wu_h.at[0], wu), (wd_h.at[0], wd), (w_hbm, w_s)))]
+        ((wg_h.at[0], wg), (wu_h.at[0], wu), (wd_h.at[0], wd)))]
     for w in ws:
         w.start()
     n_all[pl.ds(pl.multiple_of(p.c * TOK, TOK), TOK), :] = n_ref[...]
     y_all[pl.ds(pl.multiple_of(p.r * TOK, TOK), TOK), :] = n_ref[...]
-    evs = g.events()
+    w1 = Gather(p, w1_ref, w1_s, 64, 4, send.at[2], w1_r, w_pair.at[pl.ds(0, 1)])
+    w2 = Gather(p, w2_ref, w2_s, 64, 4, send.at[3], w2_r, w_pair.at[pl.ds(1, 1)])
+    for w in (w1, w2):
+        w.every[pl.ds(pl.multiple_of(p.c * 64, 64), 64), :] = w.own[...]
+    queue = []
+    last = {}
+    for ev in g.events():
+        if ev[0] == 3 and 3 not in last:
+            queue.append(w1.start)
+        queue.append(functools.partial(g.take, ev))
+        last[ev[0]] = len(queue) - 1
+
+    def level(w, d):
+        return [functools.partial(w.take, ev) for ev in w.events() if ev[1] == d]
+
+    queue += level(w1, 1) + level(w1, 2) + [w2.start] + level(w1, 3) + level(w2, 1) + level(w1, 4)
+    first_part = len(queue)
+    queue += level(w2, 2) + level(w2, 3) + level(w2, 4)
     state = {"at": 0}
-    last = {ev[0]: i for i, ev in enumerate(evs)}
 
     def tick(n):
-        for ev in evs[state["at"]:state["at"] + n]:
-            g.take(ev)
-        state["at"] = min(len(evs), state["at"] + n)
+        for do in queue[state["at"]:state["at"] + n]:
+            do()
+        state["at"] = min(len(queue), state["at"] + n)
 
     def chunk(i):
         tick(max(0, last[i] + 1 - state["at"]))
@@ -548,36 +545,40 @@
     tick(last[0] + 1)
     y.finish((1,))
     tick(4)
-    outs = [chunk(0)]
+    outs = [chunk(0), chunk(1)]
     y.finish((2, 3))
-    ws[3].wait()
-    shared_up(y_all, w_s, sact)
-    tick(6)
-    shared_down(w_s, sact, sho)
-    tick(3)
+    outs += [chunk(2), chunk(3)]
+    tick(max(0, first_part - state["at"]))
+    w1.wait_pair()
+    for j in range(3):
+        shared_up(y_all, w1_s, sact, j)
+        tick((24, 16, 4)[j])
+    tick(len(queue))
+    w2.wait_pair()
+    shared_down(w2_s, sact, sho)
     outs.append(pltpu.make_async_copy(sho, sh_out, out_sem.at[4]))
     outs[-1].start()
-    for i in range(1, 4):
-        outs.append(chunk(i))
-    g.drain()
+    for w in (g, w1, w2):
+        w.drain()
     y.drain()
     for o in outs:
         o.wait()
 
 
-def call_moe(normed, tgt, wt, w_all, wg, wu, wd):
+def call_moe(normed, tgt, wt, w1, w2, wg, wu, wd):
     return pl.pallas_call(
         kernel_moe,
         out_shape=(
             jax.ShapeDtypeStruct((32 * CAP, D), BF16),
             jax.ShapeDtypeStruct((512, D), BF16),
         ),
-        in_specs=[VM, VM, VM, ANY, ANY, ANY, ANY],
+        in_specs=[VM, VM, VM, VM, VM, ANY, ANY, ANY],
         out_specs=(ANY, ANY),
         scratch_shapes=[
             pltpu.VMEM((32 * TOK, D), BF16),
             pltpu.VMEM((512, D), BF16),
-            pltpu.VMEM((D, 3 * SPAD), BF16),
+            pltpu.VMEM((D, 2 * SPAD), BF16),
+            pltpu.VMEM((D, SPAD), BF16),
             pltpu.VMEM((D, FF), BF16),
             pltpu.VMEM((D, FF), BF16),
             pltpu.VMEM((FF, D), BF16),
@@ -588,14 +589,17 @@
             pltpu.VMEM((512, D), BF16),
             pltpu.SemaphoreType.DMA((60,)),
             pltpu.SemaphoreType.DMA((6,)),
-            pltpu.SemaphoreType.DMA((2,)),
+            pltpu.SemaphoreType.DMA((60,)),
+            pltpu.SemaphoreType.DMA((60,)),
             pltpu.SemaphoreType.DMA((4,)),
             pltpu.SemaphoreType.DMA((4,)),
+            pltpu.SemaphoreType.DMA((2,)),
+            pltpu.SemaphoreType.DMA((3,)),
             pltpu.SemaphoreType.DMA((5,)),
         ],
         compiler_params=pltpu.CompilerParams(collective_id=1, has_side_effects=True, vmem_limit_bytes=VMEM_LIMIT),
         name="moe",
-    )(normed, tgt, wt, w_all, wg, wu, wd)
+    )(normed, tgt, wt, w1, w2, wg, wu, wd)
 
 
 def kernel_return(hid_ref, tgt_ref, y_hbm, sh, out_ref, y_ref, mine, pair, rbuf, shbuf, pair_sem, recv_sem,
@@ -743,14 +747,15 @@
 def on_device(queries, keys_then_values, residual, norm_gain, prompt_lengths, expert_ids, router_logits,
               w_gate, w_up, w_down, w_shared_gate, w_shared_up, w_shared_down, page_table):
     pad = ((0, 0), (0, SPAD - 704))
-    wcat = jnp.concatenate([jnp.pad(w, pad) for w in (w_shared_gate, w_shared_up, w_shared_down)], axis=1)
+    w1 = jnp.concatenate([jnp.pad(w, pad) for w in (w_shared_gate, w_shared_up)], axis=1)
+    w2 = jnp.pad(w_shared_down, pad)
     two = ((0, 0), (0, 2))
     meta = jnp.concatenate([
         jnp.pad(expert_ids.astype(F32), two, constant_values=-1.0),
         jnp.pad(router_logits, two, constant_values=-1e30)], axis=1).T
-    w_all, hid, normed, log_totals, cache, tgt, wt = call_attend(
-        prompt_lengths, page_table, keys_then_values, wcat, meta, queries, residual, norm_gain.reshape(1, D))
-    y, sh = call_moe(normed, tgt, wt, w_all, w_gate, w_up, w_down)
+    hid, normed, log_totals, cache, tgt, wt = call_attend(
+        prompt_lengths, page_table, keys_then_values, meta, queries, residual, norm_gain.reshape(1, D))
+    y, sh = call_moe(normed, tgt, wt, w1, w2, w_gate, w_up, w_down)
     out = call_return(hid, tgt, y, sh)
     return out, cache.reshape(8, PAGE, 1024), log_totals
 

time: 215 us -> 221 us (1.028)
  Pallas kernels: 205 us -> 209 us
    pallas_call x1, Pallas kernels: 72.5 us -> 107 us  [call_moe(): pl.pallas_call(kernel_moe, out_shape=(jax.ShapeDtypeStruct((32 * CAP, D),...]
    pallas_call x1, Pallas kernels: 68.8 us -> 39.5 us  [call_attend(): pl.pallas_call(kernel_attend, out_shape=(jax.ShapeDtypeStruct((TOK, D), F...]
where the time goes in v5:
time: 221 us; the launch traced here: 219 us
  Pallas kernels  209 us (95%)
  local copies, waits for them, and re-layouts  6.02 us (3%)
  other arithmetic  3.61 us (2%)
    pallas_call x1, Pallas kernels, call_moe(): pl.pallas_call(kernel_moe, out_shape=(jax.ShapeDtypeStruct((32 * CAP, D),...  107 us
    pallas_call x1, Pallas kernels, call_return(): pl.pallas_call(kernel_return, out_shape=jax.ShapeDtypeStruct((TOK, D), BF...  62.6 us
    pallas_call x1, Pallas kernels, call_attend(): pl.pallas_call(kernel_attend, out_shape=(jax.ShapeDtypeStruct((TOK, D), F...  39.5 us

profile of v5, /device:TPU:8, one launch (start us, length us, event | category | flops | bytes accessed | tf_op | source)
XLA Modules:
  0.0 219.4 jit_solution(2828616652156574226)
XLA Ops:
  0.6 0.7 convert_element_type.7
  1.3 1.3 fusion.3.meta_ref
  2.6 1.3 reshape.12.gain_ref
  3.9 1.5 pad.21.w2_ref
  5.4 1.6 fusion.2.w1_ref
  7.1 39.5 %attend.1 = (f32[128,2048]{1,0:T(8,128)}, bf16[128,2048]{1,0:T(8,128)(2,1)}, f32[16,128]{1,0:T(8,128)}, bf16[128,1024]{1,0:T(8,128)(2,1)}, f32[32,128]{1,0:T(8,128)}, /*index=5*/f32[32,128]{1,0:T(8,128)}) custom-call(s32[1,16]{1,0:T(1,128)} %len_ref.1, s32[4,256]{1,0:T(4,128)} %table_ref.1, bf16[128,1024]{1,0:T(8,128)(2,1)} %kv_ref.1, ...), custom_call_target="tpu_custom_call" | custom-call | tf_op jit(solution)/shard_map/attend/pallas_call | solution.py:365
  46.6 107.0 %moe.1 = (bf16[1152,2048]{1,0:T(8,128)(2,1)}, bf16[512,2048]{1,0:T(8,128)(2,1)}) custom-call(bf16[128,2048]{1,0:T(8,128)(2,1)} %get-tuple-element.13.n_ref, f32[32,128]{1,0:T(8,128)} %get-tuple-element.12.tgt_ref, f32[32,128]{1,0:T(8,128)} %get-tuple-element.14.wt_ref, bf16[64,1536]{1,0:T(8,128)(2,1)} %fusion.2.w1_ref, bf16[64,768]{1,0:T(8,128)(2,1)} %pad.21.w2_ref, ...), custom_call_target="tpu_custom_call" | custom-call | tf_op jit(solution)/shard_map/moe/pallas_call | solution.py:569
  153.6 0.0 copy-start
  153.6 0.0 copy-start.1
  153.6 62.6 %give_back.1 = bf16[128,2048]{1,0:T(8,128)(2,1)} custom-call(f32[128,2048]{1,0:T(8,128)} %get-tuple-element.11.hid_ref, f32[32,128]{1,0:T(8,128)} %get-tuple-element.12.tgt_ref, bf16[1152,2048]{1,0:T(8,128)(2,1)} %get-tuple-element.15.y_hbm, bf16[512,2048]{1,0:T(8,128)(2,1)} %get-tuple-element.16.sh), custom_call_target="tpu_custom_call" | custom-call | tf_op jit(solution)/shard_map/give_back/pallas_call | solution.py:725
  216.3 1.9 copy.20
  218.1 0.0 copy-done
  218.1 0.7 copy.21
  218.8 0.0 copy-done.1
  218.8 0.6 copy.22
Async XLA Ops:
  153.6 64.5 %copy-start = (bf16[128,1024]{1,0:T(8,128)(2,1)S(1)}, bf16[128,1024]{1,0:T(8,128)(2,1)}, u32[]{:S(2)}) copy-start(bf16[128,1024]{1,0:T(8,128)(2,1)} %get-tuple-element.17) | copy-start | bytes 786436
  153.6 65.2 %copy-start.1 = (f32[16,128]{1,0:T(8,128)S(1)}, f32[16,128]{1,0:T(8,128)}, u32[]{:S(2)}) copy-start(f32[16,128]{1,0:T(8,128)} %get-tuple-element.24) | copy-start | bytes 24580

commit v6 on v4

--- a/solution.py
+++ b/solution.py
@@ -96,12 +96,14 @@
     ((1, 1), (1, 3), (3, 1), (3, 3), (2, 0), (0, 2)),
     ((2, 1), (2, 3), (1, 2), (3, 2), (2, 2)),
 )
-CHUNKS = (
-    ((0, 0), (1, 0), (3, 0), (0, 1)),
-    ((0, 3), (1, 1), (1, 3), (3, 1)),
-    ((3, 3), (2, 0), (0, 2), (2, 1)),
-    ((2, 3), (1, 2), (3, 2), (2, 2)),
-)
+CHUNKS = (NEAR[0][:1], NEAR[0][1:], NEAR[1], NEAR[2])
+BASE = (0, 80, 368, 800)
+SPAN = (80, 288, 432, 368)
+Y_ROWS = 1168
+
+
+def parts_of(i):
+    return [CHUNKS[i][k:k + 2] for k in range(0, len(CHUNKS[i]), 2)]
 
 
 class Gather:
@@ -357,13 +359,13 @@
     kv.wait_pair(2)
     attend_chunks(p, 2, *attention)
     run(w, (3,))
-    attend_end(res_ref, gain_ref, hid_ref, normed_ref, lt_ref, m_s, l_s, acc_s, lt_s)
+    meta.wait_pair()
+    plan_rows(c.astype(F32), meta_all, tgt_ref, wt_ref)
     run(w, (4,))
     w.wait_pair()
     w_out = pltpu.make_async_copy(w_s, w_all, local)
     w_out.start()
-    meta.wait_pair()
-    plan_rows(c.astype(F32), meta_all, tgt_ref, wt_ref)
+    attend_end(res_ref, gain_ref, hid_ref, normed_ref, lt_ref, m_s, l_s, acc_s, lt_s)
     place_pages(p, table_ref, pg_all, cache_ref)
     for g in (kv, w, meta):
         g.drain()
@@ -456,10 +458,18 @@
     tgt_s[...] = jnp.where(sel > 0.5, core * CAP + rank - 1.0, -1000.0)
 
 
-def pick(tgt_ref, d0, d1):
-    t0, t1 = tgt_ref[pl.ds(d0, 2), :], tgt_ref[pl.ds(d1, 2), :] + 2.0 * CAP
-    trow = jnp.concatenate([t0[0:1, :], t0[1:2, :], t1[0:1, :], t1[1:2, :]], axis=1)
-    return lax.broadcasted_iota(jnp.int32, (4 * CAP, 512), 0).astype(F32) == trow
+def join_rows(ref, devs, step):
+    rows = []
+    for k, d in enumerate(devs):
+        t = ref[pl.ds(d, 2), :] + k * step
+        rows += [t[0:1, :], t[1:2, :]]
+    return jnp.concatenate(rows, axis=1)
+
+
+def pick(tgt_ref, devs):
+    n = len(devs)
+    trow = join_rows(tgt_ref, devs, 2.0 * CAP)
+    return lax.broadcasted_iota(jnp.int32, (2 * CAP * n, 256 * n), 0).astype(F32) == trow
 
 
 def chip_of(p, o):
@@ -490,65 +500,66 @@
             g.take(ev)
         state["at"] = min(len(evs), state["at"] + n)
 
-    def chunk(i):
-        tick(max(0, last[i] + 1 - state["at"]))
+    def chunk(i, ticks):
+        tick(max(0, last.get(i, -1) + 1 - state["at"]))
         g.wait_pair(i)
+        m = 2 * CAP * len(CHUNKS[i])
         wcols = []
-        for j in range(2):
-            d0, d1 = chip_of(p, CHUNKS[i][2 * j]), chip_of(p, CHUNKS[i][2 * j + 1])
-            hit = pick(tgt_ref, d0, d1)
-            w0, w1 = wt_ref[pl.ds(d0, 2), :], wt_ref[pl.ds(d1, 2), :]
-            wrow = jnp.concatenate([w0[0:1, :], w0[1:2, :], w1[0:1, :], w1[1:2, :]], axis=1)
-            wcols.append(jnp.sum(jnp.where(hit, wrow, 0.0), axis=1, keepdims=True))
+        for j, part in enumerate(parts_of(i)):
+            devs = [chip_of(p, o) for o in part]
+            hit = pick(tgt_ref, devs)
+            wcols.append(jnp.sum(jnp.where(hit, join_rows(wt_ref, devs, 0.0), 0.0), axis=1, keepdims=True))
             one = jnp.where(hit, 1.0, 0.0).astype(BF16)
-            r0, r1 = pl.multiple_of(d0 * TOK, 256), pl.multiple_of(d1 * TOK, 256)
-
-            def fetch(n, _, j=j, one=one, r0=r0, r1=r1):
+            starts = [pl.multiple_of(d * TOK, 256) for d in devs]
+
+            def fetch(n, _, j=j, one=one, starts=starts):
                 col = pl.multiple_of(n * 512, 512)
-                v = jnp.dot(one[:, :256], n_all[pl.ds(r0, 256), pl.ds(col, 512)], preferred_element_type=F32)
-                v = v + jnp.dot(one[:, 256:], n_all[pl.ds(r1, 256), pl.ds(col, 512)], preferred_element_type=F32)
-                x_s[pl.ds(j * 144, 144), pl.ds(col, 512)] = v.astype(BF16)
+                v = 0.0
+                for k, r in enumerate(starts):
+                    v = v + jnp.dot(one[:, k * 256:(k + 1) * 256], n_all[pl.ds(r, 256), pl.ds(col, 512)],
+                                    preferred_element_type=F32)
+                x_s[pl.ds(j * 144, 72 * len(starts)), pl.ds(col, 512)] = v.astype(BF16)
                 return 0
 
             lax.fori_loop(0, 4, fetch, 0)
-            tick(2)
-        wcol = jnp.concatenate(wcols, axis=0)
+            tick(ticks[0])
+        wcol = jnp.concatenate(wcols, axis=0) if len(wcols) > 1 else wcols[0]
         if i == 0:
             ws[0].wait()
             ws[1].wait()
 
         def up(col, n):
-            gv = jnp.dot(x_s[...], wg[:, pl.ds(col, n)], preferred_element_type=F32)
-            uv = jnp.dot(x_s[...], wu[:, pl.ds(col, n)], preferred_element_type=F32)
-            act_s[:, pl.ds(col, n)] = silu_mul(gv, uv)
+            gv = jnp.dot(x_s[:m, :], wg[:, pl.ds(col, n)], preferred_element_type=F32)
+            uv = jnp.dot(x_s[:m, :], wu[:, pl.ds(col, n)], preferred_element_type=F32)
+            act_s[:m, pl.ds(col, n)] = silu_mul(gv, uv)
 
         def up_body(j, _):
             up(pl.multiple_of(j * 512, 512), 512)
             return 0
 
         lax.fori_loop(0, 2, up_body, 0)
-        tick(4)
+        tick(ticks[1])
         up(1024, 384)
-        tick(2)
+        tick(ticks[2])
         if i == 0:
             ws[2].wait()
 
-        def down(j, _, i=i):
+        def down(j, _):
             col = pl.multiple_of(j * 512, 512)
-            o = jnp.dot(act_s[...], wd[:, pl.ds(col, 512)], preferred_element_type=F32)
-            y_s[pl.ds(i * 288, 288), pl.ds(col, 512)] = (o * wcol).astype(BF16)
+            o = jnp.dot(act_s[:m, :], wd[:, pl.ds(col, 512)], preferred_element_type=F32)
+            y_s[pl.ds(BASE[i], m), pl.ds(col, 512)] = (o * wcol).astype(BF16)
             return 0
 
         lax.fori_loop(0, 4, down, 0)
-        tick(3)
-        out = pltpu.make_async_copy(y_s.at[pl.ds(i * 288, 288)], y_out.at[pl.ds(i * 288, 288)], out_sem.at[i])
+        tick(ticks[3])
+        rows = pl.ds(BASE[i], SPAN[i])
+        out = pltpu.make_async_copy(y_s.at[rows], y_out.at[rows], out_sem.at[i])
         out.start()
         return out
 
-    tick(last[0] + 1)
+    outs = [chunk(0, (0, 0, 0, 4))]
     y.finish((1,))
-    tick(4)
-    outs = [chunk(0)]
+    outs.append(chunk(1, (2, 4, 2, 3)))
     y.finish((2, 3))
     ws[3].wait()
     shared_up(y_all, w_s, sact)
@@ -557,8 +568,8 @@
     tick(3)
     outs.append(pltpu.make_async_copy(sho, sh_out, out_sem.at[4]))
     outs[-1].start()
-    for i in range(1, 4):
-        outs.append(chunk(i))
+    outs.append(chunk(2, (2, 5, 3, 4)))
+    outs.append(chunk(3, (0, 0, 0, 0)))
     g.drain()
     y.drain()
     for o in outs:
@@ -569,7 +580,7 @@
     return pl.pallas_call(
         kernel_moe,
         out_shape=(
-            jax.ShapeDtypeStruct((32 * CAP, D), BF16),
+            jax.ShapeDtypeStruct((Y_ROWS, D), BF16),
             jax.ShapeDtypeStruct((512, D), BF16),
         ),
         in_specs=[VM, VM, VM, ANY, ANY, ANY, ANY],
@@ -581,9 +592,9 @@
             pltpu.VMEM((D, FF), BF16),
             pltpu.VMEM((D, FF), BF16),
             pltpu.VMEM((FF, D), BF16),
-            pltpu.VMEM((8 * CAP, D), BF16),
-            pltpu.VMEM((8 * CAP, FF), BF16),
-            pltpu.VMEM((32 * CAP, D), BF16),
+            pltpu.VMEM((12 * CAP, D), BF16),
+            pltpu.VMEM((12 * CAP, FF), BF16),
+            pltpu.VMEM((Y_ROWS, D), BF16),
             pltpu.VMEM((512, SPAD), BF16),
             pltpu.VMEM((512, D), BF16),
             pltpu.SemaphoreType.DMA((60,)),
@@ -601,8 +612,8 @@
 def kernel_return(hid_ref, tgt_ref, y_hbm, sh, out_ref, y_ref, mine, pair, rbuf, shbuf, pair_sem, recv_sem,
                   sh_recv, send, y_sem):
     p = Place()
-    loads = [pltpu.make_async_copy(y_hbm.at[pl.ds(i * 288, 288)], y_ref.at[pl.ds(i * 288, 288)], y_sem.at[i])
-             for i in range(4)]
+    loads = [pltpu.make_async_copy(y_hbm.at[pl.ds(b, n)], y_ref.at[pl.ds(b, n)], y_sem.at[i])
+             for i, (b, n) in enumerate(zip(BASE, SPAN))]
     for i in (3, 2, 1, 0):
         loads[i].start()
     p.barrier((1, -1, 2))
@@ -620,25 +631,24 @@
 
     pairs = {}
 
-    def put(i):
-        loads[i].wait()
-        for j in (1, 0):
-            offs = CHUNKS[i][2 * j:2 * j + 2]
-            d0, d1 = chip_of(p, offs[0]), chip_of(p, offs[1])
-            one = jnp.where(pick(tgt_ref, d0, d1), 1.0, 0.0).astype(BF16)
-            r0, r1 = pl.multiple_of(d0 * TOK, 256), pl.multiple_of(d1 * TOK, 256)
-
-            def body(n, _, j=j, one=one, r0=r0, r1=r1):
+    def put(i, which):
+        for j in which:
+            part = parts_of(i)[j]
+            devs = [chip_of(p, o) for o in part]
+            one = jnp.where(pick(tgt_ref, devs), 1.0, 0.0).astype(BF16)
+            starts = [pl.multiple_of(d * TOK, 256) for d in devs]
+
+            def body(n, _, j=j, one=one, starts=starts):
                 col = pl.multiple_of(n * 1024, 1024)
                 v = lax.dot_general(
-                    one, y_ref[pl.ds(i * 288 + j * 144, 144), pl.ds(col, 1024)], (((0,), (0,)), ((), ())),
-                    preferred_element_type=F32).astype(BF16)
-                mine[pl.ds(r0, 256), pl.ds(col, 1024)] = v[:256]
-                mine[pl.ds(r1, 256), pl.ds(col, 1024)] = v[256:]
+                    one, y_ref[pl.ds(BASE[i] + j * 144, 72 * len(starts)), pl.ds(col, 1024)],
+                    (((0,), (0,)), ((), ())), preferred_element_type=F32).astype(BF16)
+                for k, r in enumerate(starts):
+                    mine[pl.ds(r, 256), pl.ds(col, 1024)] = v[k * 256:(k + 1) * 256]
                 return 0
 
             lax.fori_loop(0, 2, body, 0)
-            for o in offs[::-1]:
+            for o in part:
                 k = o[0] * 4 + o[1]
                 pairs[o] = pltpu.make_async_remote_copy(
                     blk(p.at(o[0], o[1]) + 1 - 2 * p.k), pair.at[k], send.at[0], pair_sem.at[k],
@@ -691,20 +701,24 @@
 
     todo = sorted((-depth(a, b), b, a, q) for q in range(4) for a in range(4) for b in range(4))
 
-    def nodes(i):
-        for _, b, a, q in todo:
-            dx, dz = shift(q, a, b)
-            if (-dx % 4, -dz % 4) in CHUNKS[i] and (a or b):
+    def nodes(d):
+        for dist, b, a, q in todo:
+            if -dist == d:
                 node(q, a, b)
 
-    put(3)
-    put(2)
+    loads[3].wait()
+    put(3, (2, 1, 0))
+    nodes(4)
+    loads[2].wait()
+    put(2, (0,))
     nodes(3)
-    put(1)
+    put(2, (1, 2))
+    loads[1].wait()
+    put(1, (0, 1))
     nodes(2)
-    put(0)
+    loads[0].wait()
+    put(0, (0,))
     nodes(1)
-    nodes(0)
     for s in shares:
         s.wait_recv()
     sh_own.wait()
@@ -724,7 +738,7 @@
         in_specs=[VM, VM, ANY, ANY],
         out_specs=VM,
         scratch_shapes=[
-            pltpu.VMEM((32 * CAP, D), BF16),
+            pltpu.VMEM((Y_ROWS, D), BF16),
             pltpu.VMEM((32 * TOK, D), BF16),
             pltpu.VMEM((16, TOK, D), BF16),
             pltpu.VMEM((60, 32, D), BF16),

time: 215 us -> 207 us (0.963)
  Pallas kernels: 205 us -> 196 us
    pallas_call x1, Pallas kernels: 63.3 us -> 58.4 us  [call_return(): pl.pallas_call(kernel_return, out_shape=jax.ShapeDtypeStruct((TOK, D), BF...]
    pallas_call x1, Pallas kernels: 72.5 us -> 69.1 us  [call_moe(): pl.pallas_call(kernel_moe, out_shape=(jax.ShapeDtypeStruct((Y_ROWS, D), B...]
where the time goes in v6:
time: 207 us; the launch traced here: 205 us
  Pallas kernels  196 us (95%)
  local copies, waits for them, and re-layouts  4.48 us (2%)
  other arithmetic  3.7 us (2%)
    pallas_call x1, Pallas kernels, call_moe(): pl.pallas_call(kernel_moe, out_shape=(jax.ShapeDtypeStruct((Y_ROWS, D), B...  69.1 us
    pallas_call x1, Pallas kernels, call_attend(): pl.pallas_call(kernel_attend, out_shape=(jax.ShapeDtypeStruct((D, 3 * SPA...  68.9 us
    pallas_call x1, Pallas kernels, call_return(): pl.pallas_call(kernel_return, out_shape=jax.ShapeDtypeStruct((TOK, D), BF...  58.4 us

profile of v6, /device:TPU:8, one launch (start us, length us, event | category | flops | bytes accessed | tf_op | source)
XLA Modules:
  0.0 205.2 jit_solution(3017362916873735543)
XLA Ops:
  0.6 0.7 convert_element_type.7
  1.3 1.3 fusion.6.meta_ref
  2.6 1.3 reshape.12.gain_ref
  3.9 1.7 fusion.5.w_ref
  5.6 68.9 %attend.1 = (bf16[2048,2304]{1,0:T(8,128)(2,1)}, f32[128,2048]{1,0:T(8,128)}, bf16[128,2048]{1,0:T(8,128)(2,1)}, f32[16,128]{1,0:T(8,128)}, bf16[128,1024]{1,0:T...) custom-call(s32[1,16]{1,0:T(1,128)} %len_ref.1, s32[4,256]{1,0:T(4,128)} %table_ref.1, bf16[128,1024]{1,0:T(8,128)(2,1)} %kv_ref.1, ...), custom_call_target="tpu_custom_call" | custom-call | tf_op jit(solution)/shard_map/attend/pallas_call | solution.py:378
  74.5 69.1 %moe.1 = (bf16[1168,2048]{1,0:T(8,128)(2,1)}, bf16[512,2048]{1,0:T(8,128)(2,1)}) custom-call(bf16[128,2048]{1,0:T(8,128)(2,1)} %get-tuple-element.14.n_ref, f32[32,128]{1,0:T(8,128)} %get-tuple-element.13.tgt_ref, f32[32,128]{1,0:T(8,128)} %get-tuple-element.15.wt_ref, bf16[2048,2304]{1,0:T(8,128)(2,1)} %get-tuple-element.16.w_hbm, ...), custom_call_target="tpu_custom_call" | custom-call | tf_op jit(solution)/shard_map/moe/pallas_call | solution.py:580
  143.6 0.0 copy-start
  143.6 0.0 copy-start.1
  143.6 58.4 %give_back.1 = bf16[128,2048]{1,0:T(8,128)(2,1)} custom-call(f32[128,2048]{1,0:T(8,128)} %get-tuple-element.12.hid_ref, f32[32,128]{1,0:T(8,128)} %get-tuple-element.13.tgt_ref, bf16[1168,2048]{1,0:T(8,128)(2,1)} %get-tuple-element.17.y_hbm, bf16[512,2048]{1,0:T(8,128)(2,1)} %get-tuple-element.18.sh), custom_call_target="tpu_custom_call" | custom-call | tf_op jit(solution)/shard_map/give_back/pallas_call | solution.py:735
  202.0 1.9 copy.20
  203.9 0.0 copy-done
  203.9 0.7 copy.21
  204.6 0.0 copy-done.1
  204.6 0.6 copy.22
Async XLA Ops:
  143.6 60.3 %copy-start = (bf16[128,1024]{1,0:T(8,128)(2,1)S(1)}, bf16[128,1024]{1,0:T(8,128)(2,1)}, u32[]{:S(2)}) copy-start(bf16[128,1024]{1,0:T(8,128)(2,1)} %get-tuple-element.19) | copy-start | bytes 786436
  143.6 61.0 %copy-start.1 = (f32[16,128]{1,0:T(8,128)S(1)}, f32[16,128]{1,0:T(8,128)}, u32[]{:S(2)}) copy-start(f32[16,128]{1,0:T(8,128)} %get-tuple-element.26) | copy-start | bytes 24580

commit v7 on v6

--- a/solution.py
+++ b/solution.py
@@ -378,7 +378,7 @@
     return pl.pallas_call(
         kernel_attend,
         out_shape=(
-            jax.ShapeDtypeStruct((D, 3 * SPAD), BF16),
+            jax.ShapeDtypeStruct((D, 2 * SPAD), BF16),
             jax.ShapeDtypeStruct((TOK, D), F32),
             jax.ShapeDtypeStruct((TOK, D), BF16),
             jax.ShapeDtypeStruct((QUERY_HEADS, TOK), F32),
@@ -390,7 +390,7 @@
         out_specs=(ANY,) + (VM,) * 6,
         scratch_shapes=[
             pltpu.VMEM((32 * TOK, 1024), BF16),
-            pltpu.VMEM((D, 3 * SPAD), BF16),
+            pltpu.VMEM((D, 2 * SPAD), BF16),
             pltpu.VMEM((512, 128), F32),
             pltpu.VMEM((512, 1024), BF16),
             pltpu.VMEM((n, HEAD_SIZE), BF16),
@@ -431,7 +431,7 @@
 def shared_down(w_ref, act_s, out_ref):
     def down(j, _):
         col = pl.multiple_of(j * 256, 256)
-        o = lax.dot_general(act_s[...], w_ref[pl.ds(col, 256), 2 * SPAD:], (((1,), (1,)), ((), ())),
+        o = lax.dot_general(act_s[...], w_ref[pl.ds(col, 256), :], (((1,), (1,)), ((), ())),
                             preferred_element_type=F32)
         out_ref[:, pl.ds(col, 256)] = o.astype(BF16)
         return 0
@@ -476,9 +476,9 @@
     return pl.multiple_of(p.at(o[0], o[1]) - p.k, 2)
 
 
-def kernel_moe(n_ref, tgt_ref, wt_ref, w_hbm, wg_h, wu_h, wd_h, y_out, sh_out,
-               n_all, y_all, w_s, wg, wu, wd, x_s, act_s, y_s, sact, sho,
-               n_r, y_r, send, pair, w_sem, out_sem):
+def kernel_moe(n_ref, tgt_ref, wt_ref, w2_ref, w_hbm, wg_h, wu_h, wd_h, y_out, sh_out,
+               n_all, y_all, w_s, w2_s, wg, wu, wd, x_s, act_s, y_s, sact, sho,
+               n_r, y_r, w2_r, send, pair, w2_pair, w_sem, out_sem):
     p = Place()
     p.barrier((1, -1))
     g = Gather(p, n_ref, n_all, TOK, 4, send.at[0], n_r, pair, CHUNKS)
@@ -495,6 +495,14 @@
     state = {"at": 0}
     last = {ev[0]: i for i, ev in enumerate(evs)}
 
+    w2 = Gather(p, w2_ref, w2_s, 64, 4, send.at[2], w2_r, w2_pair)
+    w2_s[pl.ds(pl.multiple_of(p.c * 64, 64), 64), :] = w2_ref[...]
+
+    def level(d):
+        for ev in w2.events():
+            if ev[1] == d:
+                w2.take(ev)
+
     def tick(n):
         for ev in evs[state["at"]:state["at"] + n]:
             g.take(ev)
@@ -502,6 +510,8 @@
 
     def chunk(i, ticks):
         tick(max(0, last.get(i, -1) + 1 - state["at"]))
+        if i == 3:
+            w2.start()
         g.wait_pair(i)
         m = 2 * CAP * len(CHUNKS[i])
         wcols = []
@@ -523,6 +533,8 @@
 
             lax.fori_loop(0, 4, fetch, 0)
             tick(ticks[0])
+            if i == 3 and j == 2:
+                level(1)
         wcol = jnp.concatenate(wcols, axis=0) if len(wcols) > 1 else wcols[0]
         if i == 0:
             ws[0].wait()
@@ -539,6 +551,8 @@
 
         lax.fori_loop(0, 2, up_body, 0)
         tick(ticks[1])
+        if i == 3:
+            level(2)
         up(1024, 384)
         tick(ticks[2])
         if i == 0:
@@ -552,6 +566,8 @@
 
         lax.fori_loop(0, 4, down, 0)
         tick(ticks[3])
+        if i == 3:
+            level(3)
         rows = pl.ds(BASE[i], SPAN[i])
         out = pltpu.make_async_copy(y_s.at[rows], y_out.at[rows], out_sem.at[i])
         out.start()
@@ -564,31 +580,34 @@
     ws[3].wait()
     shared_up(y_all, w_s, sact)
     tick(6)
-    shared_down(w_s, sact, sho)
-    tick(3)
+    outs.append(chunk(2, (2, 5, 3, 4)))
+    outs.append(chunk(3, (0, 0, 0, 0)))
+    level(4)
+    w2.wait_pair()
+    shared_down(w2_s, sact, sho)
     outs.append(pltpu.make_async_copy(sho, sh_out, out_sem.at[4]))
     outs[-1].start()
-    outs.append(chunk(2, (2, 5, 3, 4)))
-    outs.append(chunk(3, (0, 0, 0, 0)))
+    w2.drain()
     g.drain()
     y.drain()
     for o in outs:
         o.wait()
 
 
-def call_moe(normed, tgt, wt, w_all, wg, wu, wd):
+def call_moe(normed, tgt, wt, w2, w_all, wg, wu, wd):
     return pl.pallas_call(
         kernel_moe,
         out_shape=(
             jax.ShapeDtypeStruct((Y_ROWS, D), BF16),
             jax.ShapeDtypeStruct((512, D), BF16),
         ),
-        in_specs=[VM, VM, VM, ANY, ANY, ANY, ANY],
+        in_specs=[VM, VM, VM, VM, ANY, ANY, ANY, ANY],
         out_specs=(ANY, ANY),
         scratch_shapes=[
             pltpu.VMEM((32 * TOK, D), BF16),
             pltpu.VMEM((512, D), BF16),
-            pltpu.VMEM((D, 3 * SPAD), BF16),
+            pltpu.VMEM((D, 2 * SPAD), BF16),
+            pltpu.VMEM((D, SPAD), BF16),
             pltpu.VMEM((D, FF), BF16),
             pltpu.VMEM((D, FF), BF16),
             pltpu.VMEM((FF, D), BF16),
@@ -599,14 +618,16 @@
             pltpu.VMEM((512, D), BF16),
             pltpu.SemaphoreType.DMA((60,)),
             pltpu.SemaphoreType.DMA((6,)),
-            pltpu.SemaphoreType.DMA((2,)),
+            pltpu.SemaphoreType.DMA((60,)),
+            pltpu.SemaphoreType.DMA((3,)),
             pltpu.SemaphoreType.DMA((4,)),
+            pltpu.SemaphoreType.DMA((1,)),
             pltpu.SemaphoreType.DMA((4,)),
             pltpu.SemaphoreType.DMA((5,)),
         ],
         compiler_params=pltpu.CompilerParams(collective_id=1, has_side_effects=True, vmem_limit_bytes=VMEM_LIMIT),
         name="moe",
-    )(normed, tgt, wt, w_all, wg, wu, wd)
+    )(normed, tgt, wt, w2, w_all, wg, wu, wd)
 
 
 def kernel_return(hid_ref, tgt_ref, y_hbm, sh, out_ref, y_ref, mine, pair, rbuf, shbuf, pair_sem, recv_sem,
@@ -757,14 +778,15 @@
 def on_device(queries, keys_then_values, residual, norm_gain, prompt_lengths, expert_ids, router_logits,
               w_gate, w_up, w_down, w_shared_gate, w_shared_up, w_shared_down, page_table):
     pad = ((0, 0), (0, SPAD - 704))
-    wcat = jnp.concatenate([jnp.pad(w, pad) for w in (w_shared_gate, w_shared_up, w_shared_down)], axis=1)
+    w1 = jnp.concatenate([jnp.pad(w, pad) for w in (w_shared_gate, w_shared_up)], axis=1)
+    w2 = jnp.pad(w_shared_down, pad)
     two = ((0, 0), (0, 2))
     meta = jnp.concatenate([
         jnp.pad(expert_ids.astype(F32), two, constant_values=-1.0),
         jnp.pad(router_logits, two, constant_values=-1e30)], axis=1).T
     w_all, hid, normed, log_totals, cache, tgt, wt = call_attend(
-        prompt_lengths, page_table, keys_then_values, wcat, meta, queries, residual, norm_gain.reshape(1, D))
-    y, sh = call_moe(normed, tgt, wt, w_all, w_gate, w_up, w_down)
+        prompt_lengths, page_table, keys_then_values, w1, meta, queries, residual, norm_gain.reshape(1, D))
+    y, sh = call_moe(normed, tgt, wt, w2, w_all, w_gate, w_up, w_down)
     out = call_return(hid, tgt, y, sh)
     return out, cache.reshape(8, PAGE, 1024), log_totals
 

time: 207 us -> 210 us (1.014)
    pallas_call x1, Pallas kernels: 69.1 us -> 78.5 us  [call_moe(): pl.pallas_call(kernel_moe, out_shape=(jax.ShapeDtypeStruct((Y_ROWS, D), B...]
    pallas_call x1, Pallas kernels: 68.9 us -> 62.4 us  [call_attend(): pl.pallas_call(kernel_attend, out_shape=(jax.ShapeDtypeStruct((D, 2 * SPA...]
where the time goes in v7:
time: 210 us; the launch traced here: 208 us
  Pallas kernels  198 us (94%)
  local copies, waits for them, and re-layouts  6.02 us (3%)
  other arithmetic  3.61 us (2%)
    pallas_call x1, Pallas kernels, call_moe(): pl.pallas_call(kernel_moe, out_shape=(jax.ShapeDtypeStruct((Y_ROWS, D), B...  78.5 us
    pallas_call x1, Pallas kernels, call_attend(): pl.pallas_call(kernel_attend, out_shape=(jax.ShapeDtypeStruct((D, 2 * SPA...  62.4 us
    pallas_call x1, Pallas kernels, call_return(): pl.pallas_call(kernel_return, out_shape=jax.ShapeDtypeStruct((TOK, D), BF...  56.9 us

profile of v7, /device:TPU:8, one launch (start us, length us, event | category | flops | bytes accessed | tf_op | source)
XLA Modules:
  0.0 208.1 jit_solution(501219528507416627)
XLA Ops:
  0.6 0.7 convert_element_type.7
  1.3 1.3 fusion.3.meta_ref
  2.6 1.3 reshape.12.gain_ref
  3.9 1.5 pad.21.w2_ref
  5.4 1.6 fusion.2.w_ref
  7.1 62.4 %attend.1 = (bf16[2048,1536]{1,0:T(8,128)(2,1)}, f32[128,2048]{1,0:T(8,128)}, bf16[128,2048]{1,0:T(8,128)(2,1)}, f32[16,128]{1,0:T(8,128)}, bf16[128,1024]{1,0:T...) custom-call(s32[1,16]{1,0:T(1,128)} %len_ref.1, s32[4,256]{1,0:T(4,128)} %table_ref.1, bf16[128,1024]{1,0:T(8,128)(2,1)} %kv_ref.1, ...), custom_call_target="tpu_custom_call" | custom-call | tf_op jit(solution)/shard_map/attend/pallas_call | solution.py:378
  69.5 78.5 %moe.1 = (bf16[1168,2048]{1,0:T(8,128)(2,1)}, bf16[512,2048]{1,0:T(8,128)(2,1)}) custom-call(bf16[128,2048]{1,0:T(8,128)(2,1)} %get-tuple-element.14.n_ref, f32[32,128]{1,0:T(8,128)} %get-tuple-element.13.tgt_ref, f32[32,128]{1,0:T(8,128)} %get-tuple-element.15.wt_ref, bf16[64,768]{1,0:T(8,128)(2,1)} %pad.21.w2_ref, ...), custom_call_target="tpu_custom_call" | custom-call | tf_op jit(solution)/shard_map/moe/pallas_call | solution.py:598
  147.9 0.0 copy-start
  147.9 0.0 copy-start.1
  147.9 56.9 %give_back.1 = bf16[128,2048]{1,0:T(8,128)(2,1)} custom-call(f32[128,2048]{1,0:T(8,128)} %get-tuple-element.12.hid_ref, f32[32,128]{1,0:T(8,128)} %get-tuple-element.13.tgt_ref, bf16[1168,2048]{1,0:T(8,128)(2,1)} %get-tuple-element.17.y_hbm, bf16[512,2048]{1,0:T(8,128)(2,1)} %get-tuple-element.18.sh), custom_call_target="tpu_custom_call" | custom-call | tf_op jit(solution)/shard_map/give_back/pallas_call | solution.py:756
  204.9 1.9 copy.20
  206.8 0.0 copy-done
  206.8 0.7 copy.21
  207.5 0.0 copy-done.1
  207.5 0.6 copy.22
Async XLA Ops:
  147.9 58.8 %copy-start = (bf16[128,1024]{1,0:T(8,128)(2,1)S(1)}, bf16[128,1024]{1,0:T(8,128)(2,1)}, u32[]{:S(2)}) copy-start(bf16[128,1024]{1,0:T(8,128)(2,1)} %get-tuple-element.19) | copy-start | bytes 786436
  147.9 59.5 %copy-start.1 = (f32[16,128]{1,0:T(8,128)S(1)}, f32[16,128]{1,0:T(8,128)}, u32[]{:S(2)}) copy-start(f32[16,128]{1,0:T(8,128)} %get-tuple-element.26) | copy-start | bytes 24580
